TPU v7x, 32 devices: a whole 2x2x4 slice. The times are simulated.
32 devices in a mesh: wide: 8 (over z, y), orb: 4 (over x, core).
Axes of the slice: x: 2, y: 2, z: 4, core: 2. Of those that a mesh axis runs over, the one named last changes fastest.
Arguments:
- green_packed: bfloat16 [2, 8, 16, 256, 256], P(None, 'wide', 'orb'), may hold values from -6 to 6
- bubble_weight: float32 [16, 16], replicated, may hold values from -1.5 to 1.5
- tile_owner: int32 [64], replicated, may hold values from 0 to 63, as said below
- pairing: int32 [64], replicated, may hold values from 0 to 63, as said below
Outputs:
- response: bfloat16 [2, 8, 16, 256, 256], P(None, 'wide', 'orb')
Inputs may be any that keep to these rules, and one draw needn't show every extreme that they name: `tile_owner`: A permutation of the 64 time tiles; slot s lies on index s // (8 * 8 / 8) of wide. The tiles in slots s and s + 32 are mirror images (tiles i * 8 + j and j * 8 + i) or both diagonal tiles. pairing[s] is the slot whose tile is the mirror image of tile_owner[s]: s itself for a diagonal tile, else the slot 32 away.
All inputs are finite; a program needn't handle non-finite values.
Results may differ from a plain program's by a relative error of at most 0.018.
Values may be sent and summed in bfloat16 or wider, within the bound.
No kernel may reach another device: no remote copies, remote signals or barrier semaphores. Data moves between devices by JAX's collectives and lax.ppermute only.
A program may use at most 128 MiB of HBM per device.

v0:
```python
import functools
import math

import jax
import jax.numpy as jnp
from jax import lax
from jax.experimental import pallas as pl
from jax.experimental.pallas import tpu as pltpu
from jax.sharding import PartitionSpec as P


F32 = jnp.float32
BF16 = jnp.bfloat16
VMEM = pl.BlockSpec(memory_space=pltpu.VMEM)
SMEM = pl.BlockSpec(memory_space=pltpu.SMEM)
PARAMS = pltpu.CompilerParams(vmem_limit_bytes=56 * 1024 * 1024)


def grid_masks(half):
    rows = lax.broadcasted_iota(jnp.int32, (half, half), 0)
    cols = lax.broadcasted_iota(jnp.int32, (half, half), 1)
    return rows, cols


def pack_kernel(green_ref, out_ref):
    count, momenta, _, pairs, _, rows, half = out_ref.shape
    row, col = grid_masks(half)

    def one(step, carry):
        part, pair = step // pairs, step % pairs
        for k in range(momenta):
            def block(i, j):
                return green_ref[part, k, pair, i * half : (i + 1) * half, j * half : (j + 1) * half].astype(F32)

            b00, b11 = block(0, 0), block(1, 1)
            own = jnp.concatenate([block(0, 1), jnp.where(row >= col, b00, b11)], 0)
            facing = jnp.concatenate([block(1, 0).T, jnp.where(row < col, b00, b11).T], 0)
            out_ref[:, k, part, pair, 0] = own.reshape(count, rows, half).astype(BF16)
            out_ref[:, k, part, pair, 1] = facing.reshape(count, rows, half).astype(BF16)
        return carry

    lax.fori_loop(0, 2 * pairs, one, 0)


def twiddle(re, im, angle):
    cos, sin = math.cos(angle), math.sin(angle)
    if abs(sin) < 1e-12:
        return (re, im) if cos > 0 else (-re, -im)
    if abs(cos) < 1e-12:
        return (-im, re) if sin > 0 else (im, -re)
    return re * cos - im * sin, re * sin + im * cos


def dft(values, sign):
    size = len(values)
    if size == 1:
        return values
    out = [None] * size
    if size % 2:
        for r in range(size):
            terms = [twiddle(*values[k], sign * 2 * math.pi * (k * r % size) / size) for k in range(size)]
            out[r] = (sum(t[0] for t in terms), sum(t[1] for t in terms))
        return out
    even, odd = dft(values[0::2], sign), dft(values[1::2], sign)
    for r in range(size // 2):
        re, im = twiddle(*odd[r], sign * 2 * math.pi * r / size)
        out[r] = (even[r][0] + re, even[r][1] + im)
        out[r + size // 2] = (even[r][0] - re, even[r][1] - im)
    return out


def middle_kernel(device_ref, weight_ref, in_ref, out_ref, real_scr, product_scr):
    count, per_device, _, pairs, _, rows, half = in_ref.shape
    all_pairs = weight_ref.shape[0] // rows
    orbs = all_pairs // pairs
    wide = count // orbs
    momenta = wide * per_device
    factor = momenta ** -0.5
    spot = lax.broadcasted_iota(jnp.int32, (rows, half), 0) + (device_ref[0] * rows - half)
    diagonal = spot == lax.broadcasted_iota(jnp.int32, (rows, half), 1)

    def lanes(sheet, part, r):
        return pl.ds(((sheet * 2 + part) * momenta + r) * half, half)

    def forward(pair, carry):
        orb, local = pair // pairs, pair % pairs
        real = []
        for sheet in range(2):
            values = [
                tuple(in_ref[w * orbs + orb, k, part, local, sheet].astype(F32) * factor for part in range(2))
                for w in range(wide)
                for k in range(per_device)
            ]
            real.append(dft(values, 1.0))
        for sheet in range(2):
            for r in range(momenta):
                re, im = real[sheet][r]
                real_scr[pair, :, lanes(sheet, 0, r)] = re
                real_scr[pair, :, lanes(sheet, 1, r)] = im
                back = -r % momenta
                mre, mim = (
                    jnp.where(diagonal, real[sheet][back][part], real[1 - sheet][back][part]) for part in range(2)
                )
                product_scr[pair, :, lanes(sheet, 0, r)] = re * mre - im * mim
                product_scr[pair, :, lanes(sheet, 1, r)] = re * mim + im * mre
        return carry

    lax.fori_loop(0, all_pairs, forward, 0)
    product = product_scr[...].reshape(all_pairs * rows, -1).astype(BF16)
    bubble = jnp.dot(weight_ref[...], product, preferred_element_type=F32)
    product_scr[...] = bubble.reshape(product_scr.shape)

    def backward(pair, carry):
        orb, local = pair // pairs, pair % pairs
        for sheet in range(2):
            values = []
            for r in range(momenta):
                re, im = (real_scr[pair, :, lanes(sheet, part, r)] for part in range(2))
                bre, bim = (product_scr[pair, :, lanes(sheet, part, r)] * factor for part in range(2))
                values.append((re * bre - im * bim, re * bim + im * bre))
            values = dft(values, -1.0)
            for w in range(wide):
                for k in range(per_device):
                    for part in range(2):
                        out_ref[w * orbs + orb, k, part, local, sheet] = values[w * per_device + k][part].astype(BF16)
        return carry

    lax.fori_loop(0, all_pairs, backward, 0)


def langreth_kernel(orb_ref, self_ref, *refs):
    orbs = self_ref.shape[3]
    green_refs, out_ref, lhs_scr, tile_scr = refs[:orbs], refs[orbs], refs[orbs + 1], refs[orbs + 2]
    count, momenta, _, _, _, rows, half = self_ref.shape
    me = orb_ref[0]
    row, col = grid_masks(half)
    zero = jnp.zeros((half, half), F32)
    scale = (2 * half) ** -0.5
    for k in range(momenta):
        for turn in range(orbs):
            c = me ^ turn
            for part in range(2):
                def sheet(index, lower):
                    span = slice(count // 2, count) if lower else slice(0, count // 2)
                    return self_ref[span, k, part, c, index].astype(F32).reshape(half, half)

                own, facing = sheet(0, True), sheet(1, True).T
                pieces = [
                    jnp.where(row >= col, own, zero),
                    sheet(1, False).T,
                    jnp.where(row >= col, facing, zero),
                    jnp.where(row < col, facing, zero),
                    sheet(0, False),
                    jnp.where(row < col, own, zero),
                ]
                for n, piece in enumerate(pieces):
                    lhs_scr[n * half : (n + 1) * half, (2 * turn + part) * half : (2 * turn + part + 1) * half] = piece.astype(BF16)

            def tiles(local, carry):
                blocks = {}
                for part in range(2):
                    for i in range(2):
                        for j in range(2):
                            blocks[part, i, j] = green_refs[turn][
                                part, k, local, i * half : (i + 1) * half, j * half : (j + 1) * half
                            ].astype(F32)
                picks = [
                    [jnp.where(row >= col, blocks[part, 0, 0], zero) for part in range(2)],
                    [blocks[part, 1, 0] for part in range(2)],
                    [jnp.where(row >= col, blocks[part, 1, 1], zero) for part in range(2)],
                    [jnp.where(row < col, blocks[part, 0, 0], zero) for part in range(2)],
                    [blocks[part, 0, 1] for part in range(2)],
                    [jnp.where(row < col, blocks[part, 1, 1], zero) for part in range(2)],
                ]
                for n, (re, im) in enumerate(picks):
                    tile_scr[turn, local, n, :half, :half] = re.astype(BF16)
                    tile_scr[turn, local, n, :half, half:] = im.astype(BF16)
                    tile_scr[turn, local, n, half:, :half] = (-im).astype(BF16)
                    tile_scr[turn, local, n, half:, half:] = re.astype(BF16)
                return carry

            lax.fori_loop(0, orbs, tiles, 0)

        def target(turn_b, carry):
            b = me ^ turn_b

            def left(first, last):
                return lhs_scr[first * half : last * half, :]

            def plain(lhs, n):
                rhs = jnp.concatenate([tile_scr[turn, b, n] for turn in range(orbs)], 0)
                return jnp.dot(lhs, rhs, preferred_element_type=F32)

            def adjoint(lhs, n):
                rhs = jnp.concatenate([tile_scr[turn_b, me ^ turn, n] for turn in range(orbs)], 1)
                return lax.dot_general(lhs, rhs, (((1,), (1,)), ((), ())), preferred_element_type=F32)

            upper = left(0, 2)
            d1 = plain(upper, 0)
            d2 = plain(upper, 4)
            d9 = adjoint(left(4, 6), 2)
            low = left(2, 3)
            back = left(3, 4)
            out10 = d1[half:] + plain(low, 1)
            out01 = d2[:half] + d9[:half] + adjoint(back, 1)
            ret00, ret11 = d1[:half], plain(low, 2)
            les00 = plain(left(0, 1), 3) + adjoint(back, 0)
            les11 = d2[half:] + d9[half:] + plain(low, 5)
            for part in range(2):
                at = slice(part * half, (part + 1) * half)
                out_ref[part, k, b, :half, :half] = (jnp.where(row >= col, ret00[:, at], les00[:, at]) * scale).astype(BF16)
                out_ref[part, k, b, half:, half:] = (jnp.where(row >= col, ret11[:, at], les11[:, at]) * scale).astype(BF16)
                out_ref[part, k, b, :half, half:] = (out01[:, at] * scale).astype(BF16)
                out_ref[part, k, b, half:, :half] = (out10[:, at] * scale).astype(BF16)
            return carry

        lax.fori_loop(0, orbs, target, 0)


def local(wide, orbs, green, bubble_weight, tile_owner, pairing):
    parts, momenta, pairs, times, _ = green.shape
    all_pairs = bubble_weight.shape[0]
    half = times // 2
    count = wide * orbs
    rows = times // count
    axes = ("wide", "orb")
    sheet_shape = (count, momenta, parts, pairs, 2, rows, half)
    sheets = jax.ShapeDtypeStruct(sheet_shape, BF16)
    device = lax.axis_index(axes).astype(jnp.int32).reshape(1)
    orb = lax.axis_index("orb").astype(jnp.int32).reshape(1)

    packed = pl.pallas_call(
        pack_kernel, out_shape=sheets, in_specs=[VMEM], out_specs=VMEM, compiler_params=PARAMS, name="pack"
    )(green)

    greens = {0: green}
    bit = orbs // 2
    while bit:
        swap = [(i, i ^ bit) for i in range(orbs)]
        greens.update({turn ^ bit: lax.ppermute(piece, "orb", swap) for turn, piece in greens.items()})
        bit //= 2
    greens = [greens[turn] for turn in range(orbs)]

    arrived = lax.all_to_all(packed, axes, 0, 0, tiled=True)
    spread = jnp.kron(bubble_weight, jnp.eye(rows, dtype=F32)).astype(BF16)
    width = 2 * parts * momenta * wide * half
    sent = pl.pallas_call(
        middle_kernel,
        out_shape=sheets,
        in_specs=[SMEM, VMEM, VMEM],
        out_specs=VMEM,
        scratch_shapes=[pltpu.VMEM((all_pairs, rows, width), F32)] * 2,
        compiler_params=PARAMS,
        name="middle",
    )(device, spread, arrived)
    returned = lax.all_to_all(sent, axes, 0, 0, tiled=True)

    return pl.pallas_call(
        langreth_kernel,
        out_shape=jax.ShapeDtypeStruct(green.shape, BF16),
        in_specs=[SMEM, VMEM] + [VMEM] * orbs,
        out_specs=VMEM,
        scratch_shapes=[
            pltpu.VMEM((6 * half, 2 * orbs * half), BF16),
            pltpu.VMEM((orbs, orbs, 6, 2 * half, 2 * half), BF16),
        ],
        compiler_params=PARAMS,
        name="langreth",
    )(orb, returned, *greens)


def solution(mesh):
    return jax.shard_map(
        functools.partial(local, mesh.shape["wide"], mesh.shape["orb"]),
        mesh=mesh,
        in_specs=(P(None, "wide", "orb", None, None), P(), P(), P()),
        out_specs=P(None, "wide", "orb", None, None),
        check_vma=False,
    )
```

profile of v0, /device:TPU:0, one launch (start us, length us, event | category | flops | bytes accessed | tf_op | source)
XLA Modules:
  0.0 83.1 jit_solution(5670750034075214075)
XLA Ops:
  0.0 3.1 %pack.1 = bf16[32,1,2,4,2,8,128]{6,5,4,3,2,1,0:T(8,128)(2,1)} custom-call(bf16[2,1,4,256,256]{4,3,2,1,0:T(8,128)(2,1)} %refs_0_.1), custom_call_target="tpu_custom_call" | custom-call | tf_op jit(solution)/shard_map/pack/pallas_call | solution.py:232
  3.1 0.0 copy-start
  3.1 0.0 copy-start.4
  3.1 7.3 %all-to-all-start = ((bf16[32,1,2,4,2,8,128]{6,5,4,3,2,1,0:T(8,128)(2,1)}), bf16[32,1,2,4,2,8,128]{6,5,4,3,2,1,0:T(8,128)(2,1)S(1)}, u32[]{:S(2)}, u32[]{:S(2)}) async-start(bf16[32,1,2,4,2,8,128]{6,5,4,3,2,1,0:T(8,128)(2,1)} %pack.1), calls=%async_computation | async-start | bytes 2097152 | tf_op jit(solution)/shard_map/all_to_all | solution.py:244
  10.4 0.0 copy-done
  10.4 1.8 %collective-permute-start.1 = (bf16[2,1,4,256,256]{4,3,2,1,0:T(8,128)(2,1)S(1)}, bf16[2,1,4,256,256]{4,3,2,1,0:T(8,128)(2,1)}, u32[]{:S(2)}, u32[]{:S(2)}) collective-permute-start(bf16[2,1,4,256,256]{4,3,2,1,0:T(8,128)(2,1)S(1)} %copy-done), channel_id=1, source_target_pairs={{0,2},{1,3},{2,0},{3,1},{4,6},{5,7},{6,4},{7,5},{8,10},{9,11},{10,... | collective-permute-start | bytes 3145736 | tf_op jit(solution)/shard_map/ppermute | solution.py:240
  12.3 0.0 copy-done.4
  12.3 0.1 multiply_convert_fusion
  12.4 1.1 %convert_element_type.14.weight_ref = bf16[128,128]{1,0:T(8,128)(2,1)} reshape(bf16[16,8,16,8]{3,2,1,0:T(8,128)(2,1)S(1)} %multiply_convert_fusion) | data formatting | bytes 65536 | tf_op jit(solution)/shard_map/convert_element_type | solution.py:245
  13.5 23.1 %all-to-all-done.in_ref = bf16[32,1,2,4,2,8,128]{6,5,4,3,2,1,0:T(8,128)(2,1)S(1)} async-done(((bf16[32,1,2,4,2,8,128]{6,5,4,3,2,1,0:T(8,128)(2,1)}), bf16[32,1,2,4,2,8,128]{6,5,4,3,2,1,0:T(8,128)(2,1)S(1)}, u32[]{:S(2)}, u32[]{:S(2)}) %all-to-all-start) | async-done | bytes 1048608 | tf_op jit(solution)/shard_map/all_to_all | solution.py:244
  36.6 0.0 copy-start.2
  36.6 1.0 %copy-done.2 = bf16[32,1,2,4,2,8,128]{6,5,4,3,2,1,0:T(8,128)(2,1)} copy-done((bf16[32,1,2,4,2,8,128]{6,5,4,3,2,1,0:T(8,128)(2,1)}, bf16[32,1,2,4,2,8,128]{6,5,4,3,2,1,0:T(8,128)(2,1)S(1)}, u32[]{:S(2)}) %copy-start.2) | copy-done | bytes 1048600
  37.6 4.3 %middle.1 = bf16[32,1,2,4,2,8,128]{6,5,4,3,2,1,0:T(8,128)(2,1)} custom-call(s32[1]{0:T(128)} %bitcast.1.device_ref, bf16[128,128]{1,0:T(8,128)(2,1)} %convert_element_type.14.weight_ref, bf16[32,1,2,4,2,8,128]{6,5,4,3,2,1,0:T(8,128)(2,1)} %copy-done.2), custom_call_target="tpu_custom_call" | custom-call | tf_op jit(solution)/shard_map/middle/pallas_call | solution.py:247
  41.9 3.6 %all-to-all-start.1 = ((bf16[32,1,2,4,2,8,128]{6,5,4,3,2,1,0:T(8,128)(2,1)}), bf16[32,1,2,4,2,8,128]{6,5,4,3,2,1,0:T(8,128)(2,1)S(1)}, u32[]{:S(2)}, u32[]{:S(2)}) async-start(bf16[32,1,2,4,2,8,128]{6,5,4,3,2,1,0:T(8,128)(2,1)} %middle.1), calls=%async_computation.1 | async-start | bytes 2097152 | tf_op jit(solution)/shard_map/all_to_all | solution.py:256
  45.5 0.3 collective-permute-start
  45.9 1.2 %collective-permute-done.1.refs_2_ = bf16[2,1,4,256,256]{4,3,2,1,0:T(8,128)(2,1)} collective-permute-done((bf16[2,1,4,256,256]{4,3,2,1,0:T(8,128)(2,1)S(1)}, bf16[2,1,4,256,256]{4,3,2,1,0:T(8,128)(2,1)}, u32[]{:S(2)}, u32[]{:S(2)}) %collective-permute-start.1) | collective-permute-done | bytes 1048608 | tf_op jit(solution)/shard_map/ppermute | solution.py:240
  47.1 0.0 collective-permute-start.2
  47.1 1.2 %collective-permute-done.refs_1_ = bf16[2,1,4,256,256]{4,3,2,1,0:T(8,128)(2,1)S(1)} collective-permute-done((bf16[2,1,4,256,256]{4,3,2,1,0:T(8,128)(2,1)S(1)}, bf16[2,1,4,256,256]{4,3,2,1,0:T(8,128)(2,1)S(1)}, u32[]{:S(2)}, u32[]{:S(2)}) %collective-permute-start) | collective-permute-done | bytes 1048608 | tf_op jit(solution)/shard_map/ppermute | solution.py:240
  48.3 0.0 copy-start.3
  48.3 1.8 %collective-permute-done.2.refs_3_ = bf16[2,1,4,256,256]{4,3,2,1,0:T(8,128)(2,1)} collective-permute-done((bf16[2,1,4,256,256]{4,3,2,1,0:T(8,128)(2,1)}, bf16[2,1,4,256,256]{4,3,2,1,0:T(8,128)(2,1)}, u32[]{:S(2)}, u32[]{:S(2)}) %collective-permute-start.2) | collective-permute-done | bytes 1048608 | tf_op jit(solution)/shard_map/ppermute | solution.py:240
  50.1 21.7 %all-to-all-done.1.self_ref = bf16[32,1,2,4,2,8,128]{6,5,4,3,2,1,0:T(8,128)(2,1)S(1)} async-done(((bf16[32,1,2,4,2,8,128]{6,5,4,3,2,1,0:T(8,128)(2,1)}), bf16[32,1,2,4,2,8,128]{6,5,4,3,2,1,0:T(8,128)(2,1)S(1)}, u32[]{:S(2)}, u32[]{:S(2)}) %all-to-all-start.1) | async-done | bytes 1048608 | tf_op jit(solution)/shard_map/all_to_all | solution.py:256
  71.7 0.0 copy-done.3
  71.7 1.0 %copy-done.1 = bf16[32,1,2,4,2,8,128]{6,5,4,3,2,1,0:T(8,128)(2,1)} copy-done((bf16[32,1,2,4,2,8,128]{6,5,4,3,2,1,0:T(8,128)(2,1)}, bf16[32,1,2,4,2,8,128]{6,5,4,3,2,1,0:T(8,128)(2,1)S(1)}, u32[]{:S(2)}) %copy-start.1) | copy-done | bytes 1048600
  72.7 10.3 %langreth.1 = bf16[2,1,4,256,256]{4,3,2,1,0:T(8,128)(2,1)} custom-call(s32[1]{0:T(128)} %bitcast.orb_ref, bf16[32,1,2,4,2,8,128]{6,5,4,3,2,1,0:T(8,128)(2,1)} %copy-done.1, bf16[2,1,4,256,256]{4,3,2,1,0:T(8,128)(2,1)} %refs_0_.1, bf16[2,1,4,256,256]{4,3,2,1,0:T(8,128)(2,1)} %copy-done.3, bf16[2,1,4,256,256]{4,3,2,1,0:T(8,128)(2,1)} %collective-permute-done.1.refs_2_, ...), custom_call_target="tpu_custom_call" | custom-call | tf_op jit(solution)/shard_map/langreth/pallas_call | solution.py:258
  (2 shorter events, 0.0 us)
Async XLA Ops:
  3.1 7.3 %copy-start = (bf16[2,1,4,256,256]{4,3,2,1,0:T(8,128)(2,1)S(1)}, bf16[2,1,4,256,256]{4,3,2,1,0:T(8,128)(2,1)}, u32[]{:S(2)}) copy-start(bf16[2,1,4,256,256]{4,3,2,1,0:T(8,128)(2,1)} %refs_0_.1) | copy-start | bytes 3145732
  3.1 9.2 %copy-start.4 = (f32[16,16]{1,0:T(8,128)S(1)}, f32[16,16]{1,0:T(8,128)}, u32[]{:S(2)}) copy-start(f32[16,16]{1,0:T(8,128)} %param.5) | copy-start | bytes 3076
  3.1 33.5 %all-to-all-start = ((bf16[32,1,2,4,2,8,128]{6,5,4,3,2,1,0:T(8,128)(2,1)}), bf16[32,1,2,4,2,8,128]{6,5,4,3,2,1,0:T(8,128)(2,1)S(1)}, u32[]{:S(2)}, u32[]{:S(2)}) async-start(bf16[32,1,2,4,2,8,128]{6,5,4,3,2,1,0:T(8,128)(2,1)} %pack.1), calls=%async_computation | async-start | bytes 2097152 | tf_op jit(solution)/shard_map/all_to_all | solution.py:244
  10.4 36.6 %collective-permute-start.1 = (bf16[2,1,4,256,256]{4,3,2,1,0:T(8,128)(2,1)S(1)}, bf16[2,1,4,256,256]{4,3,2,1,0:T(8,128)(2,1)}, u32[]{:S(2)}, u32[]{:S(2)}) collective-permute-start(bf16[2,1,4,256,256]{4,3,2,1,0:T(8,128)(2,1)S(1)} %copy-done), channel_id=1, source_target_pairs={{0,2},{1,3},{2,0},{3,1},{4,6},{5,7},{6,4},{7,5},{8,10},{9,11},{10,... | collective-permute-start | bytes 3145736 | tf_op jit(solution)/shard_map/ppermute | solution.py:240
  36.6 1.0 %copy-start.2 = (bf16[32,1,2,4,2,8,128]{6,5,4,3,2,1,0:T(8,128)(2,1)}, bf16[32,1,2,4,2,8,128]{6,5,4,3,2,1,0:T(8,128)(2,1)S(1)}, u32[]{:S(2)}) copy-start(bf16[32,1,2,4,2,8,128]{6,5,4,3,2,1,0:T(8,128)(2,1)S(1)} %all-to-all-done.in_ref) | copy-start | bytes 3145732
  41.9 29.8 %all-to-all-start.1 = ((bf16[32,1,2,4,2,8,128]{6,5,4,3,2,1,0:T(8,128)(2,1)}), bf16[32,1,2,4,2,8,128]{6,5,4,3,2,1,0:T(8,128)(2,1)S(1)}, u32[]{:S(2)}, u32[]{:S(2)}) async-start(bf16[32,1,2,4,2,8,128]{6,5,4,3,2,1,0:T(8,128)(2,1)} %middle.1), calls=%async_computation.1 | async-start | bytes 2097152 | tf_op jit(solution)/shard_map/all_to_all | solution.py:256
  45.5 2.7 %collective-permute-start = (bf16[2,1,4,256,256]{4,3,2,1,0:T(8,128)(2,1)S(1)}, bf16[2,1,4,256,256]{4,3,2,1,0:T(8,128)(2,1)S(1)}, u32[]{:S(2)}, u32[]{:S(2)}) collective-permute-start(bf16[2,1,4,256,256]{4,3,2,1,0:T(8,128)(2,1)S(1)} %copy-done), channel_id=1, source_target_pairs={{0,1},{1,0},{2,3},{3,2},{4,5},{5,4},{6,7},{7,6},{8,9},{9,8},{10,11... | collective-permute-start | bytes 3145736 | tf_op jit(solution)/shard_map/ppermute | solution.py:240
  47.1 3.0 %collective-permute-start.2 = (bf16[2,1,4,256,256]{4,3,2,1,0:T(8,128)(2,1)}, bf16[2,1,4,256,256]{4,3,2,1,0:T(8,128)(2,1)}, u32[]{:S(2)}, u32[]{:S(2)}) collective-permute-start(bf16[2,1,4,256,256]{4,3,2,1,0:T(8,128)(2,1)} %collective-permute-done.1.refs_2_), channel_id=1, source_target_pairs={{0,1},{1,0},{2,3},{3,2},{4,5},{5,4},{6,7},{7,6},{8,9},{9,8},{10,11... | collective-permute-start | bytes 3145736 | tf_op jit(solution)/shard_map/ppermute | solution.py:240
  48.3 23.5 %copy-start.3 = (bf16[2,1,4,256,256]{4,3,2,1,0:T(8,128)(2,1)}, bf16[2,1,4,256,256]{4,3,2,1,0:T(8,128)(2,1)S(1)}, u32[]{:S(2)}) copy-start(bf16[2,1,4,256,256]{4,3,2,1,0:T(8,128)(2,1)S(1)} %collective-permute-done.refs_1_) | copy-start | bytes 3145732
  71.7 1.0 %copy-start.1 = (bf16[32,1,2,4,2,8,128]{6,5,4,3,2,1,0:T(8,128)(2,1)}, bf16[32,1,2,4,2,8,128]{6,5,4,3,2,1,0:T(8,128)(2,1)S(1)}, u32[]{:S(2)}) copy-start(bf16[32,1,2,4,2,8,128]{6,5,4,3,2,1,0:T(8,128)(2,1)S(1)} %all-to-all-done.1.self_ref) | copy-start | bytes 3145732
where the time goes:
time: 83.4 us; the launch traced here: 83.1 us
  waiting for transfers between devices  49 us (59%)
  Pallas kernels  17.7 us (21%)
  starting transfers between devices  13.1 us (16%)
  local copies, waits for them, and re-layouts  3.09 us (4%)
    all_to_all x1, waiting for transfers between devices, local(): arrived = lax.all_to_all(packed, axes, 0, 0, tiled=True)  23.1 us
    all_to_all x1, waiting for transfers between devices, local(): returned = lax.all_to_all(sent, axes, 0, 0, tiled=True)  21.7 us
    pallas_call x1, Pallas kernels, local(): pl.pallas_call(langreth_kernel, out_shape=jax.ShapeDtypeStruct(green.shap...  10.3 us
    all_to_all x1, starting transfers between devices, local(): arrived = lax.all_to_all(packed, axes, 0, 0, tiled=True)  7.33 us
    pallas_call x1, Pallas kernels, local(): pl.pallas_call(middle_kernel, out_shape=sheets, in_specs=[SMEM, VMEM, VME...  4.31 us
    ppermute x3, waiting for transfers between devices, local(): lax.ppermute(piece, 'orb', swap)  4.2 us
    all_to_all x1, starting transfers between devices, local(): returned = lax.all_to_all(sent, axes, 0, 0, tiled=True)  3.62 us
    pallas_call x1, Pallas kernels, local(): pl.pallas_call(pack_kernel, out_shape=sheets, in_specs=[VMEM], out_specs=...  3.09 us
  transfers between devices with their start and end apart: 5, of which 5 were waited for; matrix products, arithmetic and copies ran while one was open for 2% of the time, Pallas kernels for 5%

commit v1 on v0

v1 whole, which is shorter than its diff:
```python
import functools
import math

import jax
import jax.numpy as jnp
from jax import lax
from jax.experimental import pallas as pl
from jax.experimental.pallas import tpu as pltpu
from jax.sharding import PartitionSpec as P


F32 = jnp.float32
BF16 = jnp.bfloat16
VMEM = pl.BlockSpec(memory_space=pltpu.VMEM)
SMEM = pl.BlockSpec(memory_space=pltpu.SMEM)
HBM = pl.BlockSpec(memory_space=pltpu.HBM)


def limit(mebibytes):
    return pltpu.CompilerParams(vmem_limit_bytes=mebibytes * 1024 * 1024)


def grid_masks(half):
    rows = lax.broadcasted_iota(jnp.int32, (half, half), 0)
    cols = lax.broadcasted_iota(jnp.int32, (half, half), 1)
    return rows, cols


def places(count, near, sent):
    if sent:
        return [(rel // near, (rel % 2, rel % near // 2)) for rel in range(count)]
    return [(rel % near // 2, (rel % 2, rel // near)) for rel in range(count)]


def emit(block_scr, me, out_refs, spots):
    if spots is None:
        out_refs[0][...] = block_scr[...]
        return
    for rel, (n, at) in enumerate(spots):
        out_refs[n].at[at][...] = block_scr[me ^ rel]


def collect(block_scr, me, in_refs, spots):
    if spots is None:
        block_scr[...] = in_refs[0][...]
        return
    for rel, (n, at) in enumerate(spots):
        block_scr[me ^ rel] = in_refs[n].at[at][...]


def entries(spots):
    return 1 if spots is None else 1 + max(n for n, _ in spots)


def halves(own, facing, count):
    rows = own.shape[0] // count
    return [
        jnp.concatenate([own[d * rows : (d + 1) * rows], facing[d * rows : (d + 1) * rows]], 0)
        for d in range(count)
    ]


def pack_kernel(blocks, spots, device_ref, green_ref, *refs):
    raw_ref, out_refs, block_scr, green_scr, sems = refs[0], refs[1:-3], refs[-3], refs[-2], refs[-1]
    count, momenta, parts, pairs, _, half = block_scr.shape
    row, col = grid_masks(half)

    def fetch(step, target=green_scr, kind=0):
        part, pair = step // pairs, step % pairs
        return [
            pltpu.make_async_copy(
                green_ref.at[part, :, pair, pl.ds(i * half, half), pl.ds(j * half, half)],
                target.at[step, n],
                sems.at[kind, step, n],
            )
            for n, (i, j) in enumerate(blocks)
        ]

    def begin(step, carry):
        for copy in fetch(step) + fetch(step, raw_ref, 1):
            copy.start()
        return carry

    lax.fori_loop(0, parts * pairs, begin, 0)

    def one(step, carry):
        part, pair = step // pairs, step % pairs
        for copy in fetch(step):
            copy.wait()
        for k in range(momenta):
            got = {at: green_scr[step, n, k].astype(F32) for n, at in enumerate(blocks)}
            own, facing = [], []
            if (0, 1) in got:
                own.append(got[0, 1])
                facing.append(got[1, 0].T)
            if (0, 0) in got:
                own.append(jnp.where(row >= col, got[0, 0], got[1, 1]))
                facing.append(jnp.where(row < col, got[0, 0], got[1, 1]).T)
            own, facing = (jnp.concatenate(x, 0) if len(x) > 1 else x[0] for x in (own, facing))
            for d, piece in enumerate(halves(own, facing, count)):
                block_scr[d, k, part, pair] = piece.astype(BF16)
        return carry

    lax.fori_loop(0, parts * pairs, one, 0)
    emit(block_scr, device_ref[0], out_refs, spots)

    def finish(step, carry):
        for copy in fetch(step, raw_ref, 1):
            copy.wait()
        return carry

    lax.fori_loop(0, parts * pairs, finish, 0)


def twiddle(re, im, angle):
    cos, sin = math.cos(angle), math.sin(angle)
    if abs(sin) < 1e-12:
        return (re, im) if cos > 0 else (-re, -im)
    if abs(cos) < 1e-12:
        return (-im, re) if sin > 0 else (im, -re)
    return re * cos - im * sin, re * sin + im * cos


def dft(values, sign):
    size = len(values)
    if size == 1:
        return values
    out = [None] * size
    if size % 2:
        for r in range(size):
            terms = [twiddle(*values[k], sign * 2 * math.pi * (k * r % size) / size) for k in range(size)]
            out[r] = (sum(t[0] for t in terms), sum(t[1] for t in terms))
        return out
    even, odd = dft(values[0::2], sign), dft(values[1::2], sign)
    for r in range(size // 2):
        re, im = twiddle(*odd[r], sign * 2 * math.pi * r / size)
        out[r] = (even[r][0] + re, even[r][1] + im)
        out[r + size // 2] = (even[r][0] - re, even[r][1] - im)
    return out


def middle_kernel(start, came_spots, sent_spots, device_ref, weight_ref, *refs):
    real_scr, product_scr, block_scr = refs[-3:]
    count, per_device, _, pairs, rows2, half = block_scr.shape
    all_pairs = weight_ref.shape[0] // rows2
    orbs = all_pairs // pairs
    wide = count // orbs
    momenta = wide * per_device
    factor = momenta ** -0.5
    me = device_ref[0]
    inputs = entries(came_spots)
    in_refs, out_refs = refs[:inputs], refs[inputs:-3]
    rows = rows2 // 2
    if start is not None:
        spot = lax.broadcasted_iota(jnp.int32, (rows2, half), 0)
        spot = jnp.where(spot >= rows, spot - rows, spot) + (me * rows + start)
        diagonal = spot == lax.broadcasted_iota(jnp.int32, (rows2, half), 1)

    collect(block_scr, me, in_refs, came_spots)

    def lanes(part, r):
        return pl.ds((part * momenta + r) * half, half)

    def across(x):
        if rows2 == 8:
            return pltpu.roll(x, rows, 0)
        return jnp.concatenate([x[rows:], x[:rows]], 0)

    def forward(pair, carry):
        orb, local = pair // pairs, pair % pairs
        values = [
            tuple(block_scr[w * orbs + orb, k, part, local].astype(F32) * factor for part in range(2))
            for w in range(wide)
            for k in range(per_device)
        ]
        real = dft(values, 1.0)
        for r in range(momenta):
            re, im = real[r]
            real_scr[pair, :, lanes(0, r)] = re
            real_scr[pair, :, lanes(1, r)] = im
            mre, mim = (across(x) for x in real[-r % momenta])
            if start is not None:
                mre, mim = (jnp.where(diagonal, x, y) for x, y in zip(real[-r % momenta], (mre, mim)))
            product_scr[pair, :, lanes(0, r)] = re * mre - im * mim
            product_scr[pair, :, lanes(1, r)] = re * mim + im * mre
        return carry

    lax.fori_loop(0, all_pairs, forward, 0)
    product = product_scr[...].reshape(all_pairs * rows2, -1).astype(BF16)
    bubble = jnp.dot(weight_ref[...], product, preferred_element_type=F32)
    product_scr[...] = bubble.reshape(product_scr.shape)

    def backward(pair, carry):
        orb, local = pair // pairs, pair % pairs
        values = []
        for r in range(momenta):
            re, im = (real_scr[pair, :, lanes(part, r)] for part in range(2))
            bre, bim = (product_scr[pair, :, lanes(part, r)] * factor for part in range(2))
            values.append((re * bre - im * bim, re * bim + im * bre))
        values = dft(values, -1.0)
        for w in range(wide):
            for k in range(per_device):
                for part in range(2):
                    block_scr[w * orbs + orb, k, part, local] = values[w * per_device + k][part].astype(BF16)
        return carry

    lax.fori_loop(0, all_pairs, backward, 0)
    emit(block_scr, me, out_refs, sent_spots)


def near_kernel(*refs):
    for z, ref in enumerate(refs[:-1]):
        refs[-1][z] = ref[1]


def plane_kernel(far, *refs):
    came_ref, out_refs = refs[far], refs[far + 1 :]
    for m, out_ref in enumerate(out_refs):
        for z in range(far):
            out_ref[0, z] = refs[z][0, m]
            out_ref[1, z] = came_ref[z, m]


def langreth_kernel(came_spots, device_ref, *refs):
    left_scr, block_scr, green_scr, sems = refs[-4:]
    kinds = green_scr.shape[0]
    count, momenta, _, orbs, rows2, half = block_scr.shape[1:]
    total = kinds * orbs
    out_ref, green_any, self_refs = refs[-5], refs[-5 - total : -5], refs[: -5 - total]
    copies = [
        pltpu.make_async_copy(green_any[n], green_scr.at[n // orbs, n % orbs], sems.at[n]) for n in range(total)
    ]
    for copy in copies:
        copy.start()
    here = device_ref[0]
    me = here % orbs
    rows = rows2 // 2
    chunks = len(came_spots)
    for n, spots in enumerate(came_spots):
        used = entries(spots)
        collect(block_scr.at[n], here, self_refs[:used], spots)
        self_refs = self_refs[used:]
    row, col = grid_masks(half)
    lower, upper = row >= col, row < col
    keep = {1: lower.astype(F32).astype(BF16), -1: upper.astype(F32).astype(BF16)}
    scale = (2 * half) ** -0.5
    blocks = ((0, 0), (0, 1), (1, 0), (1, 1))
    for k in range(momenta):
        for turn in range(orbs):
            c = me ^ turn
            for part in range(2):
                sheets = {}
                for n in range(chunks):
                    piece = block_scr[n, :, k, part, c].astype(F32)
                    for index in range(2):
                        sheet = jnp.concatenate([piece[d, index * rows : (index + 1) * rows] for d in range(count)], 0)
                        for low in range(2) if chunks == 1 else (n,):
                            sheets[index, low] = sheet[low * half : (low + 1) * half] if chunks == 1 else sheet

                own, facing = sheets[0, 1], sheets[1, 1].T
                pieces = [
                    jnp.where(lower, own, 0.0),
                    sheets[1, 0].T,
                    jnp.where(lower, facing, 0.0),
                    jnp.where(upper, facing, 0.0),
                    sheets[0, 0],
                    jnp.where(upper, own, 0.0),
                ]
                at = slice(turn * half, (turn + 1) * half)
                for n, piece in enumerate(pieces):
                    left_scr[(2 * n + part) * half : (2 * n + part + 1) * half, at] = piece.astype(BF16)

        if k == 0:
            for copy in copies:
                copy.wait()
        for turn_b in range(orbs):
            b = me ^ turn_b

            def block(turn, pair, part, i, j, mask):
                kind, n = (int(i == j), i) if kinds == 2 else (0, (i == j) * 2 + i)
                piece = green_scr[kind, turn, part * orbs + pair, n, k]
                return piece * keep[mask] if mask else piece

            def left(first, last):
                return left_scr[2 * first * half : 2 * last * half, :]

            def rows_of(product, n):
                return (product[2 * n * half : (2 * n + 1) * half], product[(2 * n + 1) * half : (2 * n + 2) * half])

            def plain(first, last, i, j, mask):
                right = jnp.concatenate(
                    [
                        jnp.concatenate([block(turn, b, part, i, j, mask) for part in range(2)], 1)
                        for turn in range(orbs)
                    ],
                    0,
                )
                product = jnp.dot(left(first, last), right, preferred_element_type=F32)
                out = []
                for n in range(last - first):
                    real, imag = rows_of(product, n)
                    out.append((real[:, :half] - imag[:, half:], real[:, half:] + imag[:, :half]))
                return out

            def adjoint(first, last, i, j, mask):
                right = jnp.concatenate(
                    [
                        jnp.concatenate([block(turn_b, me ^ turn, part, i, j, mask) for part in range(2)], 0)
                        for turn in range(orbs)
                    ],
                    1,
                )
                product = lax.dot_general(
                    left(first, last), right, (((1,), (1,)), ((), ())), preferred_element_type=F32
                )
                out = []
                for n in range(last - first):
                    real, imag = rows_of(product, n)
                    out.append((real[:, :half] + imag[:, half:], imag[:, :half] - real[:, half:]))
                return out

            d1 = plain(0, 2, 0, 0, 1)
            d2 = plain(0, 2, 0, 1, 0)
            d3 = plain(0, 1, 0, 0, -1)[0]
            d4 = plain(2, 3, 1, 0, 0)[0]
            d5 = plain(2, 3, 1, 1, 1)[0]
            d6 = plain(2, 3, 1, 1, -1)[0]
            d7 = adjoint(3, 4, 0, 0, 1)[0]
            d8 = adjoint(3, 4, 1, 0, 0)[0]
            d9 = adjoint(4, 6, 1, 1, 1)
            for part in range(2):
                results = (
                    jnp.where(lower, d1[0][part], d3[part] + d7[part]),
                    d2[0][part] + d8[part] + d9[0][part],
                    d1[1][part] + d4[part],
                    jnp.where(lower, d5[part], d2[1][part] + d6[part] + d9[1][part]),
                )
                for (i, j), result in zip(blocks, results):
                    out_ref[part, k, b, i * half : (i + 1) * half, j * half : (j + 1) * half] = (
                        result * scale
                    ).astype(BF16)


def exchange(axes, count, sent):
    def shift(x, mask):
        return lax.ppermute(x, axes, [(i, i ^ mask) for i in range(count)])

    far, planes, block = len(sent), sent[0].shape[1], sent[0].shape[2:]
    far_sent = [shift(x, 2 * planes * z) if z else x for z, x in enumerate(sent)]
    swap = pl.pallas_call(
        near_kernel,
        out_shape=jax.ShapeDtypeStruct((far, planes) + block, BF16),
        in_specs=[VMEM] * far,
        out_specs=VMEM,
        compiler_params=limit(4),
        name="near",
    )(*far_sent)
    came = shift(swap, 1)
    joined = pl.pallas_call(
        functools.partial(plane_kernel, far),
        out_shape=[jax.ShapeDtypeStruct((2, far) + block, BF16)] * planes,
        in_specs=[VMEM] * (far + 1),
        out_specs=[VMEM] * planes,
        compiler_params=limit(4),
        name="plane",
    )(*far_sent, came)
    return [shift(x, 2 * m) if m else x for m, x in enumerate(joined)]


def gather(orbs, raw):
    held = {0: raw}
    bit = orbs // 2
    while bit:
        swap = [(i, i ^ bit) for i in range(orbs)]
        for turn, piece in list(held.items()):
            held[turn ^ bit] = lax.ppermute(piece, "orb", swap)
        bit //= 2
    return [held[turn] for turn in range(orbs)]


def local(wide, orbs, green, bubble_weight, tile_owner, pairing):
    parts, momenta, pairs, times, _ = green.shape
    all_pairs = bubble_weight.shape[0]
    half = times // 2
    count = wide * orbs
    chunks = 2 if half % count == 0 else 1
    rows2 = 2 * times // count // chunks
    axes = ("wide", "orb")
    planes = min(4, count // 2)
    far = count // (2 * planes)
    block = (momenta, parts, pairs, rows2, half)
    device = lax.axis_index(axes).astype(jnp.int32).reshape(1)
    spread = jnp.kron(bubble_weight, jnp.eye(rows2, dtype=F32)).astype(BF16)
    width = parts * momenta * wide * half

    off, on = ((0, 1), (1, 0)), ((0, 0), (1, 1))
    plan = [("d", on, 0, True), ("o", off, None, False)] if chunks == 2 else [("o", off + on, -half, False)]
    returned, greens, came_spots = {}, {}, {}

    def sheets(staged):
        if staged:
            return [jax.ShapeDtypeStruct((2, planes) + block, BF16)] * far
        return [jax.ShapeDtypeStruct((count,) + block, BF16)]

    def deliver(staged, sent):
        if staged:
            return exchange(axes, count, sent)
        return [lax.all_to_all(sent[0], axes, 0, 0, tiled=True)]

    for tag, blocks, start, staged in plan:
        sent_spots = places(count, 2 * planes, True) if staged else None
        came_spots[tag] = places(count, 2 * planes, False) if staged else None
        raw, *sent = pl.pallas_call(
            functools.partial(pack_kernel, blocks, sent_spots),
            out_shape=[jax.ShapeDtypeStruct((parts * pairs, len(blocks), momenta, half, half), BF16)]
            + sheets(staged),
            in_specs=[SMEM, HBM],
            out_specs=[HBM] + [VMEM] * len(sheets(staged)),
            scratch_shapes=[
                pltpu.VMEM((count,) + block, BF16),
                pltpu.VMEM((parts * pairs, len(blocks), momenta, half, half), BF16),
                pltpu.SemaphoreType.DMA((2, parts * pairs, len(blocks))),
            ],
            compiler_params=limit(8),
        )(device, green)
        greens[tag] = gather(orbs, raw)
        arrived = deliver(staged, sent)
        sent = pl.pallas_call(
            functools.partial(middle_kernel, start, came_spots[tag], sent_spots),
            out_shape=sheets(staged),
            in_specs=[SMEM] + [VMEM] * (1 + len(arrived)),
            out_specs=[VMEM] * len(sheets(staged)),
            scratch_shapes=[pltpu.VMEM((all_pairs, rows2, width), F32)] * 2 + [pltpu.VMEM((count,) + block, BF16)],
            compiler_params=limit(16),
        )(device, spread, *arrived)
        returned[tag] = deliver(staged, sent)

    tags = sorted(returned, reverse=True)
    came_spots = [came_spots[tag] for tag in tags]
    returned = sum((returned[tag] for tag in tags), [])
    raws = sum((greens[tag] for tag in tags), [])
    return pl.pallas_call(
        functools.partial(langreth_kernel, came_spots),
        out_shape=jax.ShapeDtypeStruct(green.shape, BF16),
        in_specs=[SMEM] + [VMEM] * len(returned) + [HBM] * len(raws),
        out_specs=VMEM,
        scratch_shapes=[
            pltpu.VMEM((12 * half, orbs * half), BF16),
            pltpu.VMEM((chunks, count) + block, BF16),
            pltpu.VMEM((chunks, orbs) + raws[0].shape, BF16),
            pltpu.SemaphoreType.DMA((len(raws),)),
        ],
        compiler_params=limit(60),
        name="langreth",
    )(device, *returned, *raws)


def solution(mesh):
    return jax.shard_map(
        functools.partial(local, mesh.shape["wide"], mesh.shape["orb"]),
        mesh=mesh,
        in_specs=(P(None, "wide", "orb", None, None), P(), P(), P()),
        out_specs=P(None, "wide", "orb", None, None),
        check_vma=False,
    )
```

time: 83.4 us -> 95 us (1.14)
  starting transfers between devices: 13.1 us -> 31.6 us
  waiting for transfers between devices: 49 us -> 43.1 us
  Pallas kernels: 17.7 us -> 15.6 us
    all_to_all x2, waiting for transfers between devices: 44.8 us -> 0.01 us  [deliver(): return [lax.all_to_all(sent[0], axes, 0, 0, tiled=True)]]
    ppermute x3 -> x20, waiting for transfers between devices: 4.2 us -> 43.1 us  [the longest x14 43.1 us: shift(): return lax.ppermute(x, axes, [(i, i ^ mask) for i in range(count)])]
    ppermute x3 -> x20, starting transfers between devices: 2.15 us -> 19.3 us  [the longest x14 16.7 us: shift(): return lax.ppermute(x, axes, [(i, i ^ mask) for i in range(count)])]
    pallas_call x3 -> x9, Pallas kernels: 17.7 us -> 15.6 us  [the longest x1 8.13 us: local(): pl.pallas_call(functools.partial(langreth_kernel, came_spots), out_shape=...]
    unnamed x10 -> x26, local copies, waits for them, and re-layouts: 1.98 us -> 3.4 us
    all_to_all x2, starting transfers between devices: 10.9 us -> 12.3 us  [deliver(): return [lax.all_to_all(sent[0], axes, 0, 0, tiled=True)]]
  transfers between devices with their start and end apart: 5 -> 22, of which waited for: 5 -> 10; matrix products, arithmetic and copies ran while one was open for 2% -> 1% of each run, Pallas kernels for 5% -> 5%
where the time goes in v1:
time: 95 us; the launch traced here: 94.5 us
  waiting for transfers between devices  43.1 us (45%)
  starting transfers between devices  31.6 us (33%)
  Pallas kernels  15.6 us (16%)
  local copies, waits for them, and re-layouts  3.89 us (4%)
    ppermute x14, waiting for transfers between devices, shift(): return lax.ppermute(x, axes, [(i, i ^ mask) for i in range(count)])  43.1 us
    ppermute x14, starting transfers between devices, shift(): return lax.ppermute(x, axes, [(i, i ^ mask) for i in range(count)])  16.7 us
    all_to_all x2, starting transfers between devices, deliver(): return [lax.all_to_all(sent[0], axes, 0, 0, tiled=True)]  12.3 us
    pallas_call x1, Pallas kernels, local(): pl.pallas_call(functools.partial(langreth_kernel, came_spots), out_shape=...  8.13 us
    pallas_call x2, Pallas kernels, local(): pl.pallas_call(functools.partial(pack_kernel, blocks, sent_spots), out_sh...  3.92 us
    unnamed x26, local copies, waits for them, and re-layouts  3.4 us
    pallas_call x2, Pallas kernels, local(): pl.pallas_call(functools.partial(middle_kernel, start, came_spots[tag], s...  3.39 us
    ppermute x6, starting transfers between devices, gather(): held[turn ^ bit] = lax.ppermute(piece, 'orb', swap)  2.53 us
  transfers between devices with their start and end apart: 22, of which 10 were waited for; matrix products, arithmetic and copies ran while one was open for 1% of the time, Pallas kernels for 5%

profile of v1, /device:TPU:0, one launch (start us, length us, event | category | flops | bytes accessed | tf_op | source)
XLA Modules:
  0.0 94.5 jit_solution(11361467985323805267)
XLA Ops:
  1.2 2.3 %shard_map.28 = (bf16[8,2,1,128,128]{4,3,2,1,0:T(8,128)(2,1)S(1)}, bf16[32,1,2,4,8,128]{5,4,3,2,1,0:T(8,128)(2,1)}) custom-call(s32[1]{0:T(128)} %bitcast.device_ref, bf16[2,1,4,256,256]{4,3,2,1,0:T(8,128)(2,1)S(1)} %copy-done), custom_call_target="tpu_custom_call" | custom-call | tf_op jit(solution)/shard_map/pallas_call | solution.py:413
  3.6 7.3 %all-to-all-start = ((bf16[32,1,2,4,8,128]{5,4,3,2,1,0:T(8,128)(2,1)}), bf16[32,1,2,4,8,128]{5,4,3,2,1,0:T(8,128)(2,1)S(1)}, u32[]{:S(2)}, u32[]{:S(2)}) async-start(bf16[32,1,2,4,8,128]{5,4,3,2,1,0:T(8,128)(2,1)} %get-tuple-element.24), calls=%async_computation | async-start | bytes 1048576 | tf_op jit(solution)/shard_map/all_to_all | solution.py:408
  10.9 1.6 %shard_map.30 = (bf16[8,2,1,128,128]{4,3,2,1,0:T(8,128)(2,1)S(1)}, bf16[2,4,1,2,4,8,128]{6,5,4,3,2,1,0:T(8,128)(2,1)S(1)}, bf16[2,4,1,2,4,8,128]{6,5,4,3,2,1,0:T...) custom-call(s32[1]{0:T(128)} %bitcast.device_ref, ...), custom_call_target="tpu_custom_call" | custom-call | tf_op jit(solution)/shard_map/pallas_call | solution.py:413
  12.5 1.8 %collective-permute-start = (bf16[2,4,1,2,4,8,128]{6,5,4,3,2,1,0:T(8,128)(2,1)S(1)}, bf16[2,4,1,2,4,8,128]{6,5,4,3,2,1,0:T(8,128)(2,1)S(1)}, u32[]{:S(2)}, u32[]{:S(2)}) collective-permute-start(bf16[2,4,1,2,4,8,128]{6,5,4,3,2,1,0:T(8,128)(2,1)S(1)} %get-tuple-element.26), channel_id=1, source_target_pairs={{0,8},{1,9},{2,10},{3,11},{4,12},{5,13},{6,14},{7,15},{8,0},{9,1},... | collective-permute-start | bytes 393224 | tf_op jit(solution)/shard_map/ppermute | solution.py:346
  14.4 2.4 %collective-permute-start.1 = (bf16[2,4,1,2,4,8,128]{6,5,4,3,2,1,0:T(8,128)(2,1)S(1)}, bf16[2,4,1,2,4,8,128]{6,5,4,3,2,1,0:T(8,128)(2,1)S(1)}, u32[]{:S(2)}, u32[]{:S(2)}) collective-permute-start(bf16[2,4,1,2,4,8,128]{6,5,4,3,2,1,0:T(8,128)(2,1)S(1)} %get-tuple-element.27), channel_id=1, source_target_pairs={{0,16},{1,17},{2,18},{3,19},{4,20},{5,21},{6,22},{7,23},{8,24},{9,... | collective-permute-start | bytes 393224 | tf_op jit(solution)/shard_map/ppermute | solution.py:346
  17.0 1.8 %collective-permute-start.18 = (bf16[8,2,1,128,128]{4,3,2,1,0:T(8,128)(2,1)S(1)}, bf16[8,2,1,128,128]{4,3,2,1,0:T(8,128)(2,1)}, u32[]{:S(2)}, u32[]{:S(2)}) collective-permute-start(bf16[8,2,1,128,128]{4,3,2,1,0:T(8,128)(2,1)S(1)} %get-tuple-element.42.refs_9_), channel_id=1, source_target_pairs={{0,2},{1,3},{2,0},{3,1},{4,6},{5,7},{6,4},{7,5},{8,10},{9,11},{10,... | collective-permute-start | bytes 1572872 | tf_op jit(solution)/shard_map/ppermute | solution.py:376
  19.0 4.9 %collective-permute-done.refs_1_ = bf16[2,4,1,2,4,8,128]{6,5,4,3,2,1,0:T(8,128)(2,1)S(1)} collective-permute-done((bf16[2,4,1,2,4,8,128]{6,5,4,3,2,1,0:T(8,128)(2,1)S(1)}, bf16[2,4,1,2,4,8,128]{6,5,4,3,2,1,0:T(8,128)(2,1)S(1)}, u32[]{:S(2)}, u32[]{:S(2)}) %collective-permute-start) | collective-permute-done | bytes 131104 | tf_op jit(solution)/shard_map/ppermute | solution.py:346
  23.9 11.0 %collective-permute-done.1.refs_2_ = bf16[2,4,1,2,4,8,128]{6,5,4,3,2,1,0:T(8,128)(2,1)S(1)} collective-permute-done((bf16[2,4,1,2,4,8,128]{6,5,4,3,2,1,0:T(8,128)(2,1)S(1)}, bf16[2,4,1,2,4,8,128]{6,5,4,3,2,1,0:T(8,128)(2,1)S(1)}, u32[]{:S(2)}, u32[]{:S(2)}) %collective-permute-start.1) | collective-permute-done | bytes 131104 | tf_op jit(solution)/shard_map/ppermute | solution.py:346
  36.3 2.1 %shard_map.29 = bf16[32,1,2,4,8,128]{5,4,3,2,1,0:T(8,128)(2,1)} custom-call(s32[1]{0:T(128)} %bitcast.device_ref, bf16[128,128]{1,0:T(8,128)(2,1)S(1)} %convert_element_type.14.weight_ref, bf16[32,1,2,4,8,128]{5,4,3,2,1,0:T(8,128)(2,1)S(1)} %all-to-all-done.refs_0_), custom_call_target="tpu_custom_call" | custom-call | tf_op jit(solution)/shard_map/pallas_call | solution.py:428
  38.3 5.0 %all-to-all-start.1 = ((bf16[32,1,2,4,8,128]{5,4,3,2,1,0:T(8,128)(2,1)}), bf16[32,1,2,4,8,128]{5,4,3,2,1,0:T(8,128)(2,1)S(1)}, u32[]{:S(2)}, u32[]{:S(2)}) async-start(bf16[32,1,2,4,8,128]{5,4,3,2,1,0:T(8,128)(2,1)} %shard_map.29), calls=%async_computation.1 | async-start | bytes 1048576 | tf_op jit(solution)/shard_map/all_to_all | solution.py:408
  43.4 1.8 %collective-permute-start.4 = (bf16[2,4,1,2,4,8,128]{6,5,4,3,2,1,0:T(8,128)(2,1)S(1)}, bf16[2,4,1,2,4,8,128]{6,5,4,3,2,1,0:T(8,128)(2,1)S(1)}, u32[]{:S(2)}, u32[]{:S(2)}) collective-permute-start(bf16[2,4,1,2,4,8,128]{6,5,4,3,2,1,0:T(8,128)(2,1)S(1)} %get-tuple-element.30), channel_id=1, source_target_pairs={{0,2},{1,3},{2,0},{3,1},{4,6},{5,7},{6,4},{7,5},{8,10},{9,11},{10,... | collective-permute-start | bytes 393224 | tf_op jit(solution)/shard_map/ppermute | solution.py:346
  45.2 1.5 %collective-permute-start.5 = (bf16[2,4,1,2,4,8,128]{6,5,4,3,2,1,0:T(8,128)(2,1)S(1)}, bf16[2,4,1,2,4,8,128]{6,5,4,3,2,1,0:T(8,128)(2,1)S(1)}, u32[]{:S(2)}, u32[]{:S(2)}) collective-permute-start(bf16[2,4,1,2,4,8,128]{6,5,4,3,2,1,0:T(8,128)(2,1)S(1)} %get-tuple-element.31), channel_id=1, source_target_pairs={{0,4},{1,5},{2,6},{3,7},{4,0},{5,1},{6,2},{7,3},{8,12},{9,13},{10,... | collective-permute-start | bytes 393224 | tf_op jit(solution)/shard_map/ppermute | solution.py:346
  46.9 6.9 %collective-permute-done.4.refs_1_ = bf16[2,4,1,2,4,8,128]{6,5,4,3,2,1,0:T(8,128)(2,1)S(1)} collective-permute-done((bf16[2,4,1,2,4,8,128]{6,5,4,3,2,1,0:T(8,128)(2,1)S(1)}, bf16[2,4,1,2,4,8,128]{6,5,4,3,2,1,0:T(8,128)(2,1)S(1)}, u32[]{:S(2)}, u32[]{:S(2)}) %collective-permute-start.4) | collective-permute-done | bytes 131104 | tf_op jit(solution)/shard_map/ppermute | solution.py:346
  54.3 3.6 %collective-permute-done.6.refs_3_ = bf16[2,4,1,2,4,8,128]{6,5,4,3,2,1,0:T(8,128)(2,1)S(1)} collective-permute-done((bf16[2,4,1,2,4,8,128]{6,5,4,3,2,1,0:T(8,128)(2,1)S(1)}, bf16[2,4,1,2,4,8,128]{6,5,4,3,2,1,0:T(8,128)(2,1)S(1)}, u32[]{:S(2)}, u32[]{:S(2)}) %collective-permute-start.6) | collective-permute-done | bytes 131104 | tf_op jit(solution)/shard_map/ppermute | solution.py:346
  57.9 1.3 %shard_map.31 = (bf16[2,4,1,2,4,8,128]{6,5,4,3,2,1,0:T(8,128)(2,1)S(1)}, bf16[2,4,1,2,4,8,128]{6,5,4,3,2,1,0:T(8,128)(2,1)S(1)}, bf16[2,4,1,2,4,8,128]{6,5,4,3,2...) custom-call(s32[1]{0:T(128)} %bitcast.device_ref, bf16[128,128]{1,0:T(8,128)(2,1)S(1)} %convert_element_type.14.weight_ref, ...), custom_call_target="tpu_custom_call" | custom-call | tf_op jit(solution)/shard_map/pallas_call | solution.py:428
  59.2 1.6 %collective-permute-start.7 = (bf16[2,4,1,2,4,8,128]{6,5,4,3,2,1,0:T(8,128)(2,1)S(1)}, bf16[2,4,1,2,4,8,128]{6,5,4,3,2,1,0:T(8,128)(2,1)S(1)}, u32[]{:S(2)}, u32[]{:S(2)}) collective-permute-start(bf16[2,4,1,2,4,8,128]{6,5,4,3,2,1,0:T(8,128)(2,1)S(1)} %get-tuple-element.34), channel_id=1, source_target_pairs={{0,8},{1,9},{2,10},{3,11},{4,12},{5,13},{6,14},{7,15},{8,0},{9,1},... | collective-permute-start | bytes 393224 | tf_op jit(solution)/shard_map/ppermute | solution.py:346
  60.8 2.7 %collective-permute-start.8 = (bf16[2,4,1,2,4,8,128]{6,5,4,3,2,1,0:T(8,128)(2,1)S(1)}, bf16[2,4,1,2,4,8,128]{6,5,4,3,2,1,0:T(8,128)(2,1)S(1)}, u32[]{:S(2)}, u32[]{:S(2)}) collective-permute-start(bf16[2,4,1,2,4,8,128]{6,5,4,3,2,1,0:T(8,128)(2,1)S(1)} %get-tuple-element.35), channel_id=1, source_target_pairs={{0,16},{1,17},{2,18},{3,19},{4,20},{5,21},{6,22},{7,23},{8,24},{9,... | collective-permute-start | bytes 393224 | tf_op jit(solution)/shard_map/ppermute | solution.py:346
  63.8 1.6 %collective-permute-done.7.refs_1_ = bf16[2,4,1,2,4,8,128]{6,5,4,3,2,1,0:T(8,128)(2,1)S(1)} collective-permute-done((bf16[2,4,1,2,4,8,128]{6,5,4,3,2,1,0:T(8,128)(2,1)S(1)}, bf16[2,4,1,2,4,8,128]{6,5,4,3,2,1,0:T(8,128)(2,1)S(1)}, u32[]{:S(2)}, u32[]{:S(2)}) %collective-permute-start.7) | collective-permute-done | bytes 131104 | tf_op jit(solution)/shard_map/ppermute | solution.py:346
  65.4 8.1 %collective-permute-done.8.refs_2_ = bf16[2,4,1,2,4,8,128]{6,5,4,3,2,1,0:T(8,128)(2,1)S(1)} collective-permute-done((bf16[2,4,1,2,4,8,128]{6,5,4,3,2,1,0:T(8,128)(2,1)S(1)}, bf16[2,4,1,2,4,8,128]{6,5,4,3,2,1,0:T(8,128)(2,1)S(1)}, u32[]{:S(2)}, u32[]{:S(2)}) %collective-permute-start.8) | collective-permute-done | bytes 131104 | tf_op jit(solution)/shard_map/ppermute | solution.py:346
  74.1 1.9 %collective-permute-done.10.refs_4_ = bf16[4,4,1,2,4,8,128]{6,5,4,3,2,1,0:T(8,128)(2,1)S(1)} collective-permute-done((bf16[4,4,1,2,4,8,128]{6,5,4,3,2,1,0:T(8,128)(2,1)S(1)}, bf16[4,4,1,2,4,8,128]{6,5,4,3,2,1,0:T(8,128)(2,1)S(1)}, u32[]{:S(2)}, u32[]{:S(2)}) %collective-permute-start.10) | collective-permute-done | bytes 262176 | tf_op jit(solution)/shard_map/ppermute | solution.py:346
  78.0 2.2 %collective-permute-start.13 = (bf16[2,4,1,2,4,8,128]{6,5,4,3,2,1,0:T(8,128)(2,1)S(1)}, bf16[2,4,1,2,4,8,128]{6,5,4,3,2,1,0:T(8,128)(2,1)S(1)}, u32[]{:S(2)}, u32[]{:S(2)}) collective-permute-start(bf16[2,4,1,2,4,8,128]{6,5,4,3,2,1,0:T(8,128)(2,1)S(1)} %get-tuple-element.40), channel_id=1, source_target_pairs={{0,6},{1,7},{2,4},{3,5},{4,2},{5,3},{6,0},{7,1},{8,14},{9,15},{10,... | collective-permute-start | bytes 393224 | tf_op jit(solution)/shard_map/ppermute | solution.py:346
  80.2 2.9 %collective-permute-done.11.refs_2_ = bf16[2,4,1,2,4,8,128]{6,5,4,3,2,1,0:T(8,128)(2,1)S(1)} collective-permute-done((bf16[2,4,1,2,4,8,128]{6,5,4,3,2,1,0:T(8,128)(2,1)S(1)}, bf16[2,4,1,2,4,8,128]{6,5,4,3,2,1,0:T(8,128)(2,1)S(1)}, u32[]{:S(2)}, u32[]{:S(2)}) %collective-permute-start.11) | collective-permute-done | bytes 131104 | tf_op jit(solution)/shard_map/ppermute | solution.py:346
  83.4 2.0 %collective-permute-done.13.refs_4_ = bf16[2,4,1,2,4,8,128]{6,5,4,3,2,1,0:T(8,128)(2,1)S(1)} collective-permute-done((bf16[2,4,1,2,4,8,128]{6,5,4,3,2,1,0:T(8,128)(2,1)S(1)}, bf16[2,4,1,2,4,8,128]{6,5,4,3,2,1,0:T(8,128)(2,1)S(1)}, u32[]{:S(2)}, u32[]{:S(2)}) %collective-permute-start.13) | collective-permute-done | bytes 131104 | tf_op jit(solution)/shard_map/ppermute | solution.py:346
  86.4 8.1 %langreth.1 = bf16[2,1,4,256,256]{4,3,2,1,0:T(8,128)(2,1)} custom-call(s32[1]{0:T(128)} %bitcast.device_ref, bf16[32,1,2,4,8,128]{5,4,3,2,1,0:T(8,128)(2,1)} %copy-done.5, bf16[2,4,1,2,4,8,128]{6,5,4,3,2,1,0:T(8,128)(2,1)} %copy-done.4, bf16[2,4,1,2,4,8,128]{6,5,4,3,2,1,0:T(8,128)(2,1)} %copy-done.9, bf16[2,4,1,2,4,8,128]{6,5,4,3,2,1,0:T(8,128)(2,1)} %copy-done.10, ...), custom_call_target="tpu_custom_call" | custom-call | tf_op jit(solution)/shard_map/langreth/pallas_call | solution.py:442
  (58 shorter events, 8.0 us)
Async XLA Ops:
  3.6 50.2 %copy-start.2 = (bf16[8,2,1,128,128]{4,3,2,1,0:T(8,128)(2,1)}, bf16[8,2,1,128,128]{4,3,2,1,0:T(8,128)(2,1)S(1)}, u32[]{:S(2)}) copy-start(bf16[8,2,1,128,128]{4,3,2,1,0:T(8,128)(2,1)S(1)} %get-tuple-element.41.refs_5_) | copy-start | bytes 1572868
  3.6 32.7 %all-to-all-start = ((bf16[32,1,2,4,8,128]{5,4,3,2,1,0:T(8,128)(2,1)}), bf16[32,1,2,4,8,128]{5,4,3,2,1,0:T(8,128)(2,1)S(1)}, u32[]{:S(2)}, u32[]{:S(2)}) async-start(bf16[32,1,2,4,8,128]{5,4,3,2,1,0:T(8,128)(2,1)} %get-tuple-element.24), calls=%async_computation | async-start | bytes 1048576 | tf_op jit(solution)/shard_map/all_to_all | solution.py:408
  12.5 41.3 %copy-start.3 = (bf16[8,2,1,128,128]{4,3,2,1,0:T(8,128)(2,1)}, bf16[8,2,1,128,128]{4,3,2,1,0:T(8,128)(2,1)S(1)}, u32[]{:S(2)}) copy-start(bf16[8,2,1,128,128]{4,3,2,1,0:T(8,128)(2,1)S(1)} %get-tuple-element.42.refs_9_) | copy-start | bytes 1572868
  12.5 11.4 %collective-permute-start = (bf16[2,4,1,2,4,8,128]{6,5,4,3,2,1,0:T(8,128)(2,1)S(1)}, bf16[2,4,1,2,4,8,128]{6,5,4,3,2,1,0:T(8,128)(2,1)S(1)}, u32[]{:S(2)}, u32[]{:S(2)}) collective-permute-start(bf16[2,4,1,2,4,8,128]{6,5,4,3,2,1,0:T(8,128)(2,1)S(1)} %get-tuple-element.26), channel_id=1, source_target_pairs={{0,8},{1,9},{2,10},{3,11},{4,12},{5,13},{6,14},{7,15},{8,0},{9,1},... | collective-permute-start | bytes 393224 | tf_op jit(solution)/shard_map/ppermute | solution.py:346
  14.4 20.5 %collective-permute-start.1 = (bf16[2,4,1,2,4,8,128]{6,5,4,3,2,1,0:T(8,128)(2,1)S(1)}, bf16[2,4,1,2,4,8,128]{6,5,4,3,2,1,0:T(8,128)(2,1)S(1)}, u32[]{:S(2)}, u32[]{:S(2)}) collective-permute-start(bf16[2,4,1,2,4,8,128]{6,5,4,3,2,1,0:T(8,128)(2,1)S(1)} %get-tuple-element.27), channel_id=1, source_target_pairs={{0,16},{1,17},{2,18},{3,19},{4,20},{5,21},{6,22},{7,23},{8,24},{9,... | collective-permute-start | bytes 393224 | tf_op jit(solution)/shard_map/ppermute | solution.py:346
  16.8 18.1 %collective-permute-start.2 = (bf16[2,4,1,2,4,8,128]{6,5,4,3,2,1,0:T(8,128)(2,1)S(1)}, bf16[2,4,1,2,4,8,128]{6,5,4,3,2,1,0:T(8,128)(2,1)S(1)}, u32[]{:S(2)}, u32[]{:S(2)}) collective-permute-start(bf16[2,4,1,2,4,8,128]{6,5,4,3,2,1,0:T(8,128)(2,1)S(1)} %get-tuple-element.28), channel_id=1, source_target_pairs={{0,24},{1,25},{2,26},{3,27},{4,28},{5,29},{6,30},{7,31},{8,16},{9,... | collective-permute-start | bytes 393224 | tf_op jit(solution)/shard_map/ppermute | solution.py:346
  17.0 43.8 %collective-permute-start.18 = (bf16[8,2,1,128,128]{4,3,2,1,0:T(8,128)(2,1)S(1)}, bf16[8,2,1,128,128]{4,3,2,1,0:T(8,128)(2,1)}, u32[]{:S(2)}, u32[]{:S(2)}) collective-permute-start(bf16[8,2,1,128,128]{4,3,2,1,0:T(8,128)(2,1)S(1)} %get-tuple-element.42.refs_9_), channel_id=1, source_target_pairs={{0,2},{1,3},{2,0},{3,1},{4,6},{5,7},{6,4},{7,5},{8,10},{9,11},{10,... | collective-permute-start | bytes 1572872 | tf_op jit(solution)/shard_map/ppermute | solution.py:376
  18.8 44.8 %collective-permute-start.15 = (bf16[8,2,1,128,128]{4,3,2,1,0:T(8,128)(2,1)S(1)}, bf16[8,2,1,128,128]{4,3,2,1,0:T(8,128)(2,1)}, u32[]{:S(2)}, u32[]{:S(2)}) collective-permute-start(bf16[8,2,1,128,128]{4,3,2,1,0:T(8,128)(2,1)S(1)} %get-tuple-element.41.refs_5_), channel_id=1, source_target_pairs={{0,2},{1,3},{2,0},{3,1},{4,6},{5,7},{6,4},{7,5},{8,10},{9,11},{10,... | collective-permute-start | bytes 1572872 | tf_op jit(solution)/shard_map/ppermute | solution.py:376
  34.9 8.4 %collective-permute-start.3 = (bf16[4,4,1,2,4,8,128]{6,5,4,3,2,1,0:T(8,128)(2,1)S(1)}, bf16[4,4,1,2,4,8,128]{6,5,4,3,2,1,0:T(8,128)(2,1)S(1)}, u32[]{:S(2)}, u32[]{:S(2)}) collective-permute-start(bf16[4,4,1,2,4,8,128]{6,5,4,3,2,1,0:T(8,128)(2,1)S(1)} %near.2), channel_id=1, source_target_pairs={{0,1},{1,0},{2,3},{3,2},{4,5},{5,4},{6,7},{7,6},{8,9},{9,8},{10,11... | collective-permute-start | bytes 786440 | tf_op jit(solution)/shard_map/ppermute | solution.py:346
  38.3 47.1 %all-to-all-start.1 = ((bf16[32,1,2,4,8,128]{5,4,3,2,1,0:T(8,128)(2,1)}), bf16[32,1,2,4,8,128]{5,4,3,2,1,0:T(8,128)(2,1)S(1)}, u32[]{:S(2)}, u32[]{:S(2)}) async-start(bf16[32,1,2,4,8,128]{5,4,3,2,1,0:T(8,128)(2,1)} %shard_map.29), calls=%async_computation.1 | async-start | bytes 1048576 | tf_op jit(solution)/shard_map/all_to_all | solution.py:408
  43.4 10.4 %collective-permute-start.4 = (bf16[2,4,1,2,4,8,128]{6,5,4,3,2,1,0:T(8,128)(2,1)S(1)}, bf16[2,4,1,2,4,8,128]{6,5,4,3,2,1,0:T(8,128)(2,1)S(1)}, u32[]{:S(2)}, u32[]{:S(2)}) collective-permute-start(bf16[2,4,1,2,4,8,128]{6,5,4,3,2,1,0:T(8,128)(2,1)S(1)} %get-tuple-element.30), channel_id=1, source_target_pairs={{0,2},{1,3},{2,0},{3,1},{4,6},{5,7},{6,4},{7,5},{8,10},{9,11},{10,... | collective-permute-start | bytes 393224 | tf_op jit(solution)/shard_map/ppermute | solution.py:346
  45.2 8.6 %collective-permute-start.5 = (bf16[2,4,1,2,4,8,128]{6,5,4,3,2,1,0:T(8,128)(2,1)S(1)}, bf16[2,4,1,2,4,8,128]{6,5,4,3,2,1,0:T(8,128)(2,1)S(1)}, u32[]{:S(2)}, u32[]{:S(2)}) collective-permute-start(bf16[2,4,1,2,4,8,128]{6,5,4,3,2,1,0:T(8,128)(2,1)S(1)} %get-tuple-element.31), channel_id=1, source_target_pairs={{0,4},{1,5},{2,6},{3,7},{4,0},{5,1},{6,2},{7,3},{8,12},{9,13},{10,... | collective-permute-start | bytes 393224 | tf_op jit(solution)/shard_map/ppermute | solution.py:346
  46.7 11.2 %collective-permute-start.6 = (bf16[2,4,1,2,4,8,128]{6,5,4,3,2,1,0:T(8,128)(2,1)S(1)}, bf16[2,4,1,2,4,8,128]{6,5,4,3,2,1,0:T(8,128)(2,1)S(1)}, u32[]{:S(2)}, u32[]{:S(2)}) collective-permute-start(bf16[2,4,1,2,4,8,128]{6,5,4,3,2,1,0:T(8,128)(2,1)S(1)} %get-tuple-element.32), channel_id=1, source_target_pairs={{0,6},{1,7},{2,4},{3,5},{4,2},{5,3},{6,0},{7,1},{8,14},{9,15},{10,... | collective-permute-start | bytes 393224 | tf_op jit(solution)/shard_map/ppermute | solution.py:346
  53.8 23.5 %collective-permute-start.17 = (bf16[8,2,1,128,128]{4,3,2,1,0:T(8,128)(2,1)S(1)}, bf16[8,2,1,128,128]{4,3,2,1,0:T(8,128)(2,1)S(1)}, u32[]{:S(2)}, u32[]{:S(2)}) collective-permute-start(bf16[8,2,1,128,128]{4,3,2,1,0:T(8,128)(2,1)S(1)} %get-tuple-element.42.refs_9_), channel_id=1, source_target_pairs={{0,1},{1,0},{2,3},{3,2},{4,5},{5,4},{6,7},{7,6},{8,9},{9,8},{10,11... | collective-permute-start | bytes 1572872 | tf_op jit(solution)/shard_map/ppermute | solution.py:376
  53.8 24.1 %collective-permute-start.14 = (bf16[8,2,1,128,128]{4,3,2,1,0:T(8,128)(2,1)S(1)}, bf16[8,2,1,128,128]{4,3,2,1,0:T(8,128)(2,1)S(1)}, u32[]{:S(2)}, u32[]{:S(2)}) collective-permute-start(bf16[8,2,1,128,128]{4,3,2,1,0:T(8,128)(2,1)S(1)} %get-tuple-element.41.refs_5_), channel_id=1, source_target_pairs={{0,1},{1,0},{2,3},{3,2},{4,5},{5,4},{6,7},{7,6},{8,9},{9,8},{10,11... | collective-permute-start | bytes 1572872 | tf_op jit(solution)/shard_map/ppermute | solution.py:376
  59.2 6.2 %collective-permute-start.7 = (bf16[2,4,1,2,4,8,128]{6,5,4,3,2,1,0:T(8,128)(2,1)S(1)}, bf16[2,4,1,2,4,8,128]{6,5,4,3,2,1,0:T(8,128)(2,1)S(1)}, u32[]{:S(2)}, u32[]{:S(2)}) collective-permute-start(bf16[2,4,1,2,4,8,128]{6,5,4,3,2,1,0:T(8,128)(2,1)S(1)} %get-tuple-element.34), channel_id=1, source_target_pairs={{0,8},{1,9},{2,10},{3,11},{4,12},{5,13},{6,14},{7,15},{8,0},{9,1},... | collective-permute-start | bytes 393224 | tf_op jit(solution)/shard_map/ppermute | solution.py:346
  60.8 12.7 %collective-permute-start.8 = (bf16[2,4,1,2,4,8,128]{6,5,4,3,2,1,0:T(8,128)(2,1)S(1)}, bf16[2,4,1,2,4,8,128]{6,5,4,3,2,1,0:T(8,128)(2,1)S(1)}, u32[]{:S(2)}, u32[]{:S(2)}) collective-permute-start(bf16[2,4,1,2,4,8,128]{6,5,4,3,2,1,0:T(8,128)(2,1)S(1)} %get-tuple-element.35), channel_id=1, source_target_pairs={{0,16},{1,17},{2,18},{3,19},{4,20},{5,21},{6,22},{7,23},{8,24},{9,... | collective-permute-start | bytes 393224 | tf_op jit(solution)/shard_map/ppermute | solution.py:346
  63.6 9.9 %collective-permute-start.9 = (bf16[2,4,1,2,4,8,128]{6,5,4,3,2,1,0:T(8,128)(2,1)S(1)}, bf16[2,4,1,2,4,8,128]{6,5,4,3,2,1,0:T(8,128)(2,1)S(1)}, u32[]{:S(2)}, u32[]{:S(2)}) collective-permute-start(bf16[2,4,1,2,4,8,128]{6,5,4,3,2,1,0:T(8,128)(2,1)S(1)} %get-tuple-element.36), channel_id=1, source_target_pairs={{0,24},{1,25},{2,26},{3,27},{4,28},{5,29},{6,30},{7,31},{8,16},{9,... | collective-permute-start | bytes 393224 | tf_op jit(solution)/shard_map/ppermute | solution.py:346
  65.4 20.0 %collective-permute-start.19 = (bf16[8,2,1,128,128]{4,3,2,1,0:T(8,128)(2,1)}, bf16[8,2,1,128,128]{4,3,2,1,0:T(8,128)(2,1)S(1)}, u32[]{:S(2)}, u32[]{:S(2)}) collective-permute-start(bf16[8,2,1,128,128]{4,3,2,1,0:T(8,128)(2,1)} %collective-permute-done.18.refs_11_), channel_id=1, source_target_pairs={{0,1},{1,0},{2,3},{3,2},{4,5},{5,4},{6,7},{7,6},{8,9},{9,8},{10,11... | collective-permute-start | bytes 1572872 | tf_op jit(solution)/shard_map/ppermute | solution.py:376
  73.5 11.9 %collective-permute-start.16 = (bf16[8,2,1,128,128]{4,3,2,1,0:T(8,128)(2,1)}, bf16[8,2,1,128,128]{4,3,2,1,0:T(8,128)(2,1)}, u32[]{:S(2)}, u32[]{:S(2)}) collective-permute-start(bf16[8,2,1,128,128]{4,3,2,1,0:T(8,128)(2,1)} %collective-permute-done.15.refs_7_), channel_id=1, source_target_pairs={{0,1},{1,0},{2,3},{3,2},{4,5},{5,4},{6,7},{7,6},{8,9},{9,8},{10,11... | collective-permute-start | bytes 1572872 | tf_op jit(solution)/shard_map/ppermute | solution.py:376
  73.5 2.5 %collective-permute-start.10 = (bf16[4,4,1,2,4,8,128]{6,5,4,3,2,1,0:T(8,128)(2,1)S(1)}, bf16[4,4,1,2,4,8,128]{6,5,4,3,2,1,0:T(8,128)(2,1)S(1)}, u32[]{:S(2)}, u32[]{:S(2)}) collective-permute-start(bf16[4,4,1,2,4,8,128]{6,5,4,3,2,1,0:T(8,128)(2,1)S(1)} %near.3), channel_id=1, source_target_pairs={{0,1},{1,0},{2,3},{3,2},{4,5},{5,4},{6,7},{7,6},{8,9},{9,8},{10,11... | collective-permute-start | bytes 786440 | tf_op jit(solution)/shard_map/ppermute | solution.py:346
  76.7 6.4 %collective-permute-start.11 = (bf16[2,4,1,2,4,8,128]{6,5,4,3,2,1,0:T(8,128)(2,1)S(1)}, bf16[2,4,1,2,4,8,128]{6,5,4,3,2,1,0:T(8,128)(2,1)S(1)}, u32[]{:S(2)}, u32[]{:S(2)}) collective-permute-start(bf16[2,4,1,2,4,8,128]{6,5,4,3,2,1,0:T(8,128)(2,1)S(1)} %get-tuple-element.38), channel_id=1, source_target_pairs={{0,2},{1,3},{2,0},{3,1},{4,6},{5,7},{6,4},{7,5},{8,10},{9,11},{10,... | collective-permute-start | bytes 393224 | tf_op jit(solution)/shard_map/ppermute | solution.py:346
  77.3 6.1 %collective-permute-start.12 = (bf16[2,4,1,2,4,8,128]{6,5,4,3,2,1,0:T(8,128)(2,1)S(1)}, bf16[2,4,1,2,4,8,128]{6,5,4,3,2,1,0:T(8,128)(2,1)S(1)}, u32[]{:S(2)}, u32[]{:S(2)}) collective-permute-start(bf16[2,4,1,2,4,8,128]{6,5,4,3,2,1,0:T(8,128)(2,1)S(1)} %get-tuple-element.39), channel_id=1, source_target_pairs={{0,4},{1,5},{2,6},{3,7},{4,0},{5,1},{6,2},{7,3},{8,12},{9,13},{10,... | collective-permute-start | bytes 393224 | tf_op jit(solution)/shard_map/ppermute | solution.py:346
  78.0 7.4 %collective-permute-start.13 = (bf16[2,4,1,2,4,8,128]{6,5,4,3,2,1,0:T(8,128)(2,1)S(1)}, bf16[2,4,1,2,4,8,128]{6,5,4,3,2,1,0:T(8,128)(2,1)S(1)}, u32[]{:S(2)}, u32[]{:S(2)}) collective-permute-start(bf16[2,4,1,2,4,8,128]{6,5,4,3,2,1,0:T(8,128)(2,1)S(1)} %get-tuple-element.40), channel_id=1, source_target_pairs={{0,6},{1,7},{2,4},{3,5},{4,2},{5,3},{6,0},{7,1},{8,14},{9,15},{10,... | collective-permute-start | bytes 393224 | tf_op jit(solution)/shard_map/ppermute | solution.py:346
  (11 other events, 34.7 us)

commit v2 on v1

--- a/solution.py
+++ b/solution.py
@@ -61,23 +61,23 @@
 
 
 def pack_kernel(blocks, spots, device_ref, green_ref, *refs):
-    raw_ref, out_refs, block_scr, green_scr, sems = refs[0], refs[1:-3], refs[-3], refs[-2], refs[-1]
+    raw_ref, out_refs, block_scr, sems = refs[0], refs[1:-2], refs[-2], refs[-1]
     count, momenta, parts, pairs, _, half = block_scr.shape
     row, col = grid_masks(half)
 
-    def fetch(step, target=green_scr, kind=0):
+    def fetch(step):
         part, pair = step // pairs, step % pairs
         return [
             pltpu.make_async_copy(
                 green_ref.at[part, :, pair, pl.ds(i * half, half), pl.ds(j * half, half)],
-                target.at[step, n],
-                sems.at[kind, step, n],
+                raw_ref.at[step, n],
+                sems.at[step, n],
             )
             for n, (i, j) in enumerate(blocks)
         ]
 
     def begin(step, carry):
-        for copy in fetch(step) + fetch(step, raw_ref, 1):
+        for copy in fetch(step):
             copy.start()
         return carry
 
@@ -88,7 +88,7 @@
         for copy in fetch(step):
             copy.wait()
         for k in range(momenta):
-            got = {at: green_scr[step, n, k].astype(F32) for n, at in enumerate(blocks)}
+            got = {at: raw_ref[step, n, k].astype(F32) for n, at in enumerate(blocks)}
             own, facing = [], []
             if (0, 1) in got:
                 own.append(got[0, 1])
@@ -103,13 +103,6 @@
 
     lax.fori_loop(0, parts * pairs, one, 0)
     emit(block_scr, device_ref[0], out_refs, spots)
-
-    def finish(step, carry):
-        for copy in fetch(step, raw_ref, 1):
-            copy.wait()
-        return carry
-
-    lax.fori_loop(0, parts * pairs, finish, 0)
 
 
 def twiddle(re, im, angle):
@@ -221,55 +214,68 @@
             out_ref[1, z] = came_ref[z, m]
 
 
-def langreth_kernel(came_spots, device_ref, *refs):
-    left_scr, block_scr, green_scr, sems = refs[-4:]
-    kinds = green_scr.shape[0]
-    count, momenta, _, orbs, rows2, half = block_scr.shape[1:]
-    total = kinds * orbs
-    out_ref, green_any, self_refs = refs[-5], refs[-5 - total : -5], refs[: -5 - total]
-    copies = [
-        pltpu.make_async_copy(green_any[n], green_scr.at[n // orbs, n % orbs], sems.at[n]) for n in range(total)
-    ]
+SUMS = ("00", "01", "10", "r11", "l11")
+SLOTS = {"o": ("10", "01"), "d": ("s00", "s11", "t00", "t11")}
+
+
+def left_kernel(kinds, spots, device_ref, *refs):
+    self_refs, left_ref, block_scr = refs[:-2], refs[-2], refs[-1]
+    count, momenta, _, orbs, rows2, half = block_scr.shape
+    rows = rows2 // 2
+    here = device_ref[0]
+    me = here % orbs
+    collect(block_scr, here, self_refs, spots)
+    row, col = grid_masks(half)
+    lower, upper = row >= col, row < col
+    for k in range(momenta):
+        for turn in range(orbs):
+            c = me ^ turn
+            for part in range(2):
+                sheets = {}
+                piece = block_scr[:, k, part, c].astype(F32)
+                for index in range(2):
+                    sheet = jnp.concatenate([piece[d, index * rows : (index + 1) * rows] for d in range(count)], 0)
+                    for n, kind in enumerate(kinds):
+                        sheets[index, kind] = sheet[n * half : (n + 1) * half]
+                pieces = []
+                if "o" in kinds:
+                    pieces += [sheets[1, "o"].T, sheets[0, "o"]]
+                if "d" in kinds:
+                    own, facing = sheets[0, "d"], sheets[1, "d"].T
+                    pieces += [
+                        jnp.where(lower, own, 0.0),
+                        jnp.where(lower, facing, 0.0),
+                        jnp.where(upper, facing, 0.0),
+                        jnp.where(upper, own, 0.0),
+                    ]
+                at = slice(turn * half, (turn + 1) * half)
+                for n, piece in enumerate(pieces):
+                    left_ref[k, (2 * n + part) * half : (2 * n + part + 1) * half, at] = piece.astype(BF16)
+
+
+def langreth_kernel(kinds, sums_in, sums_out, device_ref, left_ref, *refs):
+    if sums_in:
+        sums_ref, green_scr, out_ref = refs
+    else:
+        out_ref, green_scr, sems = refs[-3:]
+    held, orbs = green_scr.shape[:2]
+    momenta, half = green_scr.shape[-3:-1]
+    copies = []
+    if not sums_in:
+        copies = [
+            pltpu.make_async_copy(green_any, green_scr.at[n // orbs, n % orbs], sems.at[n])
+            for n, green_any in enumerate(refs[:-3])
+        ]
     for copy in copies:
         copy.start()
-    here = device_ref[0]
-    me = here % orbs
-    rows = rows2 // 2
-    chunks = len(came_spots)
-    for n, spots in enumerate(came_spots):
-        used = entries(spots)
-        collect(block_scr.at[n], here, self_refs[:used], spots)
-        self_refs = self_refs[used:]
+    me = device_ref[0] % orbs
     row, col = grid_masks(half)
     lower, upper = row >= col, row < col
     keep = {1: lower.astype(F32).astype(BF16), -1: upper.astype(F32).astype(BF16)}
     scale = (2 * half) ** -0.5
     blocks = ((0, 0), (0, 1), (1, 0), (1, 1))
+    slots = sum((SLOTS[kind] for kind in kinds), ())
     for k in range(momenta):
-        for turn in range(orbs):
-            c = me ^ turn
-            for part in range(2):
-                sheets = {}
-                for n in range(chunks):
-                    piece = block_scr[n, :, k, part, c].astype(F32)
-                    for index in range(2):
-                        sheet = jnp.concatenate([piece[d, index * rows : (index + 1) * rows] for d in range(count)], 0)
-                        for low in range(2) if chunks == 1 else (n,):
-                            sheets[index, low] = sheet[low * half : (low + 1) * half] if chunks == 1 else sheet
-
-                own, facing = sheets[0, 1], sheets[1, 1].T
-                pieces = [
-                    jnp.where(lower, own, 0.0),
-                    sheets[1, 0].T,
-                    jnp.where(lower, facing, 0.0),
-                    jnp.where(upper, facing, 0.0),
-                    sheets[0, 0],
-                    jnp.where(upper, own, 0.0),
-                ]
-                at = slice(turn * half, (turn + 1) * half)
-                for n, piece in enumerate(pieces):
-                    left_scr[(2 * n + part) * half : (2 * n + part + 1) * half, at] = piece.astype(BF16)
-
         if k == 0:
             for copy in copies:
                 copy.wait()
@@ -277,17 +283,15 @@
             b = me ^ turn_b
 
             def block(turn, pair, part, i, j, mask):
-                kind, n = (int(i == j), i) if kinds == 2 else (0, (i == j) * 2 + i)
+                kind, n = (int(i == j), i) if held == 2 else (0, (i == j) * 2 + i)
                 piece = green_scr[kind, turn, part * orbs + pair, n, k]
                 return piece * keep[mask] if mask else piece
 
-            def left(first, last):
-                return left_scr[2 * first * half : 2 * last * half, :]
-
-            def rows_of(product, n):
-                return (product[2 * n * half : (2 * n + 1) * half], product[(2 * n + 1) * half : (2 * n + 2) * half])
-
-            def plain(first, last, i, j, mask):
+            def left(slot):
+                n = slots.index(slot)
+                return left_ref[k, 2 * n * half : 2 * (n + 1) * half, :]
+
+            def plain(slot, i, j, mask):
                 right = jnp.concatenate(
                     [
                         jnp.concatenate([block(turn, b, part, i, j, mask) for part in range(2)], 1)
@@ -295,14 +299,11 @@
                     ],
                     0,
                 )
-                product = jnp.dot(left(first, last), right, preferred_element_type=F32)
-                out = []
-                for n in range(last - first):
-                    real, imag = rows_of(product, n)
-                    out.append((real[:, :half] - imag[:, half:], real[:, half:] + imag[:, :half]))
-                return out
-
-            def adjoint(first, last, i, j, mask):
+                product = jnp.dot(left(slot), right, preferred_element_type=F32)
+                real, imag = product[:half], product[half:]
+                return real[:, :half] - imag[:, half:], real[:, half:] + imag[:, :half]
+
+            def adjoint(slot, i, j, mask):
                 right = jnp.concatenate(
                     [
                         jnp.concatenate([block(turn_b, me ^ turn, part, i, j, mask) for part in range(2)], 0)
@@ -311,29 +312,42 @@
                     1,
                 )
                 product = lax.dot_general(
-                    left(first, last), right, (((1,), (1,)), ((), ())), preferred_element_type=F32
+                    left(slot), right, (((1,), (1,)), ((), ())), preferred_element_type=F32
                 )
-                out = []
-                for n in range(last - first):
-                    real, imag = rows_of(product, n)
-                    out.append((real[:, :half] + imag[:, half:], imag[:, :half] - real[:, half:]))
-                return out
-
-            d1 = plain(0, 2, 0, 0, 1)
-            d2 = plain(0, 2, 0, 1, 0)
-            d3 = plain(0, 1, 0, 0, -1)[0]
-            d4 = plain(2, 3, 1, 0, 0)[0]
-            d5 = plain(2, 3, 1, 1, 1)[0]
-            d6 = plain(2, 3, 1, 1, -1)[0]
-            d7 = adjoint(3, 4, 0, 0, 1)[0]
-            d8 = adjoint(3, 4, 1, 0, 0)[0]
-            d9 = adjoint(4, 6, 1, 1, 1)
+                real, imag = product[:half], product[half:]
+                return real[:, :half] + imag[:, half:], imag[:, :half] - real[:, half:]
+
+            def total_of(*terms):
+                return tuple(sum(term[part] for term in terms) for part in range(2))
+
+            terms = {name: [] for name in SUMS}
+            if sums_in:
+                for n, name in enumerate(SUMS):
+                    terms[name].append(tuple(sums_ref[n, part, k, b] for part in range(2)))
+            if "o" in kinds:
+                terms["01"].append(adjoint("01", 1, 1, 1))
+                terms["10"].append(plain("10", 0, 0, 1))
+                terms["l11"].append(plain("10", 0, 1, 0))
+            if "d" in kinds:
+                retarded = plain("s00", 0, 0, 1)
+                lesser = total_of(plain("s00", 0, 0, -1), adjoint("t00", 0, 0, 1))
+                terms["00"].append(tuple(jnp.where(lower, r, l) for r, l in zip(retarded, lesser)))
+                terms["01"] += [plain("s00", 0, 1, 0), adjoint("t00", 1, 0, 0)]
+                terms["10"].append(plain("s11", 1, 0, 0))
+                terms["r11"].append(plain("s11", 1, 1, 1))
+                terms["l11"] += [plain("s11", 1, 1, -1), adjoint("t11", 1, 1, 1)]
+            got = {name: total_of(*terms[name]) for name in SUMS}
+            if sums_out:
+                for n, name in enumerate(SUMS):
+                    for part in range(2):
+                        out_ref[n, part, k, b] = got[name][part]
+                continue
             for part in range(2):
                 results = (
-                    jnp.where(lower, d1[0][part], d3[part] + d7[part]),
-                    d2[0][part] + d8[part] + d9[0][part],
-                    d1[1][part] + d4[part],
-                    jnp.where(lower, d5[part], d2[1][part] + d6[part] + d9[1][part]),
+                    got["00"][part],
+                    got["01"][part],
+                    got["10"][part],
+                    jnp.where(lower, got["r11"][part], got["l11"][part]),
                 )
                 for (i, j), result in zip(blocks, results):
                     out_ref[part, k, b, i * half : (i + 1) * half, j * half : (j + 1) * half] = (
@@ -394,7 +408,10 @@
     width = parts * momenta * wide * half
 
     off, on = ((0, 1), (1, 0)), ((0, 0), (1, 1))
-    plan = [("d", on, 0, True), ("o", off, None, False)] if chunks == 2 else [("o", off + on, -half, False)]
+    if chunks == 2:
+        plan = [("d", on, 0, True, False), ("o", off, None, False, True)]
+    else:
+        plan = [("o", off + on, -half, False, False)]
     returned, greens, came_spots = {}, {}, {}
 
     def sheets(staged):
@@ -407,52 +424,64 @@
             return exchange(axes, count, sent)
         return [lax.all_to_all(sent[0], axes, 0, 0, tiled=True)]
 
-    for tag, blocks, start, staged in plan:
-        sent_spots = places(count, 2 * planes, True) if staged else None
-        came_spots[tag] = places(count, 2 * planes, False) if staged else None
+    def spots(staged, sent):
+        return places(count, 2 * planes, sent) if staged else None
+
+    for tag, blocks, start, staged, staged_back in plan:
+        came_spots[tag] = spots(staged_back, False)
         raw, *sent = pl.pallas_call(
-            functools.partial(pack_kernel, blocks, sent_spots),
+            functools.partial(pack_kernel, blocks, spots(staged, True)),
             out_shape=[jax.ShapeDtypeStruct((parts * pairs, len(blocks), momenta, half, half), BF16)]
             + sheets(staged),
             in_specs=[SMEM, HBM],
-            out_specs=[HBM] + [VMEM] * len(sheets(staged)),
-            scratch_shapes=[
-                pltpu.VMEM((count,) + block, BF16),
-                pltpu.VMEM((parts * pairs, len(blocks), momenta, half, half), BF16),
-                pltpu.SemaphoreType.DMA((2, parts * pairs, len(blocks))),
-            ],
+            out_specs=[VMEM] * (1 + len(sheets(staged))),
+            scratch_shapes=[pltpu.VMEM((count,) + block, BF16), pltpu.SemaphoreType.DMA((parts * pairs, len(blocks)))],
             compiler_params=limit(8),
         )(device, green)
         greens[tag] = gather(orbs, raw)
         arrived = deliver(staged, sent)
         sent = pl.pallas_call(
-            functools.partial(middle_kernel, start, came_spots[tag], sent_spots),
-            out_shape=sheets(staged),
+            functools.partial(middle_kernel, start, spots(staged, False), spots(staged_back, True)),
+            out_shape=sheets(staged_back),
             in_specs=[SMEM] + [VMEM] * (1 + len(arrived)),
-            out_specs=[VMEM] * len(sheets(staged)),
+            out_specs=[VMEM] * len(sheets(staged_back)),
             scratch_shapes=[pltpu.VMEM((all_pairs, rows2, width), F32)] * 2 + [pltpu.VMEM((count,) + block, BF16)],
             compiler_params=limit(16),
         )(device, spread, *arrived)
-        returned[tag] = deliver(staged, sent)
-
-    tags = sorted(returned, reverse=True)
-    came_spots = [came_spots[tag] for tag in tags]
-    returned = sum((returned[tag] for tag in tags), [])
-    raws = sum((greens[tag] for tag in tags), [])
-    return pl.pallas_call(
-        functools.partial(langreth_kernel, came_spots),
-        out_shape=jax.ShapeDtypeStruct(green.shape, BF16),
-        in_specs=[SMEM] + [VMEM] * len(returned) + [HBM] * len(raws),
-        out_specs=VMEM,
-        scratch_shapes=[
-            pltpu.VMEM((12 * half, orbs * half), BF16),
-            pltpu.VMEM((chunks, count) + block, BF16),
-            pltpu.VMEM((chunks, orbs) + raws[0].shape, BF16),
-            pltpu.SemaphoreType.DMA((len(raws),)),
-        ],
-        compiler_params=limit(60),
-        name="langreth",
-    )(device, *returned, *raws)
+        returned[tag] = deliver(staged_back, sent)
+
+    raws = sum((greens[tag] for tag in sorted(greens, reverse=True)), [])
+    sums_shape = jax.ShapeDtypeStruct((len(SUMS), parts, momenta, pairs, half, half), F32)
+    final = jax.ShapeDtypeStruct(green.shape, BF16)
+
+    held = jax.ShapeDtypeStruct((chunks, orbs) + raws[0].shape, BF16)
+
+    def left(kinds, tag):
+        slots = sum(len(SLOTS[kind]) for kind in kinds)
+        return pl.pallas_call(
+            functools.partial(left_kernel, kinds, came_spots[tag]),
+            out_shape=jax.ShapeDtypeStruct((momenta, 2 * slots * half, orbs * half), BF16),
+            in_specs=[SMEM] + [VMEM] * len(returned[tag]),
+            out_specs=VMEM,
+            scratch_shapes=[pltpu.VMEM((count,) + block, BF16)],
+            compiler_params=limit(16),
+        )(device, *returned[tag])
+
+    def langreth(kinds, tag, sums, out_shape):
+        return pl.pallas_call(
+            functools.partial(langreth_kernel, kinds, len(sums) > 0, out_shape is sums_shape),
+            out_shape=out_shape if sums else [out_shape, held],
+            in_specs=[SMEM] + [VMEM] * (1 + len(sums)) + [HBM] * (0 if sums else len(raws)),
+            out_specs=VMEM if sums else [VMEM, VMEM],
+            scratch_shapes=[] if sums else [pltpu.SemaphoreType.DMA((len(raws),))],
+            compiler_params=limit(20),
+            name="langreth",
+        )(device, left(kinds, tag), *sums, *([] if sums else raws))
+
+    if chunks == 1:
+        return langreth(("o", "d"), "o", [], final)[0]
+    sums = langreth(("d",), "d", [], sums_shape)
+    return langreth(("o",), "o", sums, final)
 
 
 def solution(mesh):

time: 95 us -> 122 us (1.28)
  waiting for transfers between devices: 43.1 us -> 70.1 us
  Pallas kernels: 15.6 us -> 14.3 us
    ppermute x14, waiting for transfers between devices: 43.1 us -> 70.1 us  [shift(): return lax.ppermute(x, axes, [(i, i ^ mask) for i in range(count)])]
    pallas_call x5 -> x8, Pallas kernels: 15.4 us -> 13.6 us  [the longest x2 6.32 us: langreth(): pl.pallas_call(functools.partial(langreth_kernel, kinds, len(sums) > 0, o...]
    unnamed x26 -> x6, local copies, waits for them, and re-layouts: 3.4 us -> 2.46 us
  transfers between devices with their start and end apart: 22 -> 22, of which waited for: 10 -> 10; matrix products, arithmetic and copies ran while one was open for 1% -> 2% of each run, Pallas kernels for 5% -> 5%
where the time goes in v2:
time: 122 us
  waiting for transfers between devices  70.1 us (57%)
  starting transfers between devices  32.5 us (27%)
  Pallas kernels  14.3 us (12%)
  local copies, waits for them, and re-layouts  3.96 us (3%)
    ppermute x14, waiting for transfers between devices, shift(): return lax.ppermute(x, axes, [(i, i ^ mask) for i in range(count)])  70.1 us
    ppermute x14, starting transfers between devices, shift(): return lax.ppermute(x, axes, [(i, i ^ mask) for i in range(count)])  17.9 us
    all_to_all x2, starting transfers between devices, deliver(): return [lax.all_to_all(sent[0], axes, 0, 0, tiled=True)]  11.4 us
    pallas_call x2, Pallas kernels, langreth(): pl.pallas_call(functools.partial(langreth_kernel, kinds, len(sums) > 0, o...  6.32 us
    pallas_call x2, Pallas kernels, local(): pl.pallas_call(functools.partial(middle_kernel, start, spots(staged, Fals...  3.38 us
    pallas_call x2, Pallas kernels, local(): pl.pallas_call(functools.partial(pack_kernel, blocks, spots(staged, True)...  3.31 us
    ppermute x6, starting transfers between devices, gather(): held[turn ^ bit] = lax.ppermute(piece, 'orb', swap)  3.18 us
    unnamed x6, local copies, waits for them, and re-layouts  2.46 us
  transfers between devices with their start and end apart: 22, of which 10 were waited for; matrix products, arithmetic and copies ran while one was open for 2% of the time, Pallas kernels for 5%

profile of v2, /device:TPU:0, one launch (start us, length us, event | category | flops | bytes accessed | tf_op | source)
XLA Modules:
  0.0 122.0 jit_solution(6155567760715223274)
XLA Ops:
  1.2 2.1 %shard_map.28 = (bf16[8,2,1,128,128]{4,3,2,1,0:T(8,128)(2,1)S(1)}, bf16[32,1,2,4,8,128]{5,4,3,2,1,0:T(8,128)(2,1)}) custom-call(s32[1]{0:T(128)} %bitcast.device_ref, bf16[2,1,4,256,256]{4,3,2,1,0:T(8,128)(2,1)S(1)} %copy-done), custom_call_target="tpu_custom_call" | custom-call | tf_op jit(solution)/shard_map/pallas_call | solution.py:432
  3.3 7.3 %all-to-all-start = ((bf16[32,1,2,4,8,128]{5,4,3,2,1,0:T(8,128)(2,1)}), bf16[32,1,2,4,8,128]{5,4,3,2,1,0:T(8,128)(2,1)S(1)}, u32[]{:S(2)}, u32[]{:S(2)}) async-start(bf16[32,1,2,4,8,128]{5,4,3,2,1,0:T(8,128)(2,1)} %get-tuple-element.26), calls=%async_computation | async-start | bytes 1048576 | tf_op jit(solution)/shard_map/all_to_all | solution.py:425
  13.1 1.8 %collective-permute-start.7 = (bf16[2,4,1,2,4,8,128]{6,5,4,3,2,1,0:T(8,128)(2,1)S(1)}, bf16[2,4,1,2,4,8,128]{6,5,4,3,2,1,0:T(8,128)(2,1)S(1)}, u32[]{:S(2)}, u32[]{:S(2)}) collective-permute-start(bf16[2,4,1,2,4,8,128]{6,5,4,3,2,1,0:T(8,128)(2,1)S(1)} %get-tuple-element.36), channel_id=1, source_target_pairs={{0,8},{1,9},{2,10},{3,11},{4,12},{5,13},{6,14},{7,15},{8,0},{9,1},... | collective-permute-start | bytes 393224 | tf_op jit(solution)/shard_map/ppermute | solution.py:360
  15.0 2.4 %collective-permute-start.8 = (bf16[2,4,1,2,4,8,128]{6,5,4,3,2,1,0:T(8,128)(2,1)S(1)}, bf16[2,4,1,2,4,8,128]{6,5,4,3,2,1,0:T(8,128)(2,1)S(1)}, u32[]{:S(2)}, u32[]{:S(2)}) collective-permute-start(bf16[2,4,1,2,4,8,128]{6,5,4,3,2,1,0:T(8,128)(2,1)S(1)} %get-tuple-element.37), channel_id=1, source_target_pairs={{0,16},{1,17},{2,18},{3,19},{4,20},{5,21},{6,22},{7,23},{8,24},{9,... | collective-permute-start | bytes 393224 | tf_op jit(solution)/shard_map/ppermute | solution.py:360
  17.6 6.1 %collective-permute-done.7.refs_1_ = bf16[2,4,1,2,4,8,128]{6,5,4,3,2,1,0:T(8,128)(2,1)S(1)} collective-permute-done((bf16[2,4,1,2,4,8,128]{6,5,4,3,2,1,0:T(8,128)(2,1)S(1)}, bf16[2,4,1,2,4,8,128]{6,5,4,3,2,1,0:T(8,128)(2,1)S(1)}, u32[]{:S(2)}, u32[]{:S(2)}) %collective-permute-start.7) | collective-permute-done | bytes 131104 | tf_op jit(solution)/shard_map/ppermute | solution.py:360
  23.7 11.0 %collective-permute-done.8.refs_2_ = bf16[2,4,1,2,4,8,128]{6,5,4,3,2,1,0:T(8,128)(2,1)S(1)} collective-permute-done((bf16[2,4,1,2,4,8,128]{6,5,4,3,2,1,0:T(8,128)(2,1)S(1)}, bf16[2,4,1,2,4,8,128]{6,5,4,3,2,1,0:T(8,128)(2,1)S(1)}, u32[]{:S(2)}, u32[]{:S(2)}) %collective-permute-start.8) | collective-permute-done | bytes 131104 | tf_op jit(solution)/shard_map/ppermute | solution.py:360
  34.7 1.5 %collective-permute-start.18 = (bf16[8,2,1,128,128]{4,3,2,1,0:T(8,128)(2,1)S(1)}, bf16[8,2,1,128,128]{4,3,2,1,0:T(8,128)(2,1)S(1)}, u32[]{:S(2)}, u32[]{:S(2)}) collective-permute-start(bf16[8,2,1,128,128]{4,3,2,1,0:T(8,128)(2,1)S(1)} %get-tuple-element.44.refs_4_), channel_id=1, source_target_pairs={{0,2},{1,3},{2,0},{3,1},{4,6},{5,7},{6,4},{7,5},{8,10},{9,11},{10,... | collective-permute-start | bytes 1572872 | tf_op jit(solution)/shard_map/ppermute | solution.py:390
  39.0 1.5 %collective-permute-start.12 = (bf16[2,4,1,2,4,8,128]{6,5,4,3,2,1,0:T(8,128)(2,1)S(1)}, bf16[2,4,1,2,4,8,128]{6,5,4,3,2,1,0:T(8,128)(2,1)S(1)}, u32[]{:S(2)}, u32[]{:S(2)}) collective-permute-start(bf16[2,4,1,2,4,8,128]{6,5,4,3,2,1,0:T(8,128)(2,1)S(1)} %get-tuple-element.41), channel_id=1, source_target_pairs={{0,4},{1,5},{2,6},{3,7},{4,0},{5,1},{6,2},{7,3},{8,12},{9,13},{10,... | collective-permute-start | bytes 393224 | tf_op jit(solution)/shard_map/ppermute | solution.py:360
  41.9 1.5 %convert_element_type.14.weight_ref = bf16[128,128]{1,0:T(8,128)(2,1)S(1)} reshape(bf16[16,8,16,8]{3,2,1,0:T(8,128)(2,1)} %multiply_convert_fusion) | data formatting | bytes 65536 | tf_op jit(solution)/shard_map/convert_element_type | solution.py:407
  43.4 20.2 %collective-permute-done.11.refs_1_ = bf16[2,4,1,2,4,8,128]{6,5,4,3,2,1,0:T(8,128)(2,1)S(1)} collective-permute-done((bf16[2,4,1,2,4,8,128]{6,5,4,3,2,1,0:T(8,128)(2,1)}, bf16[2,4,1,2,4,8,128]{6,5,4,3,2,1,0:T(8,128)(2,1)S(1)}, u32[]{:S(2)}, u32[]{:S(2)}) %collective-permute-start.11) | collective-permute-done | bytes 131104 | tf_op jit(solution)/shard_map/ppermute | solution.py:360
  63.6 3.2 %collective-permute-done.13.refs_3_ = bf16[2,4,1,2,4,8,128]{6,5,4,3,2,1,0:T(8,128)(2,1)S(1)} collective-permute-done((bf16[2,4,1,2,4,8,128]{6,5,4,3,2,1,0:T(8,128)(2,1)S(1)}, bf16[2,4,1,2,4,8,128]{6,5,4,3,2,1,0:T(8,128)(2,1)S(1)}, u32[]{:S(2)}, u32[]{:S(2)}) %collective-permute-start.13) | collective-permute-done | bytes 131104 | tf_op jit(solution)/shard_map/ppermute | solution.py:360
  66.8 2.1 %shard_map.32 = bf16[32,1,2,4,8,128]{5,4,3,2,1,0:T(8,128)(2,1)} custom-call(s32[1]{0:T(128)} %bitcast.device_ref, bf16[128,128]{1,0:T(8,128)(2,1)S(1)} %convert_element_type.14.weight_ref, bf16[2,4,1,2,4,8,128]{6,5,4,3,2,1,0:T(8,128)(2,1)S(1)} %get-tuple-element.39.refs_0_, bf16[2,4,1,2,4,8,128]{6,5,4,3,2,1,0:T(8,128)(2,1)S(1)} %collective-permute-done.11.refs_1_, ...), custom_call_target="tpu_custom_call" | custom-call | tf_op jit(solution)/shard_map/pallas_call | solution.py:443
  68.9 4.1 %all-to-all-start.1 = ((bf16[32,1,2,4,8,128]{5,4,3,2,1,0:T(8,128)(2,1)}), bf16[32,1,2,4,8,128]{5,4,3,2,1,0:T(8,128)(2,1)S(1)}, u32[]{:S(2)}, u32[]{:S(2)}) async-start(bf16[32,1,2,4,8,128]{5,4,3,2,1,0:T(8,128)(2,1)} %shard_map.32), calls=%async_computation.1 | async-start | bytes 1048576 | tf_op jit(solution)/shard_map/all_to_all | solution.py:425
  74.3 1.8 %collective-permute-start = (bf16[2,4,1,2,4,8,128]{6,5,4,3,2,1,0:T(8,128)(2,1)S(1)}, bf16[2,4,1,2,4,8,128]{6,5,4,3,2,1,0:T(8,128)(2,1)S(1)}, u32[]{:S(2)}, u32[]{:S(2)}) collective-permute-start(bf16[2,4,1,2,4,8,128]{6,5,4,3,2,1,0:T(8,128)(2,1)S(1)} %get-tuple-element.28), channel_id=1, source_target_pairs={{0,8},{1,9},{2,10},{3,11},{4,12},{5,13},{6,14},{7,15},{8,0},{9,1},... | collective-permute-start | bytes 393224 | tf_op jit(solution)/shard_map/ppermute | solution.py:360
  76.1 2.4 %collective-permute-start.1 = (bf16[2,4,1,2,4,8,128]{6,5,4,3,2,1,0:T(8,128)(2,1)S(1)}, bf16[2,4,1,2,4,8,128]{6,5,4,3,2,1,0:T(8,128)(2,1)S(1)}, u32[]{:S(2)}, u32[]{:S(2)}) collective-permute-start(bf16[2,4,1,2,4,8,128]{6,5,4,3,2,1,0:T(8,128)(2,1)S(1)} %get-tuple-element.29), channel_id=1, source_target_pairs={{0,16},{1,17},{2,18},{3,19},{4,20},{5,21},{6,22},{7,23},{8,24},{9,... | collective-permute-start | bytes 393224 | tf_op jit(solution)/shard_map/ppermute | solution.py:360
  78.7 7.3 %collective-permute-done.refs_1_ = bf16[2,4,1,2,4,8,128]{6,5,4,3,2,1,0:T(8,128)(2,1)S(1)} collective-permute-done((bf16[2,4,1,2,4,8,128]{6,5,4,3,2,1,0:T(8,128)(2,1)S(1)}, bf16[2,4,1,2,4,8,128]{6,5,4,3,2,1,0:T(8,128)(2,1)S(1)}, u32[]{:S(2)}, u32[]{:S(2)}) %collective-permute-start) | collective-permute-done | bytes 131104 | tf_op jit(solution)/shard_map/ppermute | solution.py:360
  86.0 11.0 %collective-permute-done.1.refs_2_ = bf16[2,4,1,2,4,8,128]{6,5,4,3,2,1,0:T(8,128)(2,1)S(1)} collective-permute-done((bf16[2,4,1,2,4,8,128]{6,5,4,3,2,1,0:T(8,128)(2,1)S(1)}, bf16[2,4,1,2,4,8,128]{6,5,4,3,2,1,0:T(8,128)(2,1)S(1)}, u32[]{:S(2)}, u32[]{:S(2)}) %collective-permute-start.1) | collective-permute-done | bytes 131104 | tf_op jit(solution)/shard_map/ppermute | solution.py:360
  98.6 1.5 %collective-permute-start.4 = (bf16[2,4,1,2,4,8,128]{6,5,4,3,2,1,0:T(8,128)(2,1)S(1)}, bf16[2,4,1,2,4,8,128]{6,5,4,3,2,1,0:T(8,128)(2,1)S(1)}, u32[]{:S(2)}, u32[]{:S(2)}) collective-permute-start(bf16[2,4,1,2,4,8,128]{6,5,4,3,2,1,0:T(8,128)(2,1)S(1)} %get-tuple-element.32), channel_id=1, source_target_pairs={{0,2},{1,3},{2,0},{3,1},{4,6},{5,7},{6,4},{7,5},{8,10},{9,11},{10,... | collective-permute-start | bytes 393224 | tf_op jit(solution)/shard_map/ppermute | solution.py:360
  100.2 4.1 %collective-permute-done.4.refs_1_ = bf16[2,4,1,2,4,8,128]{6,5,4,3,2,1,0:T(8,128)(2,1)S(1)} collective-permute-done((bf16[2,4,1,2,4,8,128]{6,5,4,3,2,1,0:T(8,128)(2,1)S(1)}, bf16[2,4,1,2,4,8,128]{6,5,4,3,2,1,0:T(8,128)(2,1)S(1)}, u32[]{:S(2)}, u32[]{:S(2)}) %collective-permute-start.4) | collective-permute-done | bytes 131104 | tf_op jit(solution)/shard_map/ppermute | solution.py:360
  105.7 3.5 %collective-permute-done.5.refs_2_ = bf16[2,4,1,2,4,8,128]{6,5,4,3,2,1,0:T(8,128)(2,1)S(1)} collective-permute-done((bf16[2,4,1,2,4,8,128]{6,5,4,3,2,1,0:T(8,128)(2,1)S(1)}, bf16[2,4,1,2,4,8,128]{6,5,4,3,2,1,0:T(8,128)(2,1)S(1)}, u32[]{:S(2)}, u32[]{:S(2)}) %collective-permute-start.5) | collective-permute-done | bytes 131104 | tf_op jit(solution)/shard_map/ppermute | solution.py:360
  109.2 2.4 %collective-permute-start.6 = (bf16[2,4,1,2,4,8,128]{6,5,4,3,2,1,0:T(8,128)(2,1)S(1)}, bf16[2,4,1,2,4,8,128]{6,5,4,3,2,1,0:T(8,128)(2,1)S(1)}, u32[]{:S(2)}, u32[]{:S(2)}) collective-permute-start(bf16[2,4,1,2,4,8,128]{6,5,4,3,2,1,0:T(8,128)(2,1)S(1)} %get-tuple-element.34), channel_id=1, source_target_pairs={{0,6},{1,7},{2,4},{3,5},{4,2},{5,3},{6,0},{7,1},{8,14},{9,15},{10,... | collective-permute-start | bytes 393224 | tf_op jit(solution)/shard_map/ppermute | solution.py:360
  111.6 3.5 %collective-permute-done.6.refs_3_ = bf16[2,4,1,2,4,8,128]{6,5,4,3,2,1,0:T(8,128)(2,1)S(1)} collective-permute-done((bf16[2,4,1,2,4,8,128]{6,5,4,3,2,1,0:T(8,128)(2,1)S(1)}, bf16[2,4,1,2,4,8,128]{6,5,4,3,2,1,0:T(8,128)(2,1)S(1)}, u32[]{:S(2)}, u32[]{:S(2)}) %collective-permute-start.6) | collective-permute-done | bytes 131104 | tf_op jit(solution)/shard_map/ppermute | solution.py:360
  115.7 4.3 %langreth.2 = (f32[5,2,1,4,128,128]{5,4,3,2,1,0:T(8,128)S(1)}, bf16[2,4,8,2,1,128,128]{6,5,4,3,2,1,0:T(8,128)(2,1)S(1)}) custom-call(s32[1]{0:T(128)} %bitcast.device_ref, bf16[1,1024,512]{2,1,0:T(8,128)(2,1)S(1)} %shard_map.33.left_ref, bf16[8,2,1,128,128]{4,3,2,1,0:T(8,128)(2,1)S(1)} %get-tuple-element.43.refs_0_, ...), custom_call_target="tpu_custom_call" | custom-call | tf_op jit(solution)/shard_map/langreth/pallas_call | solution.py:471
  120.0 2.0 %langreth.3 = bf16[2,1,4,256,256]{4,3,2,1,0:T(8,128)(2,1)} custom-call(s32[1]{0:T(128)} %bitcast.device_ref, bf16[1,512,512]{2,1,0:T(8,128)(2,1)S(1)} %shard_map.30.left_ref, f32[5,2,1,4,128,128]{5,4,3,2,1,0:T(8,128)S(1)} %get-tuple-element.45.refs_0_, bf16[2,4,8,2,1,128,128]{6,5,4,3,2,1,0:T(8,128)(2,1)S(1)} %get-tuple-element.46.refs_1_), custom_call_target="tpu_custom_call" | custom-call | tf_op jit(solution)/shard_map/langreth/pallas_call | solution.py:471
  (41 shorter events, 13.4 us)
Async XLA Ops:
  0.0 41.0 %copy-start.2 = (f32[16,16]{1,0:T(8,128)S(1)}, f32[16,16]{1,0:T(8,128)}, u32[]{:S(2)}) copy-start(f32[16,16]{1,0:T(8,128)} %param.5) | copy-start | bytes 3076
  0.0 1.2 %copy-start = (bf16[2,1,4,256,256]{4,3,2,1,0:T(8,128)(2,1)S(1)}, bf16[2,1,4,256,256]{4,3,2,1,0:T(8,128)(2,1)}, u32[]{:S(2)}) copy-start(bf16[2,1,4,256,256]{4,3,2,1,0:T(8,128)(2,1)} %green_ref.3) | copy-start | bytes 3145732
  3.3 65.6 %all-to-all-start = ((bf16[32,1,2,4,8,128]{5,4,3,2,1,0:T(8,128)(2,1)}), bf16[32,1,2,4,8,128]{5,4,3,2,1,0:T(8,128)(2,1)S(1)}, u32[]{:S(2)}, u32[]{:S(2)}) async-start(bf16[32,1,2,4,8,128]{5,4,3,2,1,0:T(8,128)(2,1)} %get-tuple-element.26), calls=%async_computation | async-start | bytes 1048576 | tf_op jit(solution)/shard_map/all_to_all | solution.py:425
  13.1 10.5 %collective-permute-start.7 = (bf16[2,4,1,2,4,8,128]{6,5,4,3,2,1,0:T(8,128)(2,1)S(1)}, bf16[2,4,1,2,4,8,128]{6,5,4,3,2,1,0:T(8,128)(2,1)S(1)}, u32[]{:S(2)}, u32[]{:S(2)}) collective-permute-start(bf16[2,4,1,2,4,8,128]{6,5,4,3,2,1,0:T(8,128)(2,1)S(1)} %get-tuple-element.36), channel_id=1, source_target_pairs={{0,8},{1,9},{2,10},{3,11},{4,12},{5,13},{6,14},{7,15},{8,0},{9,1},... | collective-permute-start | bytes 393224 | tf_op jit(solution)/shard_map/ppermute | solution.py:360
  15.0 19.6 %collective-permute-start.8 = (bf16[2,4,1,2,4,8,128]{6,5,4,3,2,1,0:T(8,128)(2,1)S(1)}, bf16[2,4,1,2,4,8,128]{6,5,4,3,2,1,0:T(8,128)(2,1)S(1)}, u32[]{:S(2)}, u32[]{:S(2)}) collective-permute-start(bf16[2,4,1,2,4,8,128]{6,5,4,3,2,1,0:T(8,128)(2,1)S(1)} %get-tuple-element.37), channel_id=1, source_target_pairs={{0,16},{1,17},{2,18},{3,19},{4,20},{5,21},{6,22},{7,23},{8,24},{9,... | collective-permute-start | bytes 393224 | tf_op jit(solution)/shard_map/ppermute | solution.py:360
  17.4 17.2 %collective-permute-start.9 = (bf16[2,4,1,2,4,8,128]{6,5,4,3,2,1,0:T(8,128)(2,1)S(1)}, bf16[2,4,1,2,4,8,128]{6,5,4,3,2,1,0:T(8,128)(2,1)S(1)}, u32[]{:S(2)}, u32[]{:S(2)}) collective-permute-start(bf16[2,4,1,2,4,8,128]{6,5,4,3,2,1,0:T(8,128)(2,1)S(1)} %get-tuple-element.38), channel_id=1, source_target_pairs={{0,24},{1,25},{2,26},{3,27},{4,28},{5,29},{6,30},{7,31},{8,16},{9,... | collective-permute-start | bytes 393224 | tf_op jit(solution)/shard_map/ppermute | solution.py:360
  34.6 2.2 %collective-permute-start.10 = (bf16[4,4,1,2,4,8,128]{6,5,4,3,2,1,0:T(8,128)(2,1)S(1)}, bf16[4,4,1,2,4,8,128]{6,5,4,3,2,1,0:T(8,128)(2,1)S(1)}, u32[]{:S(2)}, u32[]{:S(2)}) collective-permute-start(bf16[4,4,1,2,4,8,128]{6,5,4,3,2,1,0:T(8,128)(2,1)S(1)} %near.3), channel_id=1, source_target_pairs={{0,1},{1,0},{2,3},{3,2},{4,5},{5,4},{6,7},{7,6},{8,9},{9,8},{10,11... | collective-permute-start | bytes 786440 | tf_op jit(solution)/shard_map/ppermute | solution.py:360
  34.7 62.9 %collective-permute-start.18 = (bf16[8,2,1,128,128]{4,3,2,1,0:T(8,128)(2,1)S(1)}, bf16[8,2,1,128,128]{4,3,2,1,0:T(8,128)(2,1)S(1)}, u32[]{:S(2)}, u32[]{:S(2)}) collective-permute-start(bf16[8,2,1,128,128]{4,3,2,1,0:T(8,128)(2,1)S(1)} %get-tuple-element.44.refs_4_), channel_id=1, source_target_pairs={{0,2},{1,3},{2,0},{3,1},{4,6},{5,7},{6,4},{7,5},{8,10},{9,11},{10,... | collective-permute-start | bytes 1572872 | tf_op jit(solution)/shard_map/ppermute | solution.py:390
  36.2 61.9 %collective-permute-start.15 = (bf16[8,2,1,128,128]{4,3,2,1,0:T(8,128)(2,1)S(1)}, bf16[8,2,1,128,128]{4,3,2,1,0:T(8,128)(2,1)S(1)}, u32[]{:S(2)}, u32[]{:S(2)}) collective-permute-start(bf16[8,2,1,128,128]{4,3,2,1,0:T(8,128)(2,1)S(1)} %get-tuple-element.43.refs_0_), channel_id=1, source_target_pairs={{0,2},{1,3},{2,0},{3,1},{4,6},{5,7},{6,4},{7,5},{8,10},{9,11},{10,... | collective-permute-start | bytes 1572872 | tf_op jit(solution)/shard_map/ppermute | solution.py:390
  37.5 26.1 %collective-permute-start.11 = (bf16[2,4,1,2,4,8,128]{6,5,4,3,2,1,0:T(8,128)(2,1)}, bf16[2,4,1,2,4,8,128]{6,5,4,3,2,1,0:T(8,128)(2,1)S(1)}, u32[]{:S(2)}, u32[]{:S(2)}) collective-permute-start(bf16[2,4,1,2,4,8,128]{6,5,4,3,2,1,0:T(8,128)(2,1)} %get-tuple-element.40), channel_id=1, source_target_pairs={{0,2},{1,3},{2,0},{3,1},{4,6},{5,7},{6,4},{7,5},{8,10},{9,11},{10,... | collective-permute-start | bytes 393224 | tf_op jit(solution)/shard_map/ppermute | solution.py:360
  39.0 24.7 %collective-permute-start.12 = (bf16[2,4,1,2,4,8,128]{6,5,4,3,2,1,0:T(8,128)(2,1)S(1)}, bf16[2,4,1,2,4,8,128]{6,5,4,3,2,1,0:T(8,128)(2,1)S(1)}, u32[]{:S(2)}, u32[]{:S(2)}) collective-permute-start(bf16[2,4,1,2,4,8,128]{6,5,4,3,2,1,0:T(8,128)(2,1)S(1)} %get-tuple-element.41), channel_id=1, source_target_pairs={{0,4},{1,5},{2,6},{3,7},{4,0},{5,1},{6,2},{7,3},{8,12},{9,13},{10,... | collective-permute-start | bytes 393224 | tf_op jit(solution)/shard_map/ppermute | solution.py:360
  40.5 26.3 %collective-permute-start.13 = (bf16[2,4,1,2,4,8,128]{6,5,4,3,2,1,0:T(8,128)(2,1)S(1)}, bf16[2,4,1,2,4,8,128]{6,5,4,3,2,1,0:T(8,128)(2,1)S(1)}, u32[]{:S(2)}, u32[]{:S(2)}) collective-permute-start(bf16[2,4,1,2,4,8,128]{6,5,4,3,2,1,0:T(8,128)(2,1)S(1)} %get-tuple-element.42), channel_id=1, source_target_pairs={{0,6},{1,7},{2,4},{3,5},{4,2},{5,3},{6,0},{7,1},{8,14},{9,15},{10,... | collective-permute-start | bytes 393224 | tf_op jit(solution)/shard_map/ppermute | solution.py:360
  68.9 46.4 %all-to-all-start.1 = ((bf16[32,1,2,4,8,128]{5,4,3,2,1,0:T(8,128)(2,1)}), bf16[32,1,2,4,8,128]{5,4,3,2,1,0:T(8,128)(2,1)S(1)}, u32[]{:S(2)}, u32[]{:S(2)}) async-start(bf16[32,1,2,4,8,128]{5,4,3,2,1,0:T(8,128)(2,1)} %shard_map.32), calls=%async_computation.1 | async-start | bytes 1048576 | tf_op jit(solution)/shard_map/all_to_all | solution.py:425
  74.3 11.7 %collective-permute-start = (bf16[2,4,1,2,4,8,128]{6,5,4,3,2,1,0:T(8,128)(2,1)S(1)}, bf16[2,4,1,2,4,8,128]{6,5,4,3,2,1,0:T(8,128)(2,1)S(1)}, u32[]{:S(2)}, u32[]{:S(2)}) collective-permute-start(bf16[2,4,1,2,4,8,128]{6,5,4,3,2,1,0:T(8,128)(2,1)S(1)} %get-tuple-element.28), channel_id=1, source_target_pairs={{0,8},{1,9},{2,10},{3,11},{4,12},{5,13},{6,14},{7,15},{8,0},{9,1},... | collective-permute-start | bytes 393224 | tf_op jit(solution)/shard_map/ppermute | solution.py:360
  76.1 20.8 %collective-permute-start.1 = (bf16[2,4,1,2,4,8,128]{6,5,4,3,2,1,0:T(8,128)(2,1)S(1)}, bf16[2,4,1,2,4,8,128]{6,5,4,3,2,1,0:T(8,128)(2,1)S(1)}, u32[]{:S(2)}, u32[]{:S(2)}) collective-permute-start(bf16[2,4,1,2,4,8,128]{6,5,4,3,2,1,0:T(8,128)(2,1)S(1)} %get-tuple-element.29), channel_id=1, source_target_pairs={{0,16},{1,17},{2,18},{3,19},{4,20},{5,21},{6,22},{7,23},{8,24},{9,... | collective-permute-start | bytes 393224 | tf_op jit(solution)/shard_map/ppermute | solution.py:360
  78.5 18.4 %collective-permute-start.2 = (bf16[2,4,1,2,4,8,128]{6,5,4,3,2,1,0:T(8,128)(2,1)S(1)}, bf16[2,4,1,2,4,8,128]{6,5,4,3,2,1,0:T(8,128)(2,1)S(1)}, u32[]{:S(2)}, u32[]{:S(2)}) collective-permute-start(bf16[2,4,1,2,4,8,128]{6,5,4,3,2,1,0:T(8,128)(2,1)S(1)} %get-tuple-element.30), channel_id=1, source_target_pairs={{0,24},{1,25},{2,26},{3,27},{4,28},{5,29},{6,30},{7,31},{8,16},{9,... | collective-permute-start | bytes 393224 | tf_op jit(solution)/shard_map/ppermute | solution.py:360
  97.0 1.6 %collective-permute-start.3 = (bf16[4,4,1,2,4,8,128]{6,5,4,3,2,1,0:T(8,128)(2,1)S(1)}, bf16[4,4,1,2,4,8,128]{6,5,4,3,2,1,0:T(8,128)(2,1)S(1)}, u32[]{:S(2)}, u32[]{:S(2)}) collective-permute-start(bf16[4,4,1,2,4,8,128]{6,5,4,3,2,1,0:T(8,128)(2,1)S(1)} %near.2), channel_id=1, source_target_pairs={{0,1},{1,0},{2,3},{3,2},{4,5},{5,4},{6,7},{7,6},{8,9},{9,8},{10,11... | collective-permute-start | bytes 786440 | tf_op jit(solution)/shard_map/ppermute | solution.py:360
  97.1 18.6 %collective-permute-start.17 = (bf16[8,2,1,128,128]{4,3,2,1,0:T(8,128)(2,1)S(1)}, bf16[8,2,1,128,128]{4,3,2,1,0:T(8,128)(2,1)}, u32[]{:S(2)}, u32[]{:S(2)}) collective-permute-start(bf16[8,2,1,128,128]{4,3,2,1,0:T(8,128)(2,1)S(1)} %get-tuple-element.44.refs_4_), channel_id=1, source_target_pairs={{0,1},{1,0},{2,3},{3,2},{4,5},{5,4},{6,7},{7,6},{8,9},{9,8},{10,11... | collective-permute-start | bytes 1572872 | tf_op jit(solution)/shard_map/ppermute | solution.py:390
  97.6 18.1 %collective-permute-start.14 = (bf16[8,2,1,128,128]{4,3,2,1,0:T(8,128)(2,1)S(1)}, bf16[8,2,1,128,128]{4,3,2,1,0:T(8,128)(2,1)}, u32[]{:S(2)}, u32[]{:S(2)}) collective-permute-start(bf16[8,2,1,128,128]{4,3,2,1,0:T(8,128)(2,1)S(1)} %get-tuple-element.43.refs_0_), channel_id=1, source_target_pairs={{0,1},{1,0},{2,3},{3,2},{4,5},{5,4},{6,7},{7,6},{8,9},{9,8},{10,11... | collective-permute-start | bytes 1572872 | tf_op jit(solution)/shard_map/ppermute | solution.py:390
  97.7 18.0 %collective-permute-start.19 = (bf16[8,2,1,128,128]{4,3,2,1,0:T(8,128)(2,1)S(1)}, bf16[8,2,1,128,128]{4,3,2,1,0:T(8,128)(2,1)}, u32[]{:S(2)}, u32[]{:S(2)}) collective-permute-start(bf16[8,2,1,128,128]{4,3,2,1,0:T(8,128)(2,1)S(1)} %collective-permute-done.18.refs_6_), channel_id=1, source_target_pairs={{0,1},{1,0},{2,3},{3,2},{4,5},{5,4},{6,7},{7,6},{8,9},{9,8},{10,11... | collective-permute-start | bytes 1572872 | tf_op jit(solution)/shard_map/ppermute | solution.py:390
  98.1 17.6 %collective-permute-start.16 = (bf16[8,2,1,128,128]{4,3,2,1,0:T(8,128)(2,1)S(1)}, bf16[8,2,1,128,128]{4,3,2,1,0:T(8,128)(2,1)}, u32[]{:S(2)}, u32[]{:S(2)}) collective-permute-start(bf16[8,2,1,128,128]{4,3,2,1,0:T(8,128)(2,1)S(1)} %collective-permute-done.15.refs_2_), channel_id=1, source_target_pairs={{0,1},{1,0},{2,3},{3,2},{4,5},{5,4},{6,7},{7,6},{8,9},{9,8},{10,11... | collective-permute-start | bytes 1572872 | tf_op jit(solution)/shard_map/ppermute | solution.py:390
  98.6 5.6 %collective-permute-start.4 = (bf16[2,4,1,2,4,8,128]{6,5,4,3,2,1,0:T(8,128)(2,1)S(1)}, bf16[2,4,1,2,4,8,128]{6,5,4,3,2,1,0:T(8,128)(2,1)S(1)}, u32[]{:S(2)}, u32[]{:S(2)}) collective-permute-start(bf16[2,4,1,2,4,8,128]{6,5,4,3,2,1,0:T(8,128)(2,1)S(1)} %get-tuple-element.32), channel_id=1, source_target_pairs={{0,2},{1,3},{2,0},{3,1},{4,6},{5,7},{6,4},{7,5},{8,10},{9,11},{10,... | collective-permute-start | bytes 393224 | tf_op jit(solution)/shard_map/ppermute | solution.py:360
  104.2 5.0 %collective-permute-start.5 = (bf16[2,4,1,2,4,8,128]{6,5,4,3,2,1,0:T(8,128)(2,1)S(1)}, bf16[2,4,1,2,4,8,128]{6,5,4,3,2,1,0:T(8,128)(2,1)S(1)}, u32[]{:S(2)}, u32[]{:S(2)}) collective-permute-start(bf16[2,4,1,2,4,8,128]{6,5,4,3,2,1,0:T(8,128)(2,1)S(1)} %get-tuple-element.33), channel_id=1, source_target_pairs={{0,4},{1,5},{2,6},{3,7},{4,0},{5,1},{6,2},{7,3},{8,12},{9,13},{10,... | collective-permute-start | bytes 393224 | tf_op jit(solution)/shard_map/ppermute | solution.py:360
  109.2 5.9 %collective-permute-start.6 = (bf16[2,4,1,2,4,8,128]{6,5,4,3,2,1,0:T(8,128)(2,1)S(1)}, bf16[2,4,1,2,4,8,128]{6,5,4,3,2,1,0:T(8,128)(2,1)S(1)}, u32[]{:S(2)}, u32[]{:S(2)}) collective-permute-start(bf16[2,4,1,2,4,8,128]{6,5,4,3,2,1,0:T(8,128)(2,1)S(1)} %get-tuple-element.34), channel_id=1, source_target_pairs={{0,6},{1,7},{2,4},{3,5},{4,2},{5,3},{6,0},{7,1},{8,14},{9,15},{10,... | collective-permute-start | bytes 393224 | tf_op jit(solution)/shard_map/ppermute | solution.py:360
  (1 other events, 1.2 us)

commit v3 on v2

--- a/solution.py
+++ b/solution.py
@@ -61,34 +61,18 @@
 
 
 def pack_kernel(blocks, spots, device_ref, green_ref, *refs):
-    raw_ref, out_refs, block_scr, sems = refs[0], refs[1:-2], refs[-2], refs[-1]
+    raw_ref, out_refs, block_scr = refs[0], refs[1:-1], refs[-1]
     count, momenta, parts, pairs, _, half = block_scr.shape
     row, col = grid_masks(half)
 
-    def fetch(step):
-        part, pair = step // pairs, step % pairs
-        return [
-            pltpu.make_async_copy(
-                green_ref.at[part, :, pair, pl.ds(i * half, half), pl.ds(j * half, half)],
-                raw_ref.at[step, n],
-                sems.at[step, n],
-            )
-            for n, (i, j) in enumerate(blocks)
-        ]
-
-    def begin(step, carry):
-        for copy in fetch(step):
-            copy.start()
-        return carry
-
-    lax.fori_loop(0, parts * pairs, begin, 0)
-
     def one(step, carry):
         part, pair = step // pairs, step % pairs
-        for copy in fetch(step):
-            copy.wait()
         for k in range(momenta):
-            got = {at: raw_ref[step, n, k].astype(F32) for n, at in enumerate(blocks)}
+            got = {}
+            for n, (i, j) in enumerate(blocks):
+                piece = green_ref[part, k, pair, i * half : (i + 1) * half, j * half : (j + 1) * half]
+                raw_ref[step, n, k] = piece
+                got[i, j] = piece.astype(F32)
             own, facing = [], []
             if (0, 1) in got:
                 own.append(got[0, 1])
@@ -433,9 +417,9 @@
             functools.partial(pack_kernel, blocks, spots(staged, True)),
             out_shape=[jax.ShapeDtypeStruct((parts * pairs, len(blocks), momenta, half, half), BF16)]
             + sheets(staged),
-            in_specs=[SMEM, HBM],
+            in_specs=[SMEM, VMEM],
             out_specs=[VMEM] * (1 + len(sheets(staged))),
-            scratch_shapes=[pltpu.VMEM((count,) + block, BF16), pltpu.SemaphoreType.DMA((parts * pairs, len(blocks)))],
+            scratch_shapes=[pltpu.VMEM((count,) + block, BF16)],
             compiler_params=limit(8),
         )(device, green)
         greens[tag] = gather(orbs, raw)

time: 122 us -> 122 us (level)
  no operation moved by 1% of the time
where the time goes in v3:
time: 122 us
  waiting for transfers between devices  70.5 us (58%)
  starting transfers between devices  32.5 us (27%)
  Pallas kernels  13.6 us (11%)
  local copies, waits for them, and re-layouts  3.96 us (3%)
    ppermute x14, waiting for transfers between devices, shift(): return lax.ppermute(x, axes, [(i, i ^ mask) for i in range(count)])  70.4 us
    ppermute x14, starting transfers between devices, shift(): return lax.ppermute(x, axes, [(i, i ^ mask) for i in range(count)])  17.9 us
    all_to_all x2, starting transfers between devices, deliver(): return [lax.all_to_all(sent[0], axes, 0, 0, tiled=True)]  11.4 us
    pallas_call x2, Pallas kernels, langreth(): pl.pallas_call(functools.partial(langreth_kernel, kinds, len(sums) > 0, o...  6.32 us
    pallas_call x2, Pallas kernels, local(): pl.pallas_call(functools.partial(middle_kernel, start, spots(staged, Fals...  3.38 us
    ppermute x6, starting transfers between devices, gather(): held[turn ^ bit] = lax.ppermute(piece, 'orb', swap)  3.18 us
    pallas_call x2, Pallas kernels, local(): pl.pallas_call(functools.partial(pack_kernel, blocks, spots(staged, True)...  2.6 us
    unnamed x6, local copies, waits for them, and re-layouts  2.46 us
  transfers between devices with their start and end apart: 22, of which 10 were waited for; matrix products, arithmetic and copies ran while one was open for 2% of the time, Pallas kernels for 5%

profile of v3, /device:TPU:0, one launch (start us, length us, event | category | flops | bytes accessed | tf_op | source)
XLA Modules:
  0.0 121.7 jit_solution(17416756030014984081)
XLA Ops:
  1.2 1.7 %shard_map.28 = (bf16[8,2,1,128,128]{4,3,2,1,0:T(8,128)(2,1)S(1)}, bf16[32,1,2,4,8,128]{5,4,3,2,1,0:T(8,128)(2,1)}) custom-call(s32[1]{0:T(128)} %bitcast.device_ref, bf16[2,1,4,256,256]{4,3,2,1,0:T(8,128)(2,1)S(1)} %copy-done), custom_call_target="tpu_custom_call" | custom-call | tf_op jit(solution)/shard_map/pallas_call | solution.py:416
  2.9 7.3 %all-to-all-start = ((bf16[32,1,2,4,8,128]{5,4,3,2,1,0:T(8,128)(2,1)}), bf16[32,1,2,4,8,128]{5,4,3,2,1,0:T(8,128)(2,1)S(1)}, u32[]{:S(2)}, u32[]{:S(2)}) async-start(bf16[32,1,2,4,8,128]{5,4,3,2,1,0:T(8,128)(2,1)} %get-tuple-element.26), calls=%async_computation | async-start | bytes 1048576 | tf_op jit(solution)/shard_map/all_to_all | solution.py:409
  12.4 1.8 %collective-permute-start.7 = (bf16[2,4,1,2,4,8,128]{6,5,4,3,2,1,0:T(8,128)(2,1)S(1)}, bf16[2,4,1,2,4,8,128]{6,5,4,3,2,1,0:T(8,128)(2,1)S(1)}, u32[]{:S(2)}, u32[]{:S(2)}) collective-permute-start(bf16[2,4,1,2,4,8,128]{6,5,4,3,2,1,0:T(8,128)(2,1)S(1)} %get-tuple-element.36), channel_id=1, source_target_pairs={{0,8},{1,9},{2,10},{3,11},{4,12},{5,13},{6,14},{7,15},{8,0},{9,1},... | collective-permute-start | bytes 393224 | tf_op jit(solution)/shard_map/ppermute | solution.py:344
  14.2 2.4 %collective-permute-start.8 = (bf16[2,4,1,2,4,8,128]{6,5,4,3,2,1,0:T(8,128)(2,1)S(1)}, bf16[2,4,1,2,4,8,128]{6,5,4,3,2,1,0:T(8,128)(2,1)S(1)}, u32[]{:S(2)}, u32[]{:S(2)}) collective-permute-start(bf16[2,4,1,2,4,8,128]{6,5,4,3,2,1,0:T(8,128)(2,1)S(1)} %get-tuple-element.37), channel_id=1, source_target_pairs={{0,16},{1,17},{2,18},{3,19},{4,20},{5,21},{6,22},{7,23},{8,24},{9,... | collective-permute-start | bytes 393224 | tf_op jit(solution)/shard_map/ppermute | solution.py:344
  16.9 6.4 %collective-permute-done.7.refs_1_ = bf16[2,4,1,2,4,8,128]{6,5,4,3,2,1,0:T(8,128)(2,1)S(1)} collective-permute-done((bf16[2,4,1,2,4,8,128]{6,5,4,3,2,1,0:T(8,128)(2,1)S(1)}, bf16[2,4,1,2,4,8,128]{6,5,4,3,2,1,0:T(8,128)(2,1)S(1)}, u32[]{:S(2)}, u32[]{:S(2)}) %collective-permute-start.7) | collective-permute-done | bytes 131104 | tf_op jit(solution)/shard_map/ppermute | solution.py:344
  23.3 11.0 %collective-permute-done.8.refs_2_ = bf16[2,4,1,2,4,8,128]{6,5,4,3,2,1,0:T(8,128)(2,1)S(1)} collective-permute-done((bf16[2,4,1,2,4,8,128]{6,5,4,3,2,1,0:T(8,128)(2,1)S(1)}, bf16[2,4,1,2,4,8,128]{6,5,4,3,2,1,0:T(8,128)(2,1)S(1)}, u32[]{:S(2)}, u32[]{:S(2)}) %collective-permute-start.8) | collective-permute-done | bytes 131104 | tf_op jit(solution)/shard_map/ppermute | solution.py:344
  34.3 1.5 %collective-permute-start.18 = (bf16[8,2,1,128,128]{4,3,2,1,0:T(8,128)(2,1)S(1)}, bf16[8,2,1,128,128]{4,3,2,1,0:T(8,128)(2,1)S(1)}, u32[]{:S(2)}, u32[]{:S(2)}) collective-permute-start(bf16[8,2,1,128,128]{4,3,2,1,0:T(8,128)(2,1)S(1)} %get-tuple-element.44.refs_4_), channel_id=1, source_target_pairs={{0,2},{1,3},{2,0},{3,1},{4,6},{5,7},{6,4},{7,5},{8,10},{9,11},{10,... | collective-permute-start | bytes 1572872 | tf_op jit(solution)/shard_map/ppermute | solution.py:374
  38.6 1.5 %collective-permute-start.12 = (bf16[2,4,1,2,4,8,128]{6,5,4,3,2,1,0:T(8,128)(2,1)S(1)}, bf16[2,4,1,2,4,8,128]{6,5,4,3,2,1,0:T(8,128)(2,1)S(1)}, u32[]{:S(2)}, u32[]{:S(2)}) collective-permute-start(bf16[2,4,1,2,4,8,128]{6,5,4,3,2,1,0:T(8,128)(2,1)S(1)} %get-tuple-element.41), channel_id=1, source_target_pairs={{0,4},{1,5},{2,6},{3,7},{4,0},{5,1},{6,2},{7,3},{8,12},{9,13},{10,... | collective-permute-start | bytes 393224 | tf_op jit(solution)/shard_map/ppermute | solution.py:344
  41.6 1.5 %convert_element_type.14.weight_ref = bf16[128,128]{1,0:T(8,128)(2,1)S(1)} reshape(bf16[16,8,16,8]{3,2,1,0:T(8,128)(2,1)} %multiply_convert_fusion) | data formatting | bytes 65536 | tf_op jit(solution)/shard_map/convert_element_type | solution.py:391
  43.1 20.2 %collective-permute-done.11.refs_1_ = bf16[2,4,1,2,4,8,128]{6,5,4,3,2,1,0:T(8,128)(2,1)S(1)} collective-permute-done((bf16[2,4,1,2,4,8,128]{6,5,4,3,2,1,0:T(8,128)(2,1)}, bf16[2,4,1,2,4,8,128]{6,5,4,3,2,1,0:T(8,128)(2,1)S(1)}, u32[]{:S(2)}, u32[]{:S(2)}) %collective-permute-start.11) | collective-permute-done | bytes 131104 | tf_op jit(solution)/shard_map/ppermute | solution.py:344
  63.3 3.2 %collective-permute-done.13.refs_3_ = bf16[2,4,1,2,4,8,128]{6,5,4,3,2,1,0:T(8,128)(2,1)S(1)} collective-permute-done((bf16[2,4,1,2,4,8,128]{6,5,4,3,2,1,0:T(8,128)(2,1)S(1)}, bf16[2,4,1,2,4,8,128]{6,5,4,3,2,1,0:T(8,128)(2,1)S(1)}, u32[]{:S(2)}, u32[]{:S(2)}) %collective-permute-start.13) | collective-permute-done | bytes 131104 | tf_op jit(solution)/shard_map/ppermute | solution.py:344
  66.4 2.1 %shard_map.32 = bf16[32,1,2,4,8,128]{5,4,3,2,1,0:T(8,128)(2,1)} custom-call(s32[1]{0:T(128)} %bitcast.device_ref, bf16[128,128]{1,0:T(8,128)(2,1)S(1)} %convert_element_type.14.weight_ref, bf16[2,4,1,2,4,8,128]{6,5,4,3,2,1,0:T(8,128)(2,1)S(1)} %get-tuple-element.39.refs_0_, bf16[2,4,1,2,4,8,128]{6,5,4,3,2,1,0:T(8,128)(2,1)S(1)} %collective-permute-done.11.refs_1_, ...), custom_call_target="tpu_custom_call" | custom-call | tf_op jit(solution)/shard_map/pallas_call | solution.py:427
  68.6 4.1 %all-to-all-start.1 = ((bf16[32,1,2,4,8,128]{5,4,3,2,1,0:T(8,128)(2,1)}), bf16[32,1,2,4,8,128]{5,4,3,2,1,0:T(8,128)(2,1)S(1)}, u32[]{:S(2)}, u32[]{:S(2)}) async-start(bf16[32,1,2,4,8,128]{5,4,3,2,1,0:T(8,128)(2,1)} %shard_map.32), calls=%async_computation.1 | async-start | bytes 1048576 | tf_op jit(solution)/shard_map/all_to_all | solution.py:409
  73.9 1.8 %collective-permute-start = (bf16[2,4,1,2,4,8,128]{6,5,4,3,2,1,0:T(8,128)(2,1)S(1)}, bf16[2,4,1,2,4,8,128]{6,5,4,3,2,1,0:T(8,128)(2,1)S(1)}, u32[]{:S(2)}, u32[]{:S(2)}) collective-permute-start(bf16[2,4,1,2,4,8,128]{6,5,4,3,2,1,0:T(8,128)(2,1)S(1)} %get-tuple-element.28), channel_id=1, source_target_pairs={{0,8},{1,9},{2,10},{3,11},{4,12},{5,13},{6,14},{7,15},{8,0},{9,1},... | collective-permute-start | bytes 393224 | tf_op jit(solution)/shard_map/ppermute | solution.py:344
  75.8 2.4 %collective-permute-start.1 = (bf16[2,4,1,2,4,8,128]{6,5,4,3,2,1,0:T(8,128)(2,1)S(1)}, bf16[2,4,1,2,4,8,128]{6,5,4,3,2,1,0:T(8,128)(2,1)S(1)}, u32[]{:S(2)}, u32[]{:S(2)}) collective-permute-start(bf16[2,4,1,2,4,8,128]{6,5,4,3,2,1,0:T(8,128)(2,1)S(1)} %get-tuple-element.29), channel_id=1, source_target_pairs={{0,16},{1,17},{2,18},{3,19},{4,20},{5,21},{6,22},{7,23},{8,24},{9,... | collective-permute-start | bytes 393224 | tf_op jit(solution)/shard_map/ppermute | solution.py:344
  78.4 7.3 %collective-permute-done.refs_1_ = bf16[2,4,1,2,4,8,128]{6,5,4,3,2,1,0:T(8,128)(2,1)S(1)} collective-permute-done((bf16[2,4,1,2,4,8,128]{6,5,4,3,2,1,0:T(8,128)(2,1)S(1)}, bf16[2,4,1,2,4,8,128]{6,5,4,3,2,1,0:T(8,128)(2,1)S(1)}, u32[]{:S(2)}, u32[]{:S(2)}) %collective-permute-start) | collective-permute-done | bytes 131104 | tf_op jit(solution)/shard_map/ppermute | solution.py:344
  85.7 11.0 %collective-permute-done.1.refs_2_ = bf16[2,4,1,2,4,8,128]{6,5,4,3,2,1,0:T(8,128)(2,1)S(1)} collective-permute-done((bf16[2,4,1,2,4,8,128]{6,5,4,3,2,1,0:T(8,128)(2,1)S(1)}, bf16[2,4,1,2,4,8,128]{6,5,4,3,2,1,0:T(8,128)(2,1)S(1)}, u32[]{:S(2)}, u32[]{:S(2)}) %collective-permute-start.1) | collective-permute-done | bytes 131104 | tf_op jit(solution)/shard_map/ppermute | solution.py:344
  98.3 1.5 %collective-permute-start.4 = (bf16[2,4,1,2,4,8,128]{6,5,4,3,2,1,0:T(8,128)(2,1)S(1)}, bf16[2,4,1,2,4,8,128]{6,5,4,3,2,1,0:T(8,128)(2,1)S(1)}, u32[]{:S(2)}, u32[]{:S(2)}) collective-permute-start(bf16[2,4,1,2,4,8,128]{6,5,4,3,2,1,0:T(8,128)(2,1)S(1)} %get-tuple-element.32), channel_id=1, source_target_pairs={{0,2},{1,3},{2,0},{3,1},{4,6},{5,7},{6,4},{7,5},{8,10},{9,11},{10,... | collective-permute-start | bytes 393224 | tf_op jit(solution)/shard_map/ppermute | solution.py:344
  99.8 4.1 %collective-permute-done.4.refs_1_ = bf16[2,4,1,2,4,8,128]{6,5,4,3,2,1,0:T(8,128)(2,1)S(1)} collective-permute-done((bf16[2,4,1,2,4,8,128]{6,5,4,3,2,1,0:T(8,128)(2,1)S(1)}, bf16[2,4,1,2,4,8,128]{6,5,4,3,2,1,0:T(8,128)(2,1)S(1)}, u32[]{:S(2)}, u32[]{:S(2)}) %collective-permute-start.4) | collective-permute-done | bytes 131104 | tf_op jit(solution)/shard_map/ppermute | solution.py:344
  105.4 3.5 %collective-permute-done.5.refs_2_ = bf16[2,4,1,2,4,8,128]{6,5,4,3,2,1,0:T(8,128)(2,1)S(1)} collective-permute-done((bf16[2,4,1,2,4,8,128]{6,5,4,3,2,1,0:T(8,128)(2,1)S(1)}, bf16[2,4,1,2,4,8,128]{6,5,4,3,2,1,0:T(8,128)(2,1)S(1)}, u32[]{:S(2)}, u32[]{:S(2)}) %collective-permute-start.5) | collective-permute-done | bytes 131104 | tf_op jit(solution)/shard_map/ppermute | solution.py:344
  108.8 2.4 %collective-permute-start.6 = (bf16[2,4,1,2,4,8,128]{6,5,4,3,2,1,0:T(8,128)(2,1)S(1)}, bf16[2,4,1,2,4,8,128]{6,5,4,3,2,1,0:T(8,128)(2,1)S(1)}, u32[]{:S(2)}, u32[]{:S(2)}) collective-permute-start(bf16[2,4,1,2,4,8,128]{6,5,4,3,2,1,0:T(8,128)(2,1)S(1)} %get-tuple-element.34), channel_id=1, source_target_pairs={{0,6},{1,7},{2,4},{3,5},{4,2},{5,3},{6,0},{7,1},{8,14},{9,15},{10,... | collective-permute-start | bytes 393224 | tf_op jit(solution)/shard_map/ppermute | solution.py:344
  111.2 3.5 %collective-permute-done.6.refs_3_ = bf16[2,4,1,2,4,8,128]{6,5,4,3,2,1,0:T(8,128)(2,1)S(1)} collective-permute-done((bf16[2,4,1,2,4,8,128]{6,5,4,3,2,1,0:T(8,128)(2,1)S(1)}, bf16[2,4,1,2,4,8,128]{6,5,4,3,2,1,0:T(8,128)(2,1)S(1)}, u32[]{:S(2)}, u32[]{:S(2)}) %collective-permute-start.6) | collective-permute-done | bytes 131104 | tf_op jit(solution)/shard_map/ppermute | solution.py:344
  115.3 4.3 %langreth.2 = (f32[5,2,1,4,128,128]{5,4,3,2,1,0:T(8,128)S(1)}, bf16[2,4,8,2,1,128,128]{6,5,4,3,2,1,0:T(8,128)(2,1)S(1)}) custom-call(s32[1]{0:T(128)} %bitcast.device_ref, bf16[1,1024,512]{2,1,0:T(8,128)(2,1)S(1)} %shard_map.33.left_ref, bf16[8,2,1,128,128]{4,3,2,1,0:T(8,128)(2,1)S(1)} %get-tuple-element.43.refs_0_, ...), custom_call_target="tpu_custom_call" | custom-call | tf_op jit(solution)/shard_map/langreth/pallas_call | solution.py:455
  119.7 2.0 %langreth.3 = bf16[2,1,4,256,256]{4,3,2,1,0:T(8,128)(2,1)} custom-call(s32[1]{0:T(128)} %bitcast.device_ref, bf16[1,512,512]{2,1,0:T(8,128)(2,1)S(1)} %shard_map.30.left_ref, f32[5,2,1,4,128,128]{5,4,3,2,1,0:T(8,128)S(1)} %get-tuple-element.45.refs_0_, bf16[2,4,8,2,1,128,128]{6,5,4,3,2,1,0:T(8,128)(2,1)S(1)} %get-tuple-element.46.refs_1_), custom_call_target="tpu_custom_call" | custom-call | tf_op jit(solution)/shard_map/langreth/pallas_call | solution.py:455
  (41 shorter events, 13.0 us)
Async XLA Ops:
  0.0 40.6 %copy-start.2 = (f32[16,16]{1,0:T(8,128)S(1)}, f32[16,16]{1,0:T(8,128)}, u32[]{:S(2)}) copy-start(f32[16,16]{1,0:T(8,128)} %param.5) | copy-start | bytes 3076
  0.0 1.2 %copy-start = (bf16[2,1,4,256,256]{4,3,2,1,0:T(8,128)(2,1)S(1)}, bf16[2,1,4,256,256]{4,3,2,1,0:T(8,128)(2,1)}, u32[]{:S(2)}) copy-start(bf16[2,1,4,256,256]{4,3,2,1,0:T(8,128)(2,1)} %green_ref.3) | copy-start | bytes 3145732
  2.9 65.6 %all-to-all-start = ((bf16[32,1,2,4,8,128]{5,4,3,2,1,0:T(8,128)(2,1)}), bf16[32,1,2,4,8,128]{5,4,3,2,1,0:T(8,128)(2,1)S(1)}, u32[]{:S(2)}, u32[]{:S(2)}) async-start(bf16[32,1,2,4,8,128]{5,4,3,2,1,0:T(8,128)(2,1)} %get-tuple-element.26), calls=%async_computation | async-start | bytes 1048576 | tf_op jit(solution)/shard_map/all_to_all | solution.py:409
  12.4 10.9 %collective-permute-start.7 = (bf16[2,4,1,2,4,8,128]{6,5,4,3,2,1,0:T(8,128)(2,1)S(1)}, bf16[2,4,1,2,4,8,128]{6,5,4,3,2,1,0:T(8,128)(2,1)S(1)}, u32[]{:S(2)}, u32[]{:S(2)}) collective-permute-start(bf16[2,4,1,2,4,8,128]{6,5,4,3,2,1,0:T(8,128)(2,1)S(1)} %get-tuple-element.36), channel_id=1, source_target_pairs={{0,8},{1,9},{2,10},{3,11},{4,12},{5,13},{6,14},{7,15},{8,0},{9,1},... | collective-permute-start | bytes 393224 | tf_op jit(solution)/shard_map/ppermute | solution.py:344
  14.2 20.0 %collective-permute-start.8 = (bf16[2,4,1,2,4,8,128]{6,5,4,3,2,1,0:T(8,128)(2,1)S(1)}, bf16[2,4,1,2,4,8,128]{6,5,4,3,2,1,0:T(8,128)(2,1)S(1)}, u32[]{:S(2)}, u32[]{:S(2)}) collective-permute-start(bf16[2,4,1,2,4,8,128]{6,5,4,3,2,1,0:T(8,128)(2,1)S(1)} %get-tuple-element.37), channel_id=1, source_target_pairs={{0,16},{1,17},{2,18},{3,19},{4,20},{5,21},{6,22},{7,23},{8,24},{9,... | collective-permute-start | bytes 393224 | tf_op jit(solution)/shard_map/ppermute | solution.py:344
  16.7 17.6 %collective-permute-start.9 = (bf16[2,4,1,2,4,8,128]{6,5,4,3,2,1,0:T(8,128)(2,1)S(1)}, bf16[2,4,1,2,4,8,128]{6,5,4,3,2,1,0:T(8,128)(2,1)S(1)}, u32[]{:S(2)}, u32[]{:S(2)}) collective-permute-start(bf16[2,4,1,2,4,8,128]{6,5,4,3,2,1,0:T(8,128)(2,1)S(1)} %get-tuple-element.38), channel_id=1, source_target_pairs={{0,24},{1,25},{2,26},{3,27},{4,28},{5,29},{6,30},{7,31},{8,16},{9,... | collective-permute-start | bytes 393224 | tf_op jit(solution)/shard_map/ppermute | solution.py:344
  34.3 2.2 %collective-permute-start.10 = (bf16[4,4,1,2,4,8,128]{6,5,4,3,2,1,0:T(8,128)(2,1)S(1)}, bf16[4,4,1,2,4,8,128]{6,5,4,3,2,1,0:T(8,128)(2,1)S(1)}, u32[]{:S(2)}, u32[]{:S(2)}) collective-permute-start(bf16[4,4,1,2,4,8,128]{6,5,4,3,2,1,0:T(8,128)(2,1)S(1)} %near.3), channel_id=1, source_target_pairs={{0,1},{1,0},{2,3},{3,2},{4,5},{5,4},{6,7},{7,6},{8,9},{9,8},{10,11... | collective-permute-start | bytes 786440 | tf_op jit(solution)/shard_map/ppermute | solution.py:344
  34.3 62.9 %collective-permute-start.18 = (bf16[8,2,1,128,128]{4,3,2,1,0:T(8,128)(2,1)S(1)}, bf16[8,2,1,128,128]{4,3,2,1,0:T(8,128)(2,1)S(1)}, u32[]{:S(2)}, u32[]{:S(2)}) collective-permute-start(bf16[8,2,1,128,128]{4,3,2,1,0:T(8,128)(2,1)S(1)} %get-tuple-element.44.refs_4_), channel_id=1, source_target_pairs={{0,2},{1,3},{2,0},{3,1},{4,6},{5,7},{6,4},{7,5},{8,10},{9,11},{10,... | collective-permute-start | bytes 1572872 | tf_op jit(solution)/shard_map/ppermute | solution.py:374
  35.9 61.9 %collective-permute-start.15 = (bf16[8,2,1,128,128]{4,3,2,1,0:T(8,128)(2,1)S(1)}, bf16[8,2,1,128,128]{4,3,2,1,0:T(8,128)(2,1)S(1)}, u32[]{:S(2)}, u32[]{:S(2)}) collective-permute-start(bf16[8,2,1,128,128]{4,3,2,1,0:T(8,128)(2,1)S(1)} %get-tuple-element.43.refs_0_), channel_id=1, source_target_pairs={{0,2},{1,3},{2,0},{3,1},{4,6},{5,7},{6,4},{7,5},{8,10},{9,11},{10,... | collective-permute-start | bytes 1572872 | tf_op jit(solution)/shard_map/ppermute | solution.py:374
  37.1 26.1 %collective-permute-start.11 = (bf16[2,4,1,2,4,8,128]{6,5,4,3,2,1,0:T(8,128)(2,1)}, bf16[2,4,1,2,4,8,128]{6,5,4,3,2,1,0:T(8,128)(2,1)S(1)}, u32[]{:S(2)}, u32[]{:S(2)}) collective-permute-start(bf16[2,4,1,2,4,8,128]{6,5,4,3,2,1,0:T(8,128)(2,1)} %get-tuple-element.40), channel_id=1, source_target_pairs={{0,2},{1,3},{2,0},{3,1},{4,6},{5,7},{6,4},{7,5},{8,10},{9,11},{10,... | collective-permute-start | bytes 393224 | tf_op jit(solution)/shard_map/ppermute | solution.py:344
  38.6 24.7 %collective-permute-start.12 = (bf16[2,4,1,2,4,8,128]{6,5,4,3,2,1,0:T(8,128)(2,1)S(1)}, bf16[2,4,1,2,4,8,128]{6,5,4,3,2,1,0:T(8,128)(2,1)S(1)}, u32[]{:S(2)}, u32[]{:S(2)}) collective-permute-start(bf16[2,4,1,2,4,8,128]{6,5,4,3,2,1,0:T(8,128)(2,1)S(1)} %get-tuple-element.41), channel_id=1, source_target_pairs={{0,4},{1,5},{2,6},{3,7},{4,0},{5,1},{6,2},{7,3},{8,12},{9,13},{10,... | collective-permute-start | bytes 393224 | tf_op jit(solution)/shard_map/ppermute | solution.py:344
  40.1 26.3 %collective-permute-start.13 = (bf16[2,4,1,2,4,8,128]{6,5,4,3,2,1,0:T(8,128)(2,1)S(1)}, bf16[2,4,1,2,4,8,128]{6,5,4,3,2,1,0:T(8,128)(2,1)S(1)}, u32[]{:S(2)}, u32[]{:S(2)}) collective-permute-start(bf16[2,4,1,2,4,8,128]{6,5,4,3,2,1,0:T(8,128)(2,1)S(1)} %get-tuple-element.42), channel_id=1, source_target_pairs={{0,6},{1,7},{2,4},{3,5},{4,2},{5,3},{6,0},{7,1},{8,14},{9,15},{10,... | collective-permute-start | bytes 393224 | tf_op jit(solution)/shard_map/ppermute | solution.py:344
  68.6 46.4 %all-to-all-start.1 = ((bf16[32,1,2,4,8,128]{5,4,3,2,1,0:T(8,128)(2,1)}), bf16[32,1,2,4,8,128]{5,4,3,2,1,0:T(8,128)(2,1)S(1)}, u32[]{:S(2)}, u32[]{:S(2)}) async-start(bf16[32,1,2,4,8,128]{5,4,3,2,1,0:T(8,128)(2,1)} %shard_map.32), calls=%async_computation.1 | async-start | bytes 1048576 | tf_op jit(solution)/shard_map/all_to_all | solution.py:409
  73.9 11.7 %collective-permute-start = (bf16[2,4,1,2,4,8,128]{6,5,4,3,2,1,0:T(8,128)(2,1)S(1)}, bf16[2,4,1,2,4,8,128]{6,5,4,3,2,1,0:T(8,128)(2,1)S(1)}, u32[]{:S(2)}, u32[]{:S(2)}) collective-permute-start(bf16[2,4,1,2,4,8,128]{6,5,4,3,2,1,0:T(8,128)(2,1)S(1)} %get-tuple-element.28), channel_id=1, source_target_pairs={{0,8},{1,9},{2,10},{3,11},{4,12},{5,13},{6,14},{7,15},{8,0},{9,1},... | collective-permute-start | bytes 393224 | tf_op jit(solution)/shard_map/ppermute | solution.py:344
  75.8 20.8 %collective-permute-start.1 = (bf16[2,4,1,2,4,8,128]{6,5,4,3,2,1,0:T(8,128)(2,1)S(1)}, bf16[2,4,1,2,4,8,128]{6,5,4,3,2,1,0:T(8,128)(2,1)S(1)}, u32[]{:S(2)}, u32[]{:S(2)}) collective-permute-start(bf16[2,4,1,2,4,8,128]{6,5,4,3,2,1,0:T(8,128)(2,1)S(1)} %get-tuple-element.29), channel_id=1, source_target_pairs={{0,16},{1,17},{2,18},{3,19},{4,20},{5,21},{6,22},{7,23},{8,24},{9,... | collective-permute-start | bytes 393224 | tf_op jit(solution)/shard_map/ppermute | solution.py:344
  78.2 18.4 %collective-permute-start.2 = (bf16[2,4,1,2,4,8,128]{6,5,4,3,2,1,0:T(8,128)(2,1)S(1)}, bf16[2,4,1,2,4,8,128]{6,5,4,3,2,1,0:T(8,128)(2,1)S(1)}, u32[]{:S(2)}, u32[]{:S(2)}) collective-permute-start(bf16[2,4,1,2,4,8,128]{6,5,4,3,2,1,0:T(8,128)(2,1)S(1)} %get-tuple-element.30), channel_id=1, source_target_pairs={{0,24},{1,25},{2,26},{3,27},{4,28},{5,29},{6,30},{7,31},{8,16},{9,... | collective-permute-start | bytes 393224 | tf_op jit(solution)/shard_map/ppermute | solution.py:344
  96.6 1.6 %collective-permute-start.3 = (bf16[4,4,1,2,4,8,128]{6,5,4,3,2,1,0:T(8,128)(2,1)S(1)}, bf16[4,4,1,2,4,8,128]{6,5,4,3,2,1,0:T(8,128)(2,1)S(1)}, u32[]{:S(2)}, u32[]{:S(2)}) collective-permute-start(bf16[4,4,1,2,4,8,128]{6,5,4,3,2,1,0:T(8,128)(2,1)S(1)} %near.2), channel_id=1, source_target_pairs={{0,1},{1,0},{2,3},{3,2},{4,5},{5,4},{6,7},{7,6},{8,9},{9,8},{10,11... | collective-permute-start | bytes 786440 | tf_op jit(solution)/shard_map/ppermute | solution.py:344
  96.7 18.6 %collective-permute-start.17 = (bf16[8,2,1,128,128]{4,3,2,1,0:T(8,128)(2,1)S(1)}, bf16[8,2,1,128,128]{4,3,2,1,0:T(8,128)(2,1)}, u32[]{:S(2)}, u32[]{:S(2)}) collective-permute-start(bf16[8,2,1,128,128]{4,3,2,1,0:T(8,128)(2,1)S(1)} %get-tuple-element.44.refs_4_), channel_id=1, source_target_pairs={{0,1},{1,0},{2,3},{3,2},{4,5},{5,4},{6,7},{7,6},{8,9},{9,8},{10,11... | collective-permute-start | bytes 1572872 | tf_op jit(solution)/shard_map/ppermute | solution.py:374
  97.2 18.1 %collective-permute-start.14 = (bf16[8,2,1,128,128]{4,3,2,1,0:T(8,128)(2,1)S(1)}, bf16[8,2,1,128,128]{4,3,2,1,0:T(8,128)(2,1)}, u32[]{:S(2)}, u32[]{:S(2)}) collective-permute-start(bf16[8,2,1,128,128]{4,3,2,1,0:T(8,128)(2,1)S(1)} %get-tuple-element.43.refs_0_), channel_id=1, source_target_pairs={{0,1},{1,0},{2,3},{3,2},{4,5},{5,4},{6,7},{7,6},{8,9},{9,8},{10,11... | collective-permute-start | bytes 1572872 | tf_op jit(solution)/shard_map/ppermute | solution.py:374
  97.3 18.0 %collective-permute-start.19 = (bf16[8,2,1,128,128]{4,3,2,1,0:T(8,128)(2,1)S(1)}, bf16[8,2,1,128,128]{4,3,2,1,0:T(8,128)(2,1)}, u32[]{:S(2)}, u32[]{:S(2)}) collective-permute-start(bf16[8,2,1,128,128]{4,3,2,1,0:T(8,128)(2,1)S(1)} %collective-permute-done.18.refs_6_), channel_id=1, source_target_pairs={{0,1},{1,0},{2,3},{3,2},{4,5},{5,4},{6,7},{7,6},{8,9},{9,8},{10,11... | collective-permute-start | bytes 1572872 | tf_op jit(solution)/shard_map/ppermute | solution.py:374
  97.7 17.6 %collective-permute-start.16 = (bf16[8,2,1,128,128]{4,3,2,1,0:T(8,128)(2,1)S(1)}, bf16[8,2,1,128,128]{4,3,2,1,0:T(8,128)(2,1)}, u32[]{:S(2)}, u32[]{:S(2)}) collective-permute-start(bf16[8,2,1,128,128]{4,3,2,1,0:T(8,128)(2,1)S(1)} %collective-permute-done.15.refs_2_), channel_id=1, source_target_pairs={{0,1},{1,0},{2,3},{3,2},{4,5},{5,4},{6,7},{7,6},{8,9},{9,8},{10,11... | collective-permute-start | bytes 1572872 | tf_op jit(solution)/shard_map/ppermute | solution.py:374
  98.3 5.6 %collective-permute-start.4 = (bf16[2,4,1,2,4,8,128]{6,5,4,3,2,1,0:T(8,128)(2,1)S(1)}, bf16[2,4,1,2,4,8,128]{6,5,4,3,2,1,0:T(8,128)(2,1)S(1)}, u32[]{:S(2)}, u32[]{:S(2)}) collective-permute-start(bf16[2,4,1,2,4,8,128]{6,5,4,3,2,1,0:T(8,128)(2,1)S(1)} %get-tuple-element.32), channel_id=1, source_target_pairs={{0,2},{1,3},{2,0},{3,1},{4,6},{5,7},{6,4},{7,5},{8,10},{9,11},{10,... | collective-permute-start | bytes 393224 | tf_op jit(solution)/shard_map/ppermute | solution.py:344
  103.9 5.0 %collective-permute-start.5 = (bf16[2,4,1,2,4,8,128]{6,5,4,3,2,1,0:T(8,128)(2,1)S(1)}, bf16[2,4,1,2,4,8,128]{6,5,4,3,2,1,0:T(8,128)(2,1)S(1)}, u32[]{:S(2)}, u32[]{:S(2)}) collective-permute-start(bf16[2,4,1,2,4,8,128]{6,5,4,3,2,1,0:T(8,128)(2,1)S(1)} %get-tuple-element.33), channel_id=1, source_target_pairs={{0,4},{1,5},{2,6},{3,7},{4,0},{5,1},{6,2},{7,3},{8,12},{9,13},{10,... | collective-permute-start | bytes 393224 | tf_op jit(solution)/shard_map/ppermute | solution.py:344
  108.8 5.9 %collective-permute-start.6 = (bf16[2,4,1,2,4,8,128]{6,5,4,3,2,1,0:T(8,128)(2,1)S(1)}, bf16[2,4,1,2,4,8,128]{6,5,4,3,2,1,0:T(8,128)(2,1)S(1)}, u32[]{:S(2)}, u32[]{:S(2)}) collective-permute-start(bf16[2,4,1,2,4,8,128]{6,5,4,3,2,1,0:T(8,128)(2,1)S(1)} %get-tuple-element.34), channel_id=1, source_target_pairs={{0,6},{1,7},{2,4},{3,5},{4,2},{5,3},{6,0},{7,1},{8,14},{9,15},{10,... | collective-permute-start | bytes 393224 | tf_op jit(solution)/shard_map/ppermute | solution.py:344
  (1 other events, 1.2 us)

commit v4 on v3

--- a/solution.py
+++ b/solution.py
@@ -50,6 +50,17 @@
 
 def entries(spots):
     return 1 if spots is None else 1 + max(n for n, _ in spots)
+
+
+def grouped(size, step, group):
+    group = math.gcd(size, group)
+
+    def several(n, carry):
+        for i in range(group):
+            carry = step(group * n + i, carry)
+        return carry
+
+    lax.fori_loop(0, size // group, several, 0)
 
 
 def halves(own, facing, count):
@@ -85,7 +96,7 @@
                 block_scr[d, k, part, pair] = piece.astype(BF16)
         return carry
 
-    lax.fori_loop(0, parts * pairs, one, 0)
+    grouped(parts * pairs, one, 8)
     emit(block_scr, device_ref[0], out_refs, spots)
 
 
@@ -162,7 +173,7 @@
             product_scr[pair, :, lanes(1, r)] = re * mim + im * mre
         return carry
 
-    lax.fori_loop(0, all_pairs, forward, 0)
+    grouped(all_pairs, forward, 2)
     product = product_scr[...].reshape(all_pairs * rows2, -1).astype(BF16)
     bubble = jnp.dot(weight_ref[...], product, preferred_element_type=F32)
     product_scr[...] = bubble.reshape(product_scr.shape)
@@ -181,7 +192,7 @@
                     block_scr[w * orbs + orb, k, part, local] = values[w * per_device + k][part].astype(BF16)
         return carry
 
-    lax.fori_loop(0, all_pairs, backward, 0)
+    grouped(all_pairs, backward, 2)
     emit(block_scr, me, out_refs, sent_spots)
 
 

time: 122 us -> 121 us (level)
  Pallas kernels: 13.6 us -> 12.2 us
  transfers between devices with their start and end apart: 22 -> 22, of which waited for: 10 -> 10; matrix products, arithmetic and copies ran while one was open for 2% -> 2% of each run, Pallas kernels for 5% -> 4%
where the time goes in v4:
time: 121 us
  waiting for transfers between devices  71.2 us (59%)
  starting transfers between devices  32.5 us (27%)
  Pallas kernels  12.2 us (10%)
  local copies, waits for them, and re-layouts  3.96 us (3%)
    ppermute x14, waiting for transfers between devices, shift(): return lax.ppermute(x, axes, [(i, i ^ mask) for i in range(count)])  71.1 us
    ppermute x14, starting transfers between devices, shift(): return lax.ppermute(x, axes, [(i, i ^ mask) for i in range(count)])  17.9 us
    all_to_all x2, starting transfers between devices, deliver(): return [lax.all_to_all(sent[0], axes, 0, 0, tiled=True)]  11.4 us
    pallas_call x2, Pallas kernels, langreth(): pl.pallas_call(functools.partial(langreth_kernel, kinds, len(sums) > 0, o...  6.32 us
    ppermute x6, starting transfers between devices, gather(): held[turn ^ bit] = lax.ppermute(piece, 'orb', swap)  3.18 us
    pallas_call x2, Pallas kernels, local(): pl.pallas_call(functools.partial(middle_kernel, start, spots(staged, Fals...  3.12 us
    unnamed x6, local copies, waits for them, and re-layouts  2.46 us
  transfers between devices with their start and end apart: 22, of which 10 were waited for; matrix products, arithmetic and copies ran while one was open for 2% of the time, Pallas kernels for 4%

profile of v4, /device:TPU:0, one launch (start us, length us, event | category | flops | bytes accessed | tf_op | source)
XLA Modules:
  0.0 121.0 jit_solution(2485195264355440573)
XLA Ops:
  2.4 7.3 %all-to-all-start = ((bf16[32,1,2,4,8,128]{5,4,3,2,1,0:T(8,128)(2,1)}), bf16[32,1,2,4,8,128]{5,4,3,2,1,0:T(8,128)(2,1)S(1)}, u32[]{:S(2)}, u32[]{:S(2)}) async-start(bf16[32,1,2,4,8,128]{5,4,3,2,1,0:T(8,128)(2,1)} %get-tuple-element.26), calls=%async_computation | async-start | bytes 1048576 | tf_op jit(solution)/shard_map/all_to_all | solution.py:420
  11.3 1.8 %collective-permute-start.7 = (bf16[2,4,1,2,4,8,128]{6,5,4,3,2,1,0:T(8,128)(2,1)S(1)}, bf16[2,4,1,2,4,8,128]{6,5,4,3,2,1,0:T(8,128)(2,1)S(1)}, u32[]{:S(2)}, u32[]{:S(2)}) collective-permute-start(bf16[2,4,1,2,4,8,128]{6,5,4,3,2,1,0:T(8,128)(2,1)S(1)} %get-tuple-element.36), channel_id=1, source_target_pairs={{0,8},{1,9},{2,10},{3,11},{4,12},{5,13},{6,14},{7,15},{8,0},{9,1},... | collective-permute-start | bytes 393224 | tf_op jit(solution)/shard_map/ppermute | solution.py:355
  13.1 2.4 %collective-permute-start.8 = (bf16[2,4,1,2,4,8,128]{6,5,4,3,2,1,0:T(8,128)(2,1)S(1)}, bf16[2,4,1,2,4,8,128]{6,5,4,3,2,1,0:T(8,128)(2,1)S(1)}, u32[]{:S(2)}, u32[]{:S(2)}) collective-permute-start(bf16[2,4,1,2,4,8,128]{6,5,4,3,2,1,0:T(8,128)(2,1)S(1)} %get-tuple-element.37), channel_id=1, source_target_pairs={{0,16},{1,17},{2,18},{3,19},{4,20},{5,21},{6,22},{7,23},{8,24},{9,... | collective-permute-start | bytes 393224 | tf_op jit(solution)/shard_map/ppermute | solution.py:355
  15.7 7.0 %collective-permute-done.7.refs_1_ = bf16[2,4,1,2,4,8,128]{6,5,4,3,2,1,0:T(8,128)(2,1)S(1)} collective-permute-done((bf16[2,4,1,2,4,8,128]{6,5,4,3,2,1,0:T(8,128)(2,1)S(1)}, bf16[2,4,1,2,4,8,128]{6,5,4,3,2,1,0:T(8,128)(2,1)S(1)}, u32[]{:S(2)}, u32[]{:S(2)}) %collective-permute-start.7) | collective-permute-done | bytes 131104 | tf_op jit(solution)/shard_map/ppermute | solution.py:355
  22.7 11.0 %collective-permute-done.8.refs_2_ = bf16[2,4,1,2,4,8,128]{6,5,4,3,2,1,0:T(8,128)(2,1)S(1)} collective-permute-done((bf16[2,4,1,2,4,8,128]{6,5,4,3,2,1,0:T(8,128)(2,1)S(1)}, bf16[2,4,1,2,4,8,128]{6,5,4,3,2,1,0:T(8,128)(2,1)S(1)}, u32[]{:S(2)}, u32[]{:S(2)}) %collective-permute-start.8) | collective-permute-done | bytes 131104 | tf_op jit(solution)/shard_map/ppermute | solution.py:355
  33.8 1.5 %collective-permute-start.18 = (bf16[8,2,1,128,128]{4,3,2,1,0:T(8,128)(2,1)S(1)}, bf16[8,2,1,128,128]{4,3,2,1,0:T(8,128)(2,1)S(1)}, u32[]{:S(2)}, u32[]{:S(2)}) collective-permute-start(bf16[8,2,1,128,128]{4,3,2,1,0:T(8,128)(2,1)S(1)} %get-tuple-element.44.refs_4_), channel_id=1, source_target_pairs={{0,2},{1,3},{2,0},{3,1},{4,6},{5,7},{6,4},{7,5},{8,10},{9,11},{10,... | collective-permute-start | bytes 1572872 | tf_op jit(solution)/shard_map/ppermute | solution.py:385
  38.0 1.5 %collective-permute-start.12 = (bf16[2,4,1,2,4,8,128]{6,5,4,3,2,1,0:T(8,128)(2,1)S(1)}, bf16[2,4,1,2,4,8,128]{6,5,4,3,2,1,0:T(8,128)(2,1)S(1)}, u32[]{:S(2)}, u32[]{:S(2)}) collective-permute-start(bf16[2,4,1,2,4,8,128]{6,5,4,3,2,1,0:T(8,128)(2,1)S(1)} %get-tuple-element.41), channel_id=1, source_target_pairs={{0,4},{1,5},{2,6},{3,7},{4,0},{5,1},{6,2},{7,3},{8,12},{9,13},{10,... | collective-permute-start | bytes 393224 | tf_op jit(solution)/shard_map/ppermute | solution.py:355
  41.0 1.5 %convert_element_type.14.weight_ref = bf16[128,128]{1,0:T(8,128)(2,1)S(1)} reshape(bf16[16,8,16,8]{3,2,1,0:T(8,128)(2,1)} %multiply_convert_fusion) | data formatting | bytes 65536 | tf_op jit(solution)/shard_map/convert_element_type | solution.py:402
  42.5 20.2 %collective-permute-done.11.refs_1_ = bf16[2,4,1,2,4,8,128]{6,5,4,3,2,1,0:T(8,128)(2,1)S(1)} collective-permute-done((bf16[2,4,1,2,4,8,128]{6,5,4,3,2,1,0:T(8,128)(2,1)}, bf16[2,4,1,2,4,8,128]{6,5,4,3,2,1,0:T(8,128)(2,1)S(1)}, u32[]{:S(2)}, u32[]{:S(2)}) %collective-permute-start.11) | collective-permute-done | bytes 131104 | tf_op jit(solution)/shard_map/ppermute | solution.py:355
  62.7 3.2 %collective-permute-done.13.refs_3_ = bf16[2,4,1,2,4,8,128]{6,5,4,3,2,1,0:T(8,128)(2,1)S(1)} collective-permute-done((bf16[2,4,1,2,4,8,128]{6,5,4,3,2,1,0:T(8,128)(2,1)S(1)}, bf16[2,4,1,2,4,8,128]{6,5,4,3,2,1,0:T(8,128)(2,1)S(1)}, u32[]{:S(2)}, u32[]{:S(2)}) %collective-permute-start.13) | collective-permute-done | bytes 131104 | tf_op jit(solution)/shard_map/ppermute | solution.py:355
  65.9 2.0 %shard_map.32 = bf16[32,1,2,4,8,128]{5,4,3,2,1,0:T(8,128)(2,1)} custom-call(s32[1]{0:T(128)} %bitcast.device_ref, bf16[128,128]{1,0:T(8,128)(2,1)S(1)} %convert_element_type.14.weight_ref, bf16[2,4,1,2,4,8,128]{6,5,4,3,2,1,0:T(8,128)(2,1)S(1)} %get-tuple-element.39.refs_0_, bf16[2,4,1,2,4,8,128]{6,5,4,3,2,1,0:T(8,128)(2,1)S(1)} %collective-permute-done.11.refs_1_, ...), custom_call_target="tpu_custom_call" | custom-call | tf_op jit(solution)/shard_map/pallas_call | solution.py:438
  67.9 4.1 %all-to-all-start.1 = ((bf16[32,1,2,4,8,128]{5,4,3,2,1,0:T(8,128)(2,1)}), bf16[32,1,2,4,8,128]{5,4,3,2,1,0:T(8,128)(2,1)S(1)}, u32[]{:S(2)}, u32[]{:S(2)}) async-start(bf16[32,1,2,4,8,128]{5,4,3,2,1,0:T(8,128)(2,1)} %shard_map.32), calls=%async_computation.1 | async-start | bytes 1048576 | tf_op jit(solution)/shard_map/all_to_all | solution.py:420
  73.1 1.8 %collective-permute-start = (bf16[2,4,1,2,4,8,128]{6,5,4,3,2,1,0:T(8,128)(2,1)S(1)}, bf16[2,4,1,2,4,8,128]{6,5,4,3,2,1,0:T(8,128)(2,1)S(1)}, u32[]{:S(2)}, u32[]{:S(2)}) collective-permute-start(bf16[2,4,1,2,4,8,128]{6,5,4,3,2,1,0:T(8,128)(2,1)S(1)} %get-tuple-element.28), channel_id=1, source_target_pairs={{0,8},{1,9},{2,10},{3,11},{4,12},{5,13},{6,14},{7,15},{8,0},{9,1},... | collective-permute-start | bytes 393224 | tf_op jit(solution)/shard_map/ppermute | solution.py:355
  74.9 2.4 %collective-permute-start.1 = (bf16[2,4,1,2,4,8,128]{6,5,4,3,2,1,0:T(8,128)(2,1)S(1)}, bf16[2,4,1,2,4,8,128]{6,5,4,3,2,1,0:T(8,128)(2,1)S(1)}, u32[]{:S(2)}, u32[]{:S(2)}) collective-permute-start(bf16[2,4,1,2,4,8,128]{6,5,4,3,2,1,0:T(8,128)(2,1)S(1)} %get-tuple-element.29), channel_id=1, source_target_pairs={{0,16},{1,17},{2,18},{3,19},{4,20},{5,21},{6,22},{7,23},{8,24},{9,... | collective-permute-start | bytes 393224 | tf_op jit(solution)/shard_map/ppermute | solution.py:355
  77.6 7.4 %collective-permute-done.refs_1_ = bf16[2,4,1,2,4,8,128]{6,5,4,3,2,1,0:T(8,128)(2,1)S(1)} collective-permute-done((bf16[2,4,1,2,4,8,128]{6,5,4,3,2,1,0:T(8,128)(2,1)S(1)}, bf16[2,4,1,2,4,8,128]{6,5,4,3,2,1,0:T(8,128)(2,1)S(1)}, u32[]{:S(2)}, u32[]{:S(2)}) %collective-permute-start) | collective-permute-done | bytes 131104 | tf_op jit(solution)/shard_map/ppermute | solution.py:355
  85.0 11.0 %collective-permute-done.1.refs_2_ = bf16[2,4,1,2,4,8,128]{6,5,4,3,2,1,0:T(8,128)(2,1)S(1)} collective-permute-done((bf16[2,4,1,2,4,8,128]{6,5,4,3,2,1,0:T(8,128)(2,1)S(1)}, bf16[2,4,1,2,4,8,128]{6,5,4,3,2,1,0:T(8,128)(2,1)S(1)}, u32[]{:S(2)}, u32[]{:S(2)}) %collective-permute-start.1) | collective-permute-done | bytes 131104 | tf_op jit(solution)/shard_map/ppermute | solution.py:355
  97.6 1.5 %collective-permute-start.4 = (bf16[2,4,1,2,4,8,128]{6,5,4,3,2,1,0:T(8,128)(2,1)S(1)}, bf16[2,4,1,2,4,8,128]{6,5,4,3,2,1,0:T(8,128)(2,1)S(1)}, u32[]{:S(2)}, u32[]{:S(2)}) collective-permute-start(bf16[2,4,1,2,4,8,128]{6,5,4,3,2,1,0:T(8,128)(2,1)S(1)} %get-tuple-element.32), channel_id=1, source_target_pairs={{0,2},{1,3},{2,0},{3,1},{4,6},{5,7},{6,4},{7,5},{8,10},{9,11},{10,... | collective-permute-start | bytes 393224 | tf_op jit(solution)/shard_map/ppermute | solution.py:355
  99.1 4.1 %collective-permute-done.4.refs_1_ = bf16[2,4,1,2,4,8,128]{6,5,4,3,2,1,0:T(8,128)(2,1)S(1)} collective-permute-done((bf16[2,4,1,2,4,8,128]{6,5,4,3,2,1,0:T(8,128)(2,1)S(1)}, bf16[2,4,1,2,4,8,128]{6,5,4,3,2,1,0:T(8,128)(2,1)S(1)}, u32[]{:S(2)}, u32[]{:S(2)}) %collective-permute-start.4) | collective-permute-done | bytes 131104 | tf_op jit(solution)/shard_map/ppermute | solution.py:355
  103.2 1.5 %collective-permute-start.5 = (bf16[2,4,1,2,4,8,128]{6,5,4,3,2,1,0:T(8,128)(2,1)S(1)}, bf16[2,4,1,2,4,8,128]{6,5,4,3,2,1,0:T(8,128)(2,1)S(1)}, u32[]{:S(2)}, u32[]{:S(2)}) collective-permute-start(bf16[2,4,1,2,4,8,128]{6,5,4,3,2,1,0:T(8,128)(2,1)S(1)} %get-tuple-element.33), channel_id=1, source_target_pairs={{0,4},{1,5},{2,6},{3,7},{4,0},{5,1},{6,2},{7,3},{8,12},{9,13},{10,... | collective-permute-start | bytes 393224 | tf_op jit(solution)/shard_map/ppermute | solution.py:355
  104.7 3.5 %collective-permute-done.5.refs_2_ = bf16[2,4,1,2,4,8,128]{6,5,4,3,2,1,0:T(8,128)(2,1)S(1)} collective-permute-done((bf16[2,4,1,2,4,8,128]{6,5,4,3,2,1,0:T(8,128)(2,1)S(1)}, bf16[2,4,1,2,4,8,128]{6,5,4,3,2,1,0:T(8,128)(2,1)S(1)}, u32[]{:S(2)}, u32[]{:S(2)}) %collective-permute-start.5) | collective-permute-done | bytes 131104 | tf_op jit(solution)/shard_map/ppermute | solution.py:355
  108.1 2.4 %collective-permute-start.6 = (bf16[2,4,1,2,4,8,128]{6,5,4,3,2,1,0:T(8,128)(2,1)S(1)}, bf16[2,4,1,2,4,8,128]{6,5,4,3,2,1,0:T(8,128)(2,1)S(1)}, u32[]{:S(2)}, u32[]{:S(2)}) collective-permute-start(bf16[2,4,1,2,4,8,128]{6,5,4,3,2,1,0:T(8,128)(2,1)S(1)} %get-tuple-element.34), channel_id=1, source_target_pairs={{0,6},{1,7},{2,4},{3,5},{4,2},{5,3},{6,0},{7,1},{8,14},{9,15},{10,... | collective-permute-start | bytes 393224 | tf_op jit(solution)/shard_map/ppermute | solution.py:355
  110.5 3.5 %collective-permute-done.6.refs_3_ = bf16[2,4,1,2,4,8,128]{6,5,4,3,2,1,0:T(8,128)(2,1)S(1)} collective-permute-done((bf16[2,4,1,2,4,8,128]{6,5,4,3,2,1,0:T(8,128)(2,1)S(1)}, bf16[2,4,1,2,4,8,128]{6,5,4,3,2,1,0:T(8,128)(2,1)S(1)}, u32[]{:S(2)}, u32[]{:S(2)}) %collective-permute-start.6) | collective-permute-done | bytes 131104 | tf_op jit(solution)/shard_map/ppermute | solution.py:355
  114.6 4.3 %langreth.2 = (f32[5,2,1,4,128,128]{5,4,3,2,1,0:T(8,128)S(1)}, bf16[2,4,8,2,1,128,128]{6,5,4,3,2,1,0:T(8,128)(2,1)S(1)}) custom-call(s32[1]{0:T(128)} %bitcast.device_ref, bf16[1,1024,512]{2,1,0:T(8,128)(2,1)S(1)} %shard_map.33.left_ref, bf16[8,2,1,128,128]{4,3,2,1,0:T(8,128)(2,1)S(1)} %get-tuple-element.43.refs_0_, ...), custom_call_target="tpu_custom_call" | custom-call | tf_op jit(solution)/shard_map/langreth/pallas_call | solution.py:466
  119.0 2.0 %langreth.3 = bf16[2,1,4,256,256]{4,3,2,1,0:T(8,128)(2,1)} custom-call(s32[1]{0:T(128)} %bitcast.device_ref, bf16[1,512,512]{2,1,0:T(8,128)(2,1)S(1)} %shard_map.30.left_ref, f32[5,2,1,4,128,128]{5,4,3,2,1,0:T(8,128)S(1)} %get-tuple-element.45.refs_0_, bf16[2,4,8,2,1,128,128]{6,5,4,3,2,1,0:T(8,128)(2,1)S(1)} %get-tuple-element.46.refs_1_), custom_call_target="tpu_custom_call" | custom-call | tf_op jit(solution)/shard_map/langreth/pallas_call | solution.py:466
  (41 shorter events, 12.0 us)
Async XLA Ops:
  0.0 40.1 %copy-start.2 = (f32[16,16]{1,0:T(8,128)S(1)}, f32[16,16]{1,0:T(8,128)}, u32[]{:S(2)}) copy-start(f32[16,16]{1,0:T(8,128)} %param.5) | copy-start | bytes 3076
  0.0 1.2 %copy-start = (bf16[2,1,4,256,256]{4,3,2,1,0:T(8,128)(2,1)S(1)}, bf16[2,1,4,256,256]{4,3,2,1,0:T(8,128)(2,1)}, u32[]{:S(2)}) copy-start(bf16[2,1,4,256,256]{4,3,2,1,0:T(8,128)(2,1)} %green_ref.3) | copy-start | bytes 3145732
  2.4 65.5 %all-to-all-start = ((bf16[32,1,2,4,8,128]{5,4,3,2,1,0:T(8,128)(2,1)}), bf16[32,1,2,4,8,128]{5,4,3,2,1,0:T(8,128)(2,1)S(1)}, u32[]{:S(2)}, u32[]{:S(2)}) async-start(bf16[32,1,2,4,8,128]{5,4,3,2,1,0:T(8,128)(2,1)} %get-tuple-element.26), calls=%async_computation | async-start | bytes 1048576 | tf_op jit(solution)/shard_map/all_to_all | solution.py:420
  11.3 11.4 %collective-permute-start.7 = (bf16[2,4,1,2,4,8,128]{6,5,4,3,2,1,0:T(8,128)(2,1)S(1)}, bf16[2,4,1,2,4,8,128]{6,5,4,3,2,1,0:T(8,128)(2,1)S(1)}, u32[]{:S(2)}, u32[]{:S(2)}) collective-permute-start(bf16[2,4,1,2,4,8,128]{6,5,4,3,2,1,0:T(8,128)(2,1)S(1)} %get-tuple-element.36), channel_id=1, source_target_pairs={{0,8},{1,9},{2,10},{3,11},{4,12},{5,13},{6,14},{7,15},{8,0},{9,1},... | collective-permute-start | bytes 393224 | tf_op jit(solution)/shard_map/ppermute | solution.py:355
  13.1 20.6 %collective-permute-start.8 = (bf16[2,4,1,2,4,8,128]{6,5,4,3,2,1,0:T(8,128)(2,1)S(1)}, bf16[2,4,1,2,4,8,128]{6,5,4,3,2,1,0:T(8,128)(2,1)S(1)}, u32[]{:S(2)}, u32[]{:S(2)}) collective-permute-start(bf16[2,4,1,2,4,8,128]{6,5,4,3,2,1,0:T(8,128)(2,1)S(1)} %get-tuple-element.37), channel_id=1, source_target_pairs={{0,16},{1,17},{2,18},{3,19},{4,20},{5,21},{6,22},{7,23},{8,24},{9,... | collective-permute-start | bytes 393224 | tf_op jit(solution)/shard_map/ppermute | solution.py:355
  15.5 18.2 %collective-permute-start.9 = (bf16[2,4,1,2,4,8,128]{6,5,4,3,2,1,0:T(8,128)(2,1)S(1)}, bf16[2,4,1,2,4,8,128]{6,5,4,3,2,1,0:T(8,128)(2,1)S(1)}, u32[]{:S(2)}, u32[]{:S(2)}) collective-permute-start(bf16[2,4,1,2,4,8,128]{6,5,4,3,2,1,0:T(8,128)(2,1)S(1)} %get-tuple-element.38), channel_id=1, source_target_pairs={{0,24},{1,25},{2,26},{3,27},{4,28},{5,29},{6,30},{7,31},{8,16},{9,... | collective-permute-start | bytes 393224 | tf_op jit(solution)/shard_map/ppermute | solution.py:355
  33.7 2.2 %collective-permute-start.10 = (bf16[4,4,1,2,4,8,128]{6,5,4,3,2,1,0:T(8,128)(2,1)S(1)}, bf16[4,4,1,2,4,8,128]{6,5,4,3,2,1,0:T(8,128)(2,1)S(1)}, u32[]{:S(2)}, u32[]{:S(2)}) collective-permute-start(bf16[4,4,1,2,4,8,128]{6,5,4,3,2,1,0:T(8,128)(2,1)S(1)} %near.3), channel_id=1, source_target_pairs={{0,1},{1,0},{2,3},{3,2},{4,5},{5,4},{6,7},{7,6},{8,9},{9,8},{10,11... | collective-permute-start | bytes 786440 | tf_op jit(solution)/shard_map/ppermute | solution.py:355
  33.8 62.8 %collective-permute-start.18 = (bf16[8,2,1,128,128]{4,3,2,1,0:T(8,128)(2,1)S(1)}, bf16[8,2,1,128,128]{4,3,2,1,0:T(8,128)(2,1)S(1)}, u32[]{:S(2)}, u32[]{:S(2)}) collective-permute-start(bf16[8,2,1,128,128]{4,3,2,1,0:T(8,128)(2,1)S(1)} %get-tuple-element.44.refs_4_), channel_id=1, source_target_pairs={{0,2},{1,3},{2,0},{3,1},{4,6},{5,7},{6,4},{7,5},{8,10},{9,11},{10,... | collective-permute-start | bytes 1572872 | tf_op jit(solution)/shard_map/ppermute | solution.py:385
  35.3 61.7 %collective-permute-start.15 = (bf16[8,2,1,128,128]{4,3,2,1,0:T(8,128)(2,1)S(1)}, bf16[8,2,1,128,128]{4,3,2,1,0:T(8,128)(2,1)S(1)}, u32[]{:S(2)}, u32[]{:S(2)}) collective-permute-start(bf16[8,2,1,128,128]{4,3,2,1,0:T(8,128)(2,1)S(1)} %get-tuple-element.43.refs_0_), channel_id=1, source_target_pairs={{0,2},{1,3},{2,0},{3,1},{4,6},{5,7},{6,4},{7,5},{8,10},{9,11},{10,... | collective-permute-start | bytes 1572872 | tf_op jit(solution)/shard_map/ppermute | solution.py:385
  36.6 26.1 %collective-permute-start.11 = (bf16[2,4,1,2,4,8,128]{6,5,4,3,2,1,0:T(8,128)(2,1)}, bf16[2,4,1,2,4,8,128]{6,5,4,3,2,1,0:T(8,128)(2,1)S(1)}, u32[]{:S(2)}, u32[]{:S(2)}) collective-permute-start(bf16[2,4,1,2,4,8,128]{6,5,4,3,2,1,0:T(8,128)(2,1)} %get-tuple-element.40), channel_id=1, source_target_pairs={{0,2},{1,3},{2,0},{3,1},{4,6},{5,7},{6,4},{7,5},{8,10},{9,11},{10,... | collective-permute-start | bytes 393224 | tf_op jit(solution)/shard_map/ppermute | solution.py:355
  38.0 24.7 %collective-permute-start.12 = (bf16[2,4,1,2,4,8,128]{6,5,4,3,2,1,0:T(8,128)(2,1)S(1)}, bf16[2,4,1,2,4,8,128]{6,5,4,3,2,1,0:T(8,128)(2,1)S(1)}, u32[]{:S(2)}, u32[]{:S(2)}) collective-permute-start(bf16[2,4,1,2,4,8,128]{6,5,4,3,2,1,0:T(8,128)(2,1)S(1)} %get-tuple-element.41), channel_id=1, source_target_pairs={{0,4},{1,5},{2,6},{3,7},{4,0},{5,1},{6,2},{7,3},{8,12},{9,13},{10,... | collective-permute-start | bytes 393224 | tf_op jit(solution)/shard_map/ppermute | solution.py:355
  39.5 26.3 %collective-permute-start.13 = (bf16[2,4,1,2,4,8,128]{6,5,4,3,2,1,0:T(8,128)(2,1)S(1)}, bf16[2,4,1,2,4,8,128]{6,5,4,3,2,1,0:T(8,128)(2,1)S(1)}, u32[]{:S(2)}, u32[]{:S(2)}) collective-permute-start(bf16[2,4,1,2,4,8,128]{6,5,4,3,2,1,0:T(8,128)(2,1)S(1)} %get-tuple-element.42), channel_id=1, source_target_pairs={{0,6},{1,7},{2,4},{3,5},{4,2},{5,3},{6,0},{7,1},{8,14},{9,15},{10,... | collective-permute-start | bytes 393224 | tf_op jit(solution)/shard_map/ppermute | solution.py:355
  67.9 46.4 %all-to-all-start.1 = ((bf16[32,1,2,4,8,128]{5,4,3,2,1,0:T(8,128)(2,1)}), bf16[32,1,2,4,8,128]{5,4,3,2,1,0:T(8,128)(2,1)S(1)}, u32[]{:S(2)}, u32[]{:S(2)}) async-start(bf16[32,1,2,4,8,128]{5,4,3,2,1,0:T(8,128)(2,1)} %shard_map.32), calls=%async_computation.1 | async-start | bytes 1048576 | tf_op jit(solution)/shard_map/all_to_all | solution.py:420
  73.1 11.9 %collective-permute-start = (bf16[2,4,1,2,4,8,128]{6,5,4,3,2,1,0:T(8,128)(2,1)S(1)}, bf16[2,4,1,2,4,8,128]{6,5,4,3,2,1,0:T(8,128)(2,1)S(1)}, u32[]{:S(2)}, u32[]{:S(2)}) collective-permute-start(bf16[2,4,1,2,4,8,128]{6,5,4,3,2,1,0:T(8,128)(2,1)S(1)} %get-tuple-element.28), channel_id=1, source_target_pairs={{0,8},{1,9},{2,10},{3,11},{4,12},{5,13},{6,14},{7,15},{8,0},{9,1},... | collective-permute-start | bytes 393224 | tf_op jit(solution)/shard_map/ppermute | solution.py:355
  74.9 21.0 %collective-permute-start.1 = (bf16[2,4,1,2,4,8,128]{6,5,4,3,2,1,0:T(8,128)(2,1)S(1)}, bf16[2,4,1,2,4,8,128]{6,5,4,3,2,1,0:T(8,128)(2,1)S(1)}, u32[]{:S(2)}, u32[]{:S(2)}) collective-permute-start(bf16[2,4,1,2,4,8,128]{6,5,4,3,2,1,0:T(8,128)(2,1)S(1)} %get-tuple-element.29), channel_id=1, source_target_pairs={{0,16},{1,17},{2,18},{3,19},{4,20},{5,21},{6,22},{7,23},{8,24},{9,... | collective-permute-start | bytes 393224 | tf_op jit(solution)/shard_map/ppermute | solution.py:355
  77.4 18.6 %collective-permute-start.2 = (bf16[2,4,1,2,4,8,128]{6,5,4,3,2,1,0:T(8,128)(2,1)S(1)}, bf16[2,4,1,2,4,8,128]{6,5,4,3,2,1,0:T(8,128)(2,1)S(1)}, u32[]{:S(2)}, u32[]{:S(2)}) collective-permute-start(bf16[2,4,1,2,4,8,128]{6,5,4,3,2,1,0:T(8,128)(2,1)S(1)} %get-tuple-element.30), channel_id=1, source_target_pairs={{0,24},{1,25},{2,26},{3,27},{4,28},{5,29},{6,30},{7,31},{8,16},{9,... | collective-permute-start | bytes 393224 | tf_op jit(solution)/shard_map/ppermute | solution.py:355
  95.9 1.6 %collective-permute-start.3 = (bf16[4,4,1,2,4,8,128]{6,5,4,3,2,1,0:T(8,128)(2,1)S(1)}, bf16[4,4,1,2,4,8,128]{6,5,4,3,2,1,0:T(8,128)(2,1)S(1)}, u32[]{:S(2)}, u32[]{:S(2)}) collective-permute-start(bf16[4,4,1,2,4,8,128]{6,5,4,3,2,1,0:T(8,128)(2,1)S(1)} %near.2), channel_id=1, source_target_pairs={{0,1},{1,0},{2,3},{3,2},{4,5},{5,4},{6,7},{7,6},{8,9},{9,8},{10,11... | collective-permute-start | bytes 786440 | tf_op jit(solution)/shard_map/ppermute | solution.py:355
  96.0 18.6 %collective-permute-start.17 = (bf16[8,2,1,128,128]{4,3,2,1,0:T(8,128)(2,1)S(1)}, bf16[8,2,1,128,128]{4,3,2,1,0:T(8,128)(2,1)}, u32[]{:S(2)}, u32[]{:S(2)}) collective-permute-start(bf16[8,2,1,128,128]{4,3,2,1,0:T(8,128)(2,1)S(1)} %get-tuple-element.44.refs_4_), channel_id=1, source_target_pairs={{0,1},{1,0},{2,3},{3,2},{4,5},{5,4},{6,7},{7,6},{8,9},{9,8},{10,11... | collective-permute-start | bytes 1572872 | tf_op jit(solution)/shard_map/ppermute | solution.py:385
  96.5 18.1 %collective-permute-start.14 = (bf16[8,2,1,128,128]{4,3,2,1,0:T(8,128)(2,1)S(1)}, bf16[8,2,1,128,128]{4,3,2,1,0:T(8,128)(2,1)}, u32[]{:S(2)}, u32[]{:S(2)}) collective-permute-start(bf16[8,2,1,128,128]{4,3,2,1,0:T(8,128)(2,1)S(1)} %get-tuple-element.43.refs_0_), channel_id=1, source_target_pairs={{0,1},{1,0},{2,3},{3,2},{4,5},{5,4},{6,7},{7,6},{8,9},{9,8},{10,11... | collective-permute-start | bytes 1572872 | tf_op jit(solution)/shard_map/ppermute | solution.py:385
  96.6 18.0 %collective-permute-start.19 = (bf16[8,2,1,128,128]{4,3,2,1,0:T(8,128)(2,1)S(1)}, bf16[8,2,1,128,128]{4,3,2,1,0:T(8,128)(2,1)}, u32[]{:S(2)}, u32[]{:S(2)}) collective-permute-start(bf16[8,2,1,128,128]{4,3,2,1,0:T(8,128)(2,1)S(1)} %collective-permute-done.18.refs_6_), channel_id=1, source_target_pairs={{0,1},{1,0},{2,3},{3,2},{4,5},{5,4},{6,7},{7,6},{8,9},{9,8},{10,11... | collective-permute-start | bytes 1572872 | tf_op jit(solution)/shard_map/ppermute | solution.py:385
  97.0 17.6 %collective-permute-start.16 = (bf16[8,2,1,128,128]{4,3,2,1,0:T(8,128)(2,1)S(1)}, bf16[8,2,1,128,128]{4,3,2,1,0:T(8,128)(2,1)}, u32[]{:S(2)}, u32[]{:S(2)}) collective-permute-start(bf16[8,2,1,128,128]{4,3,2,1,0:T(8,128)(2,1)S(1)} %collective-permute-done.15.refs_2_), channel_id=1, source_target_pairs={{0,1},{1,0},{2,3},{3,2},{4,5},{5,4},{6,7},{7,6},{8,9},{9,8},{10,11... | collective-permute-start | bytes 1572872 | tf_op jit(solution)/shard_map/ppermute | solution.py:385
  97.6 5.6 %collective-permute-start.4 = (bf16[2,4,1,2,4,8,128]{6,5,4,3,2,1,0:T(8,128)(2,1)S(1)}, bf16[2,4,1,2,4,8,128]{6,5,4,3,2,1,0:T(8,128)(2,1)S(1)}, u32[]{:S(2)}, u32[]{:S(2)}) collective-permute-start(bf16[2,4,1,2,4,8,128]{6,5,4,3,2,1,0:T(8,128)(2,1)S(1)} %get-tuple-element.32), channel_id=1, source_target_pairs={{0,2},{1,3},{2,0},{3,1},{4,6},{5,7},{6,4},{7,5},{8,10},{9,11},{10,... | collective-permute-start | bytes 393224 | tf_op jit(solution)/shard_map/ppermute | solution.py:355
  103.2 5.0 %collective-permute-start.5 = (bf16[2,4,1,2,4,8,128]{6,5,4,3,2,1,0:T(8,128)(2,1)S(1)}, bf16[2,4,1,2,4,8,128]{6,5,4,3,2,1,0:T(8,128)(2,1)S(1)}, u32[]{:S(2)}, u32[]{:S(2)}) collective-permute-start(bf16[2,4,1,2,4,8,128]{6,5,4,3,2,1,0:T(8,128)(2,1)S(1)} %get-tuple-element.33), channel_id=1, source_target_pairs={{0,4},{1,5},{2,6},{3,7},{4,0},{5,1},{6,2},{7,3},{8,12},{9,13},{10,... | collective-permute-start | bytes 393224 | tf_op jit(solution)/shard_map/ppermute | solution.py:355
  108.1 5.9 %collective-permute-start.6 = (bf16[2,4,1,2,4,8,128]{6,5,4,3,2,1,0:T(8,128)(2,1)S(1)}, bf16[2,4,1,2,4,8,128]{6,5,4,3,2,1,0:T(8,128)(2,1)S(1)}, u32[]{:S(2)}, u32[]{:S(2)}) collective-permute-start(bf16[2,4,1,2,4,8,128]{6,5,4,3,2,1,0:T(8,128)(2,1)S(1)} %get-tuple-element.34), channel_id=1, source_target_pairs={{0,6},{1,7},{2,4},{3,5},{4,2},{5,3},{6,0},{7,1},{8,14},{9,15},{10,... | collective-permute-start | bytes 393224 | tf_op jit(solution)/shard_map/ppermute | solution.py:355
  (1 other events, 1.2 us)
